TPU v7x, 512 devices: a whole 4x4x16 slice. The times are simulated.
512 devices in a mesh: quad: 16 (over z_lo, core), gy: 8 (over y, z_hi), gx: 4 (over x).
Axes of the slice: x: 4, y: 4, z: 16 (z_hi: 2, z_lo: 8; z = z_hi * 8 + z_lo), core: 2. Of those that a mesh axis runs over, the one named last changes fastest.
Arguments:
- modes_now: bfloat16 [1024, 64, 512], P('quad', 'gy', 'gx'), may hold values from -4 to 4
- basis_rows: bfloat16 [4096, 1024], P('quad'), may hold values from -0.25 to 0.25
- quad_weights: float32 [4096], P('quad'), may hold values from 0.2 to 2
- germ_nodes: float32 [4096, 8], P('quad'), may hold values from -1.5 to 1.5
- log_fields: float32 [8, 64, 512], P(None, 'gy', 'gx'), may hold values from -1 to 1
- reaction_rates: float32 [4096], P('quad'), may hold values from 0.08 to 0.32
Outputs:
- modes_next: float32 [1024, 64, 512], P('quad', 'gy', 'gx')
All inputs are finite; a program needn't handle non-finite values.
Results may differ from a plain program's by a relative error of at most 0.02.
Values may be sent and summed in bfloat16 or wider, within the bound.
No kernel may reach another device: no remote copies, remote signals or barrier semaphores. Data moves between devices by JAX's collectives and lax.ppermute only.
A program may use at most 64 MiB of HBM per device.

v0:
```python
import jax
import jax.numpy as jnp
from jax import lax
from jax.sharding import PartitionSpec as P

time_step = 0.04


def with_halo(array, sides, width):
    for axis, dim in sides:
        peers, length = (lax.axis_size(axis), array.shape[dim])
        up = [(i, (i + 1) % peers) for i in range(peers - 1)]
        down = [(j, i) for i, j in up]
        last = lax.slice_in_dim(array, length - width, length, axis=dim)
        leading = lax.slice_in_dim(array, 0, width, axis=dim)
        before = lax.ppermute(last, axis, up)
        after = lax.ppermute(leading, axis, down)
        array = jnp.concatenate([before, array, after], axis=dim)
    return array


def neighbour(array, drow, dcol):
    return array[:, 1 + drow : array.shape[1] - 1 + drow, 1 + dcol : array.shape[2] - 1 + dcol]


def drive_with(field_ext, coeff_ext, rates, weights):
    center = neighbour(field_ext, 0, 0)
    coeff_mid = neighbour(coeff_ext, 0, 0)
    total = jnp.zeros_like(center)
    for drow, dcol in ((-1, 0), (1, 0), (0, -1), (0, 1)):
        total = total + (coeff_mid + neighbour(coeff_ext, drow, dcol)) * (
            neighbour(field_ext, drow, dcol) - center
        )
    total = total + rates[:, None, None] * (center - center * center * center)
    return (weights[:, None, None] * total).astype(jnp.bfloat16).reshape(center.shape[0], -1)


def rim_fields(field):
    return with_halo(field, (("gy", 1), ("gx", 2)), 1)


def body(modes_now, basis_rows, quad_weights, germ_nodes, log_fields, reaction_rates):
    k_local, rows_y, cols_x = modes_now.shape
    q_local, modes_total = basis_rows.shape
    log_ext = with_halo(log_fields, (("gy", 1), ("gx", 2)), 1)
    coeff_ext = jnp.exp(
        jnp.einsum("qj,jyx->qyx", germ_nodes, log_ext, precision=lax.Precision.HIGHEST)
    )

    def realize(block_flat):
        return jnp.dot(
            basis_rows,
            lax.all_gather(block_flat, "quad", axis=0, tiled=True),
            preferred_element_type=jnp.float32,
        )

    def field_of(block):
        return rim_fields(realize(block.reshape(k_local, -1)).reshape(q_local, rows_y, cols_x))

    def drive(field_ext):
        return drive_with(field_ext, coeff_ext, reaction_rates, quad_weights)

    def spread(weighted):
        return (
            lax.psum_scatter(
                lax.dot_general(
                    basis_rows,
                    weighted,
                    (((0,), (0,)), ((), ())),
                    preferred_element_type=jnp.float32,
                ).astype(jnp.bfloat16),
                "quad",
                scatter_dimension=0,
                tiled=True,
            )
            .astype(jnp.float32)
            .reshape(k_local, rows_y, cols_x)
        )

    current = modes_now.astype(jnp.float32)
    first = spread(drive(field_of(modes_now)))
    iterate_one = (current + time_step * first).astype(jnp.bfloat16)
    field_one = field_of(iterate_one)
    second = spread(drive(field_one))
    return current + time_step * second


def solution(mesh):
    in_specs = (
        P("quad", "gy", "gx"),
        P("quad", None),
        P("quad"),
        P("quad", None),
        P(None, "gy", "gx"),
        P("quad"),
    )
    out_specs = P("quad", "gy", "gx")
    return jax.shard_map(body, mesh=mesh, in_specs=in_specs, out_specs=out_specs, check_vma=False)
```

profile of v0, /device:TPU:1, one launch (start us, length us, event | category | flops | bytes accessed | tf_op | source)
XLA Modules:
  0.0 522.0 jit_solution(11073676379611655207)
XLA Ops:
  6.5 1.6 copy.32
  9.1 16.3 %collective-permute-start = (f32[8,1,128]{2,0,1:T(8,128)S(1)}, f32[8,1,128]{2,0,1:T(8,128)S(1)}, u32[]{:S(2)}, u32[]{:S(2)}) collective-permute-start(f32[8,1,128]{2,0,1:T(8,128)S(1)} %copy.29), channel_id=1, source_target_pairs={{0,4},{4,8},{8,12},{12,16},{16,20},{20,24},{24,28},{1,5},{5,9},{9,... | collective-permute-start | bytes 12296 | tf_op jit(solution)/shard_map/ppermute | solution.py:16
  25.4 1.3 collective-permute-start.1
  27.5 11.1 %collective-permute-done.1 = f32[8,1,128]{2,0,1:T(8,128)S(1)} collective-permute-done((f32[8,1,128]{2,0,1:T(8,128)S(1)}, f32[8,1,128]{2,0,1:T(8,128)S(1)}, u32[]{:S(2)}, u32[]{:S(2)}) %collective-permute-start.1) | collective-permute-done | bytes 4128 | tf_op jit(solution)/shard_map/ppermute | solution.py:17
  38.5 76.7 %all-gather.3.cloned.1.call-done = bf16[1024,1024]{1,0:T(8,128)(2,1)} async-done(((bf16[64,1024]{1,0:T(8,128)(2,1)}), bf16[1024,1024]{1,0:T(8,128)(2,1)}) %all-gather.3.cloned.1.call-update) | async-done | bytes 2097168 | tf_op jit(solution)/shard_map/all_gather | solution.py:53
  115.3 2.5 fusion.43
  117.8 4.9 collective-permute-start.4
  122.8 1.3 collective-permute-start.5
  124.2 3.1 collective-permute-start.2
  127.3 1.3 collective-permute-start.3
  128.6 8.6 %collective-permute-done.5 = f32[256,1,128]{0,2,1:T(8,128)S(1)} collective-permute-done((f32[256,1,128]{0,2,1:T(8,128)S(1)}, f32[256,1,128]{0,2,1:T(8,128)S(1)}, u32[]{:S(2)}, u32[]{:S(2)}) %collective-permute-start.5) | collective-permute-done | bytes 131104 | tf_op jit(solution)/shard_map/ppermute | solution.py:17
  137.2 4.0 collective-permute-start.6
  141.2 1.3 collective-permute-start.7
  142.6 1.5 fusion
  144.1 1.8 collective-permute-done.7
  146.0 1.3 fusion.4
  147.3 2.0 convert_bitcast_fusion.1
  149.3 3.9 copy.20
  153.3 111.5 %reduce-scatter.7.cloned.1.call-done = bf16[64,1024]{1,0:T(8,128)(2,1)} async-done(((bf16[1024,1024]{1,0:T(8,128)(2,1)}), bf16[64,1024]{1,0:T(8,128)(2,1)}) %reduce-scatter.7.cloned.1.call-update) | async-done | bytes 131088
  264.8 1.1 copy.21
  266.9 102.2 %all-gather.5.cloned.1.call-done = bf16[1024,1024]{1,0:T(8,128)(2,1)} async-done(((bf16[64,1024]{1,0:T(8,128)(2,1)}), bf16[1024,1024]{1,0:T(8,128)(2,1)}) %all-gather.5.cloned.1.call-update) | async-done | bytes 2097168 | tf_op jit(solution)/shard_map/all_gather | solution.py:53
  369.1 2.3 fusion.44
  371.5 4.9 collective-permute-start.8
  376.4 1.3 collective-permute-start.9
  377.7 2.5 collective-permute-done.8
  380.2 11.1 %collective-permute-done.9 = f32[256,1,128]{0,2,1:T(8,128)S(1)} collective-permute-done((f32[256,1,128]{0,2,1:T(8,128)S(1)}, f32[256,1,128]{0,2,1:T(8,128)S(1)}, u32[]{:S(2)}, u32[]{:S(2)}) %collective-permute-start.9) | collective-permute-done | bytes 131104 | tf_op jit(solution)/shard_map/ppermute | solution.py:17
  391.3 3.4 collective-permute-start.10
  394.7 1.3 collective-permute-start.11
  396.0 3.1 collective-permute-done.11
  399.1 1.3 fusion.8
  401.1 2.6 copy.22
  403.7 109.7 %reduce-scatter.9.cloned.1.call-done = bf16[64,1024]{1,0:T(8,128)(2,1)} async-done(((bf16[1024,1024]{1,0:T(8,128)(2,1)}), bf16[64,1024]{1,0:T(8,128)(2,1)}) %reduce-scatter.9.cloned.1.call-update) | async-done | bytes 131088
  (44 shorter events, 5.7 us)
Async XLA Ops:
  6.5 108.7 %copy-start = (bf16[256,1024]{1,0:T(8,128)(2,1)S(1)}, bf16[256,1024]{1,0:T(8,128)(2,1)}, u32[]{:S(2)}) copy-start(bf16[256,1024]{1,0:T(8,128)(2,1)} %param.7) | copy-start | bytes 1572868
  6.5 108.7 %all-gather.3.cloned.1.call-start = ((), (), s32[]{:S(2)}) async-start(), calls=%async_computation.2 | async-start | bytes 2228224 | tf_op jit(solution)/shard_map/all_gather | solution.py:53
  8.2 256.6 %reduce-scatter.7.cloned.1.call-start = ((), (), s32[]{:S(2)}) async-start(), calls=%async_computation.4 | async-start | bytes 2228224
  9.1 17.6 %collective-permute-start = (f32[8,1,128]{2,0,1:T(8,128)S(1)}, f32[8,1,128]{2,0,1:T(8,128)S(1)}, u32[]{:S(2)}, u32[]{:S(2)}) collective-permute-start(f32[8,1,128]{2,0,1:T(8,128)S(1)} %copy.29), channel_id=1, source_target_pairs={{0,4},{4,8},{8,12},{12,16},{16,20},{20,24},{24,28},{1,5},{5,9},{9,... | collective-permute-start | bytes 12296 | tf_op jit(solution)/shard_map/ppermute | solution.py:16
  25.4 13.2 %collective-permute-start.1 = (f32[8,1,128]{2,0,1:T(8,128)S(1)}, f32[8,1,128]{2,0,1:T(8,128)S(1)}, u32[]{:S(2)}, u32[]{:S(2)}) collective-permute-start(f32[8,1,128]{2,0,1:T(8,128)S(1)} %copy.30), channel_id=1, source_target_pairs={{4,0},{8,4},{12,8},{16,12},{20,16},{24,20},{28,24},{5,1},{9,5},{13... | collective-permute-start | bytes 12296 | tf_op jit(solution)/shard_map/ppermute | solution.py:17
  38.5 104.0 %copy-start.2 = (f32[256,8]{0,1:T(8,128)S(1)}, f32[256,8]{0,1:T(8,128)}, u32[]{:S(2)}) copy-start(f32[256,8]{0,1:T(8,128)} %param.9) | copy-start | bytes 24580
  117.8 28.2 %copy-start.3 = (f32[256]{0:T(256)S(1)}, f32[256]{0:T(256)}, u32[]{:S(2)}) copy-start(f32[256]{0:T(256)} %param.11) | copy-start | bytes 3076
  117.8 28.2 %copy-start.4 = (f32[256]{0:T(256)S(1)}, f32[256]{0:T(256)}, u32[]{:S(2)}) copy-start(f32[256]{0:T(256)} %param.8) | copy-start | bytes 3076
  117.8 10.7 %collective-permute-start.4 = (f32[256,1,128]{0,2,1:T(8,128)S(1)}, f32[256,1,128]{0,2,1:T(8,128)S(1)}, u32[]{:S(2)}, u32[]{:S(2)}) collective-permute-start(f32[256,1,128]{0,2,1:T(8,128)S(1)} %get-tuple-element.11), channel_id=1, source_target_pairs={{0,4},{4,8},{8,12},{12,16},{16,20},{20,24},{24,28},{1,5},{5,9},{9,... | collective-permute-start | bytes 393224 | tf_op jit(solution)/shard_map/ppermute | solution.py:16
  122.8 14.4 %collective-permute-start.5 = (f32[256,1,128]{0,2,1:T(8,128)S(1)}, f32[256,1,128]{0,2,1:T(8,128)S(1)}, u32[]{:S(2)}, u32[]{:S(2)}) collective-permute-start(f32[256,1,128]{0,2,1:T(8,128)S(1)} %get-tuple-element.12), channel_id=1, source_target_pairs={{4,0},{8,4},{12,8},{16,12},{20,16},{24,20},{28,24},{5,1},{9,5},{13... | collective-permute-start | bytes 393224 | tf_op jit(solution)/shard_map/ppermute | solution.py:17
  124.2 18.4 %collective-permute-start.2 = (f32[8,10,1]{2,0,1:T(8,128)S(1)}, f32[8,10,1]{2,0,1:T(8,128)S(1)}, u32[]{:S(2)}, u32[]{:S(2)}) collective-permute-start(f32[8,10,1]{2,0,1:T(8,128)S(1)} %get-tuple-element.13), channel_id=1, source_target_pairs={{0,1},{1,2},{2,3},{4,5},{5,6},{6,7},{8,9},{9,10},{10,11},{12,13},{... | collective-permute-start | bytes 968 | tf_op jit(solution)/shard_map/ppermute | solution.py:16
  127.3 15.3 %collective-permute-start.3 = (f32[8,10,1]{2,0,1:T(8,128)S(1)}, f32[8,10,1]{2,0,1:T(8,128)S(1)}, u32[]{:S(2)}, u32[]{:S(2)}) collective-permute-start(f32[8,10,1]{2,0,1:T(8,128)S(1)} %get-tuple-element.14), channel_id=1, source_target_pairs={{1,0},{2,1},{3,2},{5,4},{6,5},{7,6},{9,8},{10,9},{11,10},{13,12},{... | collective-permute-start | bytes 968 | tf_op jit(solution)/shard_map/ppermute | solution.py:17
  137.2 6.9 %collective-permute-start.6 = (f32[256,10,1]{0,2,1:T(1,128)S(1)}, f32[256,10,1]{0,2,1:T(1,128)S(1)}, u32[]{:S(2)}, u32[]{:S(2)}) collective-permute-start(f32[256,10,1]{0,2,1:T(1,128)S(1)} %get-tuple-element.7), channel_id=1, source_target_pairs={{0,1},{1,2},{2,3},{4,5},{5,6},{6,7},{8,9},{9,10},{10,11},{12,13},{... | collective-permute-start | bytes 30728 | tf_op jit(solution)/shard_map/ppermute | solution.py:16
  141.2 4.7 collective-permute-start.7
  153.2 112.9 %copy-start.1 = (bf16[64,8,128]{2,1,0:T(8,128)(2,1)S(1)}, bf16[64,8,128]{2,1,0:T(8,128)(2,1)}, u32[]{:S(2)}) copy-start(bf16[64,8,128]{2,1,0:T(8,128)(2,1)} %param.6) | copy-start | bytes 393220
  153.3 215.8 %all-gather.5.cloned.1.call-start = ((), (), s32[]{:S(2)}) async-start(), calls=%async_computation.3 | async-start | bytes 2228224 | tf_op jit(solution)/shard_map/all_gather | solution.py:53
  266.9 246.5 %reduce-scatter.9.cloned.1.call-start = ((), (), s32[]{:S(2)}) async-start(), calls=%async_computation.5 | async-start | bytes 2228224
  371.5 8.7 %collective-permute-start.8 = (f32[256,1,128]{0,2,1:T(8,128)S(1)}, f32[256,1,128]{0,2,1:T(8,128)S(1)}, u32[]{:S(2)}, u32[]{:S(2)}) collective-permute-start(f32[256,1,128]{0,2,1:T(8,128)S(1)} %get-tuple-element.9), channel_id=1, source_target_pairs={{0,4},{4,8},{8,12},{12,16},{16,20},{20,24},{24,28},{1,5},{5,9},{9,... | collective-permute-start | bytes 393224 | tf_op jit(solution)/shard_map/ppermute | solution.py:16
  376.4 14.9 %collective-permute-start.9 = (f32[256,1,128]{0,2,1:T(8,128)S(1)}, f32[256,1,128]{0,2,1:T(8,128)S(1)}, u32[]{:S(2)}, u32[]{:S(2)}) collective-permute-start(f32[256,1,128]{0,2,1:T(8,128)S(1)} %get-tuple-element.10), channel_id=1, source_target_pairs={{4,0},{8,4},{12,8},{16,12},{20,16},{24,20},{28,24},{5,1},{9,5},{13... | collective-permute-start | bytes 393224 | tf_op jit(solution)/shard_map/ppermute | solution.py:17
  391.3 4.7 collective-permute-start.10
  394.7 4.4 collective-permute-start.11
Sparse Core Ops, SparseCore 0:
  9.4 105.7 all-gather.2
  153.4 111.3 reduce-scatter.6
  267.0 102.0 all-gather.4
  403.9 109.4 reduce-scatter.8
where the time goes:
time: 530 us; the launch traced here: 522 us
  waiting for transfers between devices  438 us (83%)
  starting transfers between devices  44.4 us (8%)
  between operations  13.4 us (3%)
  local copies, waits for them, and re-layouts  13.1 us (2%)
  matrix products  9.14 us (2%)
    unnamed x6, waiting for transfers between devices  221 us
    all_gather x2, waiting for transfers between devices, realize(): lax.all_gather(block_flat, 'quad', axis=0, tiled=True)  179 us
    ppermute x6, starting transfers between devices, with_halo(): before = lax.ppermute(last, axis, up)  36.5 us
    ppermute x6, waiting for transfers between devices, with_halo(): after = lax.ppermute(leading, axis, down)  35.7 us
    unnamed x20, local copies, waits for them, and re-layouts  11.8 us
  transfers between devices with their start and end apart: 16, of which 10 were waited for; matrix products, arithmetic and copies ran while one was open for 1% of the time, Pallas kernels for 0%

commit v1 on v0

v1 whole, which is shorter than its diff:
```python
import functools

import jax
import jax.numpy as jnp
from jax import lax
from jax.experimental import pallas as pl
from jax.experimental.pallas import tpu as pltpu
from jax.sharding import PartitionSpec as P

STEP = 0.04
BF = jnp.bfloat16
F32 = jnp.float32
VM = pltpu.VMEM
OFFS = (0, -1, 1, 2)


def halo(array, axis, dim, width):
    peers, length = lax.axis_size(axis), array.shape[dim]
    up = [(i, i + 1) for i in range(peers - 1)]
    down = [(j, i) for i, j in up]
    before = lax.ppermute(lax.slice_in_dim(array, length - width, length, axis=dim), axis, up)
    after = lax.ppermute(lax.slice_in_dim(array, 0, width, axis=dim), axis, down)
    return jnp.concatenate([before, array, after], axis=dim)


def split3(x):
    hi = lax.reduce_precision(x, 8, 7)
    mid = lax.reduce_precision(x - hi, 8, 7)
    low = (x - hi) - mid
    return hi.astype(BF), mid.astype(BF), low.astype(BF)


def join3(a, b, c):
    return a.astype(F32) + (b.astype(F32) + c.astype(F32))


def ring(array, axis, stride):
    n = lax.axis_size(axis)
    fwd = [(i, (i + stride) % n) for i in range(n)]
    bwd = [(j, i) for i, j in fwd]
    below = lax.ppermute(array, axis, fwd)
    above = lax.ppermute(array, axis, bwd)
    return below, above, fwd, bwd


def gather_small(array, axis, stride):
    below, above, fwd, _ = ring(array, axis, stride)
    far = lax.ppermute(below, axis, fwd)
    return jnp.concatenate([array, below, above, far], axis=0)


def gather_large(array, axis, stride):
    below, above, fwd, bwd = ring(array, axis, stride)
    half = array.shape[0] // 2
    far0 = lax.ppermute(below[:half], axis, fwd)
    far1 = lax.ppermute(above[half:], axis, bwd)
    return [array, below, above, far0, far1]


def coef_kernel(log_ref, nodes_ref, out_ref):
    cols = [log_ref[:, j : j + 1] for j in range(8)]
    for c in range(16):
        acc = cols[0] * nodes_ref[0:1, c * 128 : (c + 1) * 128]
        for j in range(1, 8):
            acc = acc + cols[j] * nodes_ref[j : j + 1, c * 128 : (c + 1) * 128]
        out_ref[c] = jnp.exp(acc)


def drive(f_ref, h, coef_ref, c, rows, skip, rate, weight):
    def f(d):
        return f_ref[h, 20 + d : 20 + d + rows, :]

    def k(d):
        return coef_ref[c, skip + 20 + d : skip + 20 + d + rows, :]

    mid, kmid = f(0), k(0)
    total = (kmid + k(-20)) * (f(-20) - mid)
    for d in (20, -1, 1):
        total = total + (kmid + k(d)) * (f(d) - mid)
    total = total + rate * (mid - mid * mid * mid)
    return (weight * total).astype(BF)


def sweep(state, basis_refs, coef_ref, wt_ref, rate_ref, f_ref, acc_ref, rows, skip):
    acc_ref[...] = jnp.zeros_like(acc_ref)
    c = 0
    for ref in basis_refs:
        for s in range(0, ref.shape[0], 256):
            size = min(256, ref.shape[0] - s)
            block = ref[s : s + size, :]
            field = lax.dot_general(state, block, (((1,), (1,)), ((), ())), preferred_element_type=F32)
            parts = []
            for h in range(size // 128):
                f_ref[h, : field.shape[0], :] = field[:, h * 128 : (h + 1) * 128]
                parts.append(
                    drive(f_ref, h, coef_ref, c, rows, skip, rate_ref[c : c + 1, :], wt_ref[c : c + 1, :])
                )
                c += 1
            w = jnp.concatenate(parts, axis=1) if len(parts) > 1 else parts[0]
            acc_ref[...] += jnp.dot(w, block, preferred_element_type=F32)


def first_kernel(*refs):
    basis_refs = refs[:10]
    state_ref, coef_ref, wt_ref, rate_ref, out_ref, f_ref, acc_ref = refs[10:]
    sweep(state_ref[...], basis_refs, coef_ref, wt_ref, rate_ref, f_ref, acc_ref, 200, 0)
    out_ref[...] = acc_ref[...].astype(BF)


def second_kernel(*refs):
    basis_refs = refs[:10]
    state_ref, coef_ref, wt_ref, rate_ref, own_ref, other_ref, mask_ref, out_ref, f_ref, acc_ref = refs[10:]
    total = own_ref[...].astype(F32) + other_ref[...].astype(F32)
    now = state_ref[...].astype(F32)[20:220]
    state = ((now + STEP * total) * mask_ref[...][:, 0:1]).astype(BF)
    sweep(state, basis_refs, coef_ref, wt_ref, rate_ref, f_ref, acc_ref, 160, 20)
    out_ref[...] = acc_ref[...]


def body(modes_now, basis_rows, quad_weights, germ_nodes, log_fields, reaction_rates):
    quad, gy, gx = lax.axis_index("quad"), lax.axis_index("gy"), lax.axis_index("gx")
    zl, core, y, x = quad // 2, quad % 2, gy // 2, gx
    logs = split3(log_fields)
    chan = jnp.concatenate([modes_now, *logs], axis=0).transpose(1, 2, 0)
    ext = halo(halo(chan, "gx", 1, 2), "gy", 0, 2)
    logp = lax.dynamic_slice_in_dim(ext, zl * 16, 20, axis=1)[:, :, 64:88].reshape(240, 24)
    logp = join3(logp[:, 0:8], logp[:, 8:16], logp[:, 16:24])
    patch = jnp.stack([ext[:, 16 * d : 16 * d + 20, :64] for d in range(8)])
    patch = patch.reshape(8, 2, 120, 64).transpose(0, 2, 1, 3).reshape(8, 120, 128)
    patch = jnp.pad(patch, ((0, 0), (0, 8), (0, 0)))
    patch = patch.reshape(8, 8, 16, 128).transpose(0, 2, 1, 3).reshape(8, 16, 1024)
    part = lax.dynamic_slice_in_dim(basis_rows, (y * 4 + x) * 16, 16, axis=0)
    pars = jnp.concatenate([quad_weights[None], reaction_rates[None], germ_nodes.T], axis=0)
    pars = jnp.concatenate(split3(pars), axis=0)
    pars = jnp.pad(pars, ((0, 2), (0, 0))).reshape(8, 1024)
    same = jnp.concatenate([part, pars], axis=0)
    send = jnp.concatenate([patch, jnp.broadcast_to(same[None], (8, 24, 1024))], axis=1)
    groups = [list(range(0, 16, 2)), list(range(1, 16, 2))]
    recv = lax.all_to_all(send, "quad", 0, 0, axis_index_groups=groups, tiled=True)
    sub = recv[:, 16:32].reshape(8, 2, 8, 1024)
    first, second = sub[:, 0].reshape(64, 1024), sub[:, 1].reshape(64, 1024)
    a_row = gather_small(first, "gx", 1)
    b_col = gather_small(second, "gy", 2)
    blocks = gather_large(a_row, "gy", 2) + gather_large(b_col, "gx", 1)
    mine = recv[:, :16]
    swap = [(i, i ^ 1) for i in range(16)]
    theirs = lax.ppermute(mine, "quad", swap)
    pair = jnp.where(core == 0, jnp.stack([mine, theirs]), jnp.stack([theirs, mine]))
    pair = pair.reshape(2, 8, 16, 8, 2, 64).transpose(4, 3, 2, 1, 0, 5)
    state = pair.reshape(2, 128, 1024)[:, :120].reshape(240, 1024)
    pars = recv[:, 32:].reshape(8, 32, 256)[:, :30].reshape(8, 3, 10, 16, 2, 8)
    pars = join3(pars[:, 0], pars[:, 1], pars[:, 2])
    pars = pars.transpose(1, 3, 2, 0, 4).reshape(10, 2, 4, 4, 64)
    oy = jnp.asarray([d for d in OFFS], jnp.int32)
    pars = jnp.take(jnp.take(pars, (y + oy) % 4, axis=2), (x + oy) % 4, axis=3)
    pars = jnp.concatenate(
        [pars[:, 0].reshape(10, 1024), pars[:, 1].transpose(0, 2, 1, 3).reshape(10, 1024)], axis=1
    )
    wts, rates, nodes = pars[0].reshape(16, 128), pars[1].reshape(16, 128), pars[2:]
    coef = pl.pallas_call(
        coef_kernel, out_shape=jax.ShapeDtypeStruct((16, 240, 128), F32), name="coef"
    )(logp, nodes)
    part1 = pl.pallas_call(
        first_kernel,
        out_shape=jax.ShapeDtypeStruct((200, 1024), BF),
        scratch_shapes=[VM((2, 240, 128), F32), VM((200, 1024), F32)],
        name="first",
    )(*blocks, state, coef, wts, rates)
    other1 = lax.ppermute(part1, "quad", swap)
    cell = jnp.arange(200)
    row, col = gy * 8 + cell // 20 - 1, gx * 128 + zl * 16 + cell % 20 - 2
    inside = (row >= 0) & (row < 64) & (col >= 0) & (col < 512)
    mask = jnp.broadcast_to(inside.astype(F32)[:, None], (200, 128))
    part2 = pl.pallas_call(
        second_kernel,
        out_shape=jax.ShapeDtypeStruct((160, 1024), F32),
        scratch_shapes=[VM((2, 200, 128), F32), VM((160, 1024), F32)],
        name="second",
    )(*blocks, state, coef, wts, rates, part1, other1, mask)
    out = part2.astype(BF).reshape(2, 4, 20, 16, 64)[:, :, 2:18]
    out = out.transpose(3, 1, 2, 0, 4).reshape(16, 64, 128)
    back = lax.all_to_all(out, "quad", 0, 0, tiled=True)
    back = back.reshape(8, 2, 64, 128).astype(F32).sum(axis=1)
    back = back.reshape(8, 4, 16, 2, 64).transpose(4, 3, 1, 0, 2).reshape(64, 8, 128)
    return modes_now.astype(F32) + STEP * back


def solution(mesh):
    in_specs = (
        P("quad", "gy", "gx"),
        P("quad", None),
        P("quad"),
        P("quad", None),
        P(None, "gy", "gx"),
        P("quad"),
    )
    out_specs = P("quad", "gy", "gx")
    return jax.shard_map(body, mesh=mesh, in_specs=in_specs, out_specs=out_specs, check_vma=False)
```

time: 530 us -> 217 us (0.41); the launches traced: 522 us -> 216 us
  waiting for transfers between devices: 438 us -> 44.8 us
  starting transfers between devices: 44.4 us -> 90.2 us
  blocking collectives: 0 us -> 21.5 us
  Pallas kernels: 0 us -> 18.7 us
  local copies, waits for them, and re-layouts: 13.1 us -> 27 us
  between operations: 13.4 us -> 0.87 us
  matrix products: 9.14 us -> 0 us
  other arithmetic: 3.51 us -> 12.5 us
    unnamed x6 -> x0, waiting for transfers between devices: 221 us -> none
    all_gather x2 -> x0, waiting for transfers between devices: 179 us -> none  [realize(): lax.all_gather(block_flat, 'quad', axis=0, tiled=True)]
    ppermute x12 -> x20, starting transfers between devices: 44.3 us -> 82.4 us  [the longest x2 20.2 us: halo(): lax.ppermute(lax.slice_in_dim(array, length - width, length, axis=dim), a...]
    all_to_all x0 -> x1, waiting for transfers between devices: none -> 22.8 us  [body(): lax.all_to_all(send, 'quad', 0, 0, axis_index_groups=groups, tiled=True)]
    all_to_all x0 -> x1, blocking collectives: none -> 21.5 us  [body(): back = lax.all_to_all(out, 'quad', 0, 0, tiled=True)]
    pallas_call x0 -> x3, Pallas kernels: none -> 18.7 us  [the longest x1 7.57 us: body(): pl.pallas_call(second_kernel, out_shape=jax.ShapeDtypeStruct((160, 1024),...]
    ppermute x12 -> x20, waiting for transfers between devices: 38.3 us -> 22 us  [the longest x2 17.4 us: halo(): lax.ppermute(lax.slice_in_dim(array, 0, width, axis=dim), axis, down)]
    dot_general x5 -> x0, matrix products: 9.14 us -> none  [the longest x2 4.87 us: realize(): jnp.dot(basis_rows, lax.all_gather(block_flat, 'quad', axis=0, tiled=True...]
  transfers between devices with their start and end apart: 16 -> 21, of which waited for: 10 -> 8; matrix products, arithmetic and copies ran while one was open for 1% -> 12% of each run, Pallas kernels for 0% -> 2%
where the time goes in v1:
time: 217 us; the launch traced here: 216 us
  starting transfers between devices  90.2 us (42%)
  waiting for transfers between devices  44.8 us (21%)
  local copies, waits for them, and re-layouts  27 us (12%)
  blocking collectives  21.5 us (10%)
  Pallas kernels  18.7 us (9%)
  other arithmetic  12.5 us (6%)
    all_to_all x1, waiting for transfers between devices, body(): lax.all_to_all(send, 'quad', 0, 0, axis_index_groups=groups, tiled=True)  22.8 us
    all_to_all x1, blocking collectives, body(): back = lax.all_to_all(out, 'quad', 0, 0, tiled=True)  21.5 us
    ppermute x2, starting transfers between devices, halo(): lax.ppermute(lax.slice_in_dim(array, length - width, length, axis=dim), a...  20.2 us
    ppermute x2, waiting for transfers between devices, halo(): lax.ppermute(lax.slice_in_dim(array, 0, width, axis=dim), axis, down)  17.4 us
    ppermute x1, starting transfers between devices, body(): theirs = lax.ppermute(mine, 'quad', swap)  14.2 us
    ppermute x4, starting transfers between devices, ring(): above = lax.ppermute(array, axis, bwd)  11.5 us
    ppermute x4, starting transfers between devices, ring(): below = lax.ppermute(array, axis, fwd)  10.7 us
    ppermute x2, starting transfers between devices, gather_large(): far1 = lax.ppermute(above[half:], axis, bwd)  9.12 us
  transfers between devices with their start and end apart: 21, of which 8 were waited for; matrix products, arithmetic and copies ran while one was open for 12% of the time, Pallas kernels for 2%

profile of v1, /device:TPU:1, one launch (start us, length us, event | category | flops | bytes accessed | tf_op | source)
XLA Modules:
  0.0 215.6 jit_solution(13598764132381316774)
XLA Ops:
  1.9 3.9 %collective-permute-start = (bf16[8,2,88]{1,0,2:T(8,128)(2,1)S(1)}, bf16[8,2,88]{1,0,2:T(8,128)(2,1)S(1)}, u32[]{:S(2)}, u32[]{:S(2)}) collective-permute-start(bf16[8,2,88]{1,0,2:T(8,128)(2,1)S(1)} %get-tuple-element.23), channel_id=1, source_target_pairs={{0,1},{1,2},{2,3},{4,5},{5,6},{6,7},{8,9},{9,10},{10,11},{12,13},{... | collective-permute-start | bytes 8456 | tf_op jit(solution)/shard_map/ppermute | solution.py:21
  8.3 3.8 %collective-permute-done.1 = bf16[8,2,88]{1,0,2:T(8,128)(2,1)S(1)} collective-permute-done((bf16[8,2,88]{1,0,2:T(8,128)(2,1)S(1)}, bf16[8,2,88]{1,0,2:T(8,128)(2,1)S(1)}, u32[]{:S(2)}, u32[]{:S(2)}) %collective-permute-start.1) | collective-permute-done | bytes 2848 | tf_op jit(solution)/shard_map/ppermute | solution.py:22
  12.5 16.3 %collective-permute-start.2 = (bf16[2,132,88]{1,0,2:T(2,128)(2,1)S(1)}, bf16[2,132,88]{1,0,2:T(2,128)(2,1)S(1)}, u32[]{:S(2)}, u32[]{:S(2)}) collective-permute-start(bf16[2,132,88]{1,0,2:T(2,128)(2,1)S(1)} %get-tuple-element.19), channel_id=1, source_target_pairs={{0,4},{4,8},{8,12},{12,16},{16,20},{20,24},{24,28},{1,5},{5,9},{9,... | collective-permute-start | bytes 139400 | tf_op jit(solution)/shard_map/ppermute | solution.py:21
  30.3 13.6 %collective-permute-done.3 = bf16[2,132,88]{1,0,2:T(2,128)(2,1)S(1)} collective-permute-done((bf16[2,132,88]{1,0,2:T(2,128)(2,1)S(1)}, bf16[2,132,88]{1,0,2:T(2,128)(2,1)S(1)}, u32[]{:S(2)}, u32[]{:S(2)}) %collective-permute-start.3) | collective-permute-done | bytes 46496 | tf_op jit(solution)/shard_map/ppermute | solution.py:22
  49.6 7.8 %all-to-all-start = ((bf16[8,40,1024]{2,1,0:T(8,128)(2,1)}), bf16[8,40,1024]{2,1,0:T(8,128)(2,1)S(1)}, u32[]{:S(2)}, u32[]{:S(2)}) async-start(bf16[8,40,1024]{2,1,0:T(8,128)(2,1)} %pad_maximum_fusion.1), calls=%async_computation | async-start | bytes 1310720 | tf_op jit(solution)/shard_map/all_to_all | solution.py:139
  58.8 22.8 %all-to-all-done = bf16[8,40,1024]{2,1,0:T(8,128)(2,1)S(1)} async-done(((bf16[8,40,1024]{2,1,0:T(8,128)(2,1)}), bf16[8,40,1024]{2,1,0:T(8,128)(2,1)S(1)}, u32[]{:S(2)}, u32[]{:S(2)}) %all-to-all-start) | async-done | bytes 655392 | tf_op jit(solution)/shard_map/all_to_all | solution.py:139
  81.6 1.9 collective-permute-start.12
  83.6 3.4 %collective-permute-start.11 = (bf16[64,1024]{1,0:T(8,128)(2,1)S(1)}, bf16[64,1024]{1,0:T(8,128)(2,1)}, u32[]{:S(2)}, u32[]{:S(2)}) collective-permute-start(bf16[64,1024]{1,0:T(8,128)(2,1)S(1)} %get-tuple-element.21), channel_id=1, source_target_pairs={{0,8},{4,12},{8,16},{12,20},{16,24},{20,28},{24,0},{28,4},{1,9},{5... | collective-permute-start | bytes 393224 | tf_op jit(solution)/shard_map/ppermute | solution.py:41
  86.9 1.9 collective-permute-start.5
  88.9 3.4 %collective-permute-start.4 = (bf16[64,1024]{1,0:T(8,128)(2,1)S(1)}, bf16[64,1024]{1,0:T(8,128)(2,1)S(1)}, u32[]{:S(2)}, u32[]{:S(2)}) collective-permute-start(bf16[64,1024]{1,0:T(8,128)(2,1)S(1)} %get-tuple-element.22), channel_id=1, source_target_pairs={{0,1},{1,2},{2,3},{3,0},{4,5},{5,6},{6,7},{7,4},{8,9},{9,10},{10,1... | collective-permute-start | bytes 393224 | tf_op jit(solution)/shard_map/ppermute | solution.py:41
  92.4 14.2 %collective-permute-start.18 = (bf16[8,16,1024]{2,1,0:T(8,128)(2,1)S(1)}, bf16[8,16,1024]{2,1,0:T(8,128)(2,1)}, u32[]{:S(2)}, u32[]{:S(2)}) collective-permute-start(bf16[8,16,1024]{2,1,0:T(8,128)(2,1)S(1)} %get-tuple-element.17), channel_id=1, source_target_pairs={{0,32},{32,0},{64,96},{96,64},{128,160},{160,128},{192,224},{224,1... | collective-permute-start | bytes 786440 | tf_op jit(solution)/shard_map/ppermute | solution.py:147
  106.6 2.3 %reshape.131 = bf16[8,3,10,16,2,8]{5,4,3,0,2,1:T(2,128)(2,1)S(1)} reshape(bf16[8,30,256]{2,0,1:T(8,128)(2,1)S(1)} %copy.90) | data formatting | bytes 245760 | tf_op jit(solution)/shard_map/reshape | solution.py:151
  112.9 3.1 %collective-permute-start.6 = (bf16[64,1024]{1,0:T(8,128)(2,1)S(1)}, bf16[64,1024]{1,0:T(8,128)(2,1)S(1)}, u32[]{:S(2)}, u32[]{:S(2)}) collective-permute-start(bf16[64,1024]{1,0:T(8,128)(2,1)S(1)} %collective-permute-done.4), channel_id=1, source_target_pairs={{0,1},{1,2},{2,3},{3,0},{4,5},{5,6},{6,7},{7,4},{8,9},{9,10},{10,1... | collective-permute-start | bytes 393224 | tf_op jit(solution)/shard_map/ppermute | solution.py:48
  116.2 2.0 collective-permute-start.13
  122.1 4.2 %collective-permute-start.8 = (bf16[256,1024]{1,0:T(8,128)(2,1)S(1)}, bf16[256,1024]{1,0:T(8,128)(2,1)S(1)}, u32[]{:S(2)}, u32[]{:S(2)}) collective-permute-start(bf16[256,1024]{1,0:T(8,128)(2,1)S(1)} %pad_maximum_fusion.2.refs_0_), channel_id=1, source_target_pairs={{8,0},{12,4},{16,8},{20,12},{24,16},{28,20},{0,24},{4,28},{9,1},{1... | collective-permute-start | bytes 1572872 | tf_op jit(solution)/shard_map/ppermute | solution.py:42
  126.3 1.9 collective-permute-start.7
  129.3 3.4 %collective-permute-start.15 = (bf16[256,1024]{1,0:T(8,128)(2,1)S(1)}, bf16[256,1024]{1,0:T(8,128)(2,1)S(1)}, u32[]{:S(2)}, u32[]{:S(2)}) collective-permute-start(bf16[256,1024]{1,0:T(8,128)(2,1)S(1)} %pad_maximum_fusion.3.refs_5_), channel_id=1, source_target_pairs={{1,0},{2,1},{3,2},{0,3},{5,4},{6,5},{7,6},{4,7},{9,8},{10,9},{11,1... | collective-permute-start | bytes 1572872 | tf_op jit(solution)/shard_map/ppermute | solution.py:42
  132.7 2.1 collective-permute-start.14
  136.1 3.6 %coef.1.refs_11_ = f32[16,240,128]{2,1,0:T(8,128)} custom-call(f32[240,8]{1,0:T(8,128)} %add_add_fusion.log_ref, f32[8,2048]{1,0:T(8,128)} %slice.177.nodes_ref), custom_call_target="tpu_custom_call" | custom-call | tf_op jit(solution)/shard_map/coef/pallas_call | solution.py:160
  139.7 1.5 fusion.19
  141.2 2.1 stack.51
  144.1 4.6 %collective-permute-start.10 = (bf16[128,1024]{1,0:T(8,128)(2,1)}, bf16[128,1024]{1,0:T(8,128)(2,1)S(1)}, u32[]{:S(2)}, u32[]{:S(2)}) collective-permute-start(bf16[128,1024]{1,0:T(8,128)(2,1)} %slice.161), channel_id=1, source_target_pairs={{8,0},{12,4},{16,8},{20,12},{24,16},{28,20},{0,24},{4,28},{9,1},{1... | collective-permute-start | bytes 786440 | tf_op jit(solution)/shard_map/ppermute | solution.py:56
  149.5 1.9 collective-permute-start.9
  152.3 4.6 %collective-permute-start.17 = (bf16[128,1024]{1,0:T(8,128)(2,1)}, bf16[128,1024]{1,0:T(8,128)(2,1)}, u32[]{:S(2)}, u32[]{:S(2)}) collective-permute-start(bf16[128,1024]{1,0:T(8,128)(2,1)} %slice.164), channel_id=1, source_target_pairs={{1,0},{2,1},{3,2},{0,3},{5,4},{6,5},{7,6},{4,7},{9,8},{10,9},{11,1... | collective-permute-start | bytes 786440 | tf_op jit(solution)/shard_map/ppermute | solution.py:56
  156.8 1.7 slice.163
  158.5 1.9 collective-permute-start.16
  160.4 1.9 fusion
  165.1 2.5 %collective-permute-done.16.refs_8_ = bf16[128,1024]{1,0:T(8,128)(2,1)} collective-permute-done((bf16[128,1024]{1,0:T(8,128)(2,1)}, bf16[128,1024]{1,0:T(8,128)(2,1)}, u32[]{:S(2)}, u32[]{:S(2)}) %collective-permute-start.16) | collective-permute-done | bytes 262176 | tf_op jit(solution)/shard_map/ppermute | solution.py:55
  167.5 7.5 %first.1.refs_14_ = bf16[200,1024]{1,0:T(8,128)(2,1)} custom-call(bf16[256,1024]{1,0:T(8,128)(2,1)} %copy-done.1, bf16[256,1024]{1,0:T(8,128)(2,1)} %copy-done.4, bf16[256,1024]{1,0:T(8,128)(2,1)} %copy-done.3, bf16[128,1024]{1,0:T(8,128)(2,1)} %collective-permute-done.9.refs_3_, bf16[128,1024]{1,0:T(8,128)(2,1)} %copy-done.8, bf16[256,1024]{1,0:T(8,128)(2,1)} %copy-done.2, ...), custom_call_target="tpu_custom_call" | custom-call | tf_op jit(solution)/shard_map/first/pallas_call | solution.py:163
  175.1 5.2 %collective-permute-start.19 = (bf16[200,1024]{1,0:T(8,128)(2,1)}, bf16[200,1024]{1,0:T(8,128)(2,1)S(1)}, u32[]{:S(2)}, u32[]{:S(2)}) collective-permute-start(bf16[200,1024]{1,0:T(8,128)(2,1)} %first.1.refs_14_), channel_id=1, source_target_pairs={{0,32},{32,0},{64,96},{96,64},{128,160},{160,128},{192,224},{224,1... | collective-permute-start | bytes 1228808 | tf_op jit(solution)/shard_map/ppermute | solution.py:169
  182.4 7.6 %second.1 = f32[160,1024]{1,0:T(8,128)} custom-call(bf16[256,1024]{1,0:T(8,128)(2,1)} %copy-done.1, bf16[256,1024]{1,0:T(8,128)(2,1)} %copy-done.4, bf16[256,1024]{1,0:T(8,128)(2,1)} %copy-done.3, bf16[128,1024]{1,0:T(8,128)(2,1)} %collective-permute-done.9.refs_3_, bf16[128,1024]{1,0:T(8,128)(2,1)} %copy-done.8, bf16[256,1024]{1,0:T(8,128)(2,1)} %copy-done.2, ...), custom_call_target="tpu_custom_call" | custom-call | tf_op jit(solution)/shard_map/second/pallas_call | solution.py:174
  192.4 21.5 %all_to_all.10 = bf16[16,64,128]{2,1,0:T(8,128)(2,1)S(1)} all-to-all(bf16[16,64,128]{2,1,0:T(8,128)(2,1)S(1)} %reshape.135), channel_id=1, replica_groups=mesh['quad'=16,'gy'=8,'gx'=4] {'quad'}, dimensions={0} | all-to-all | bytes 524288 | tf_op jit(solution)/shard_map/all_to_all | solution.py:182
  (144 shorter events, 34.6 us)
Async XLA Ops:
  1.9 6.4 %collective-permute-start = (bf16[8,2,88]{1,0,2:T(8,128)(2,1)S(1)}, bf16[8,2,88]{1,0,2:T(8,128)(2,1)S(1)}, u32[]{:S(2)}, u32[]{:S(2)}) collective-permute-start(bf16[8,2,88]{1,0,2:T(8,128)(2,1)S(1)} %get-tuple-element.23), channel_id=1, source_target_pairs={{0,1},{1,2},{2,3},{4,5},{5,6},{6,7},{8,9},{9,10},{10,11},{12,13},{... | collective-permute-start | bytes 8456 | tf_op jit(solution)/shard_map/ppermute | solution.py:21
  5.8 6.2 %collective-permute-start.1 = (bf16[8,2,88]{1,0,2:T(8,128)(2,1)S(1)}, bf16[8,2,88]{1,0,2:T(8,128)(2,1)S(1)}, u32[]{:S(2)}, u32[]{:S(2)}) collective-permute-start(bf16[8,2,88]{1,0,2:T(8,128)(2,1)S(1)} %get-tuple-element.24), channel_id=1, source_target_pairs={{1,0},{2,1},{3,2},{5,4},{6,5},{7,6},{9,8},{10,9},{11,10},{13,12},{... | collective-permute-start | bytes 8456 | tf_op jit(solution)/shard_map/ppermute | solution.py:22
  12.5 17.8 %collective-permute-start.2 = (bf16[2,132,88]{1,0,2:T(2,128)(2,1)S(1)}, bf16[2,132,88]{1,0,2:T(2,128)(2,1)S(1)}, u32[]{:S(2)}, u32[]{:S(2)}) collective-permute-start(bf16[2,132,88]{1,0,2:T(2,128)(2,1)S(1)} %get-tuple-element.19), channel_id=1, source_target_pairs={{0,4},{4,8},{8,12},{12,16},{16,20},{20,24},{24,28},{1,5},{5,9},{9,... | collective-permute-start | bytes 139400 | tf_op jit(solution)/shard_map/ppermute | solution.py:21
  28.8 15.2 %collective-permute-start.3 = (bf16[2,132,88]{1,0,2:T(2,128)(2,1)S(1)}, bf16[2,132,88]{1,0,2:T(2,128)(2,1)S(1)}, u32[]{:S(2)}, u32[]{:S(2)}) collective-permute-start(bf16[2,132,88]{1,0,2:T(2,128)(2,1)S(1)} %get-tuple-element.20), channel_id=1, source_target_pairs={{4,0},{8,4},{12,8},{16,12},{20,16},{24,20},{28,24},{5,1},{9,5},{13... | collective-permute-start | bytes 139400 | tf_op jit(solution)/shard_map/ppermute | solution.py:22
  48.7 8.7 %copy-start.15 = (s32[4]{0:T(128)S(1)}, s32[4]{0:T(128)}, u32[]{:S(2)}) copy-start(s32[4]{0:T(128)} %constant.136.clone) | copy-start | bytes 52
  49.6 32.0 %all-to-all-start = ((bf16[8,40,1024]{2,1,0:T(8,128)(2,1)}), bf16[8,40,1024]{2,1,0:T(8,128)(2,1)S(1)}, u32[]{:S(2)}, u32[]{:S(2)}) async-start(bf16[8,40,1024]{2,1,0:T(8,128)(2,1)} %pad_maximum_fusion.1), calls=%async_computation | async-start | bytes 1310720 | tf_op jit(solution)/shard_map/all_to_all | solution.py:139
  81.6 46.6 %collective-permute-start.12 = (bf16[64,1024]{1,0:T(8,128)(2,1)S(1)}, bf16[64,1024]{1,0:T(8,128)(2,1)}, u32[]{:S(2)}, u32[]{:S(2)}) collective-permute-start(bf16[64,1024]{1,0:T(8,128)(2,1)S(1)} %get-tuple-element.21), channel_id=1, source_target_pairs={{8,0},{12,4},{16,8},{20,12},{24,16},{28,20},{0,24},{4,28},{9,1},{1... | collective-permute-start | bytes 393224 | tf_op jit(solution)/shard_map/ppermute | solution.py:42
  83.6 32.6 %collective-permute-start.11 = (bf16[64,1024]{1,0:T(8,128)(2,1)S(1)}, bf16[64,1024]{1,0:T(8,128)(2,1)}, u32[]{:S(2)}, u32[]{:S(2)}) collective-permute-start(bf16[64,1024]{1,0:T(8,128)(2,1)S(1)} %get-tuple-element.21), channel_id=1, source_target_pairs={{0,8},{4,12},{8,16},{12,20},{16,24},{20,28},{24,0},{28,4},{1,9},{5... | collective-permute-start | bytes 393224 | tf_op jit(solution)/shard_map/ppermute | solution.py:41
  86.9 33.8 %collective-permute-start.5 = (bf16[64,1024]{1,0:T(8,128)(2,1)S(1)}, bf16[64,1024]{1,0:T(8,128)(2,1)}, u32[]{:S(2)}, u32[]{:S(2)}) collective-permute-start(bf16[64,1024]{1,0:T(8,128)(2,1)S(1)} %get-tuple-element.22), channel_id=1, source_target_pairs={{1,0},{2,1},{3,2},{0,3},{5,4},{6,5},{7,6},{4,7},{9,8},{10,9},{11,1... | collective-permute-start | bytes 393224 | tf_op jit(solution)/shard_map/ppermute | solution.py:42
  88.9 24.0 %collective-permute-start.4 = (bf16[64,1024]{1,0:T(8,128)(2,1)S(1)}, bf16[64,1024]{1,0:T(8,128)(2,1)S(1)}, u32[]{:S(2)}, u32[]{:S(2)}) collective-permute-start(bf16[64,1024]{1,0:T(8,128)(2,1)S(1)} %get-tuple-element.22), channel_id=1, source_target_pairs={{0,1},{1,2},{2,3},{3,0},{4,5},{5,6},{6,7},{7,4},{8,9},{9,10},{10,1... | collective-permute-start | bytes 393224 | tf_op jit(solution)/shard_map/ppermute | solution.py:41
  92.4 48.8 %collective-permute-start.18 = (bf16[8,16,1024]{2,1,0:T(8,128)(2,1)S(1)}, bf16[8,16,1024]{2,1,0:T(8,128)(2,1)}, u32[]{:S(2)}, u32[]{:S(2)}) collective-permute-start(bf16[8,16,1024]{2,1,0:T(8,128)(2,1)S(1)} %get-tuple-element.17), channel_id=1, source_target_pairs={{0,32},{32,0},{64,96},{96,64},{128,160},{160,128},{192,224},{224,1... | collective-permute-start | bytes 786440 | tf_op jit(solution)/shard_map/ppermute | solution.py:147
  112.9 7.9 %copy-start.14 = (bf16[64,1024]{1,0:T(8,128)(2,1)}, bf16[64,1024]{1,0:T(8,128)(2,1)S(1)}, u32[]{:S(2)}) copy-start(bf16[64,1024]{1,0:T(8,128)(2,1)S(1)} %collective-permute-done.4) | copy-start | bytes 393220
  112.9 8.1 %collective-permute-start.6 = (bf16[64,1024]{1,0:T(8,128)(2,1)S(1)}, bf16[64,1024]{1,0:T(8,128)(2,1)S(1)}, u32[]{:S(2)}, u32[]{:S(2)}) collective-permute-start(bf16[64,1024]{1,0:T(8,128)(2,1)S(1)} %collective-permute-done.4), channel_id=1, source_target_pairs={{0,1},{1,2},{2,3},{3,0},{4,5},{5,6},{6,7},{7,4},{8,9},{9,10},{10,1... | collective-permute-start | bytes 393224 | tf_op jit(solution)/shard_map/ppermute | solution.py:48
  116.2 12.0 %collective-permute-start.13 = (bf16[64,1024]{1,0:T(8,128)(2,1)}, bf16[64,1024]{1,0:T(8,128)(2,1)S(1)}, u32[]{:S(2)}, u32[]{:S(2)}) collective-permute-start(bf16[64,1024]{1,0:T(8,128)(2,1)} %collective-permute-done.11), channel_id=1, source_target_pairs={{0,8},{4,12},{8,16},{12,20},{16,24},{20,28},{24,0},{28,4},{1,9},{5... | collective-permute-start | bytes 393224 | tf_op jit(solution)/shard_map/ppermute | solution.py:48
  120.7 14.0 %copy-start.11 = (f32[10,1024]{1,0:T(8,128)S(1)}, f32[10,1024]{1,0:T(8,128)}, u32[]{:S(2)}) copy-start(f32[10,1024]{1,0:T(8,128)} %reshape.133) | copy-start | bytes 122884
  120.7 14.0 %copy-start.12 = (f32[10,2048]{1,0:T(8,128)S(1)}, f32[10,2048]{1,0:T(8,128)}, u32[]{:S(2)}) copy-start(f32[10,2048]{1,0:T(8,128)} %constant_dynamic-update-slice_fusion.9) | copy-start | bytes 245764
  122.1 17.7 %copy-start.1 = (bf16[256,1024]{1,0:T(8,128)(2,1)}, bf16[256,1024]{1,0:T(8,128)(2,1)S(1)}, u32[]{:S(2)}) copy-start(bf16[256,1024]{1,0:T(8,128)(2,1)S(1)} %pad_maximum_fusion.2.refs_0_) | copy-start | bytes 1572868
  122.1 21.3 %collective-permute-start.8 = (bf16[256,1024]{1,0:T(8,128)(2,1)S(1)}, bf16[256,1024]{1,0:T(8,128)(2,1)S(1)}, u32[]{:S(2)}, u32[]{:S(2)}) collective-permute-start(bf16[256,1024]{1,0:T(8,128)(2,1)S(1)} %pad_maximum_fusion.2.refs_0_), channel_id=1, source_target_pairs={{8,0},{12,4},{16,8},{20,12},{24,16},{28,20},{0,24},{4,28},{9,1},{1... | collective-permute-start | bytes 1572872 | tf_op jit(solution)/shard_map/ppermute | solution.py:42
  126.3 22.4 %collective-permute-start.7 = (bf16[256,1024]{1,0:T(8,128)(2,1)S(1)}, bf16[256,1024]{1,0:T(8,128)(2,1)S(1)}, u32[]{:S(2)}, u32[]{:S(2)}) collective-permute-start(bf16[256,1024]{1,0:T(8,128)(2,1)S(1)} %pad_maximum_fusion.2.refs_0_), channel_id=1, source_target_pairs={{0,8},{4,12},{8,16},{12,20},{16,24},{20,28},{24,0},{28,4},{1,9},{5... | collective-permute-start | bytes 1572872 | tf_op jit(solution)/shard_map/ppermute | solution.py:41
  129.3 14.1 %copy-start.2 = (bf16[256,1024]{1,0:T(8,128)(2,1)}, bf16[256,1024]{1,0:T(8,128)(2,1)S(1)}, u32[]{:S(2)}) copy-start(bf16[256,1024]{1,0:T(8,128)(2,1)S(1)} %pad_maximum_fusion.3.refs_5_) | copy-start | bytes 1572868
  129.3 22.2 %collective-permute-start.15 = (bf16[256,1024]{1,0:T(8,128)(2,1)S(1)}, bf16[256,1024]{1,0:T(8,128)(2,1)S(1)}, u32[]{:S(2)}, u32[]{:S(2)}) collective-permute-start(bf16[256,1024]{1,0:T(8,128)(2,1)S(1)} %pad_maximum_fusion.3.refs_5_), channel_id=1, source_target_pairs={{1,0},{2,1},{3,2},{0,3},{5,4},{6,5},{7,6},{4,7},{9,8},{10,9},{11,1... | collective-permute-start | bytes 1572872 | tf_op jit(solution)/shard_map/ppermute | solution.py:42
  132.7 24.2 %collective-permute-start.14 = (bf16[256,1024]{1,0:T(8,128)(2,1)S(1)}, bf16[256,1024]{1,0:T(8,128)(2,1)}, u32[]{:S(2)}, u32[]{:S(2)}) collective-permute-start(bf16[256,1024]{1,0:T(8,128)(2,1)S(1)} %pad_maximum_fusion.3.refs_5_), channel_id=1, source_target_pairs={{0,1},{1,2},{2,3},{3,0},{4,5},{5,6},{6,7},{7,4},{8,9},{9,10},{10,1... | collective-permute-start | bytes 1572872 | tf_op jit(solution)/shard_map/ppermute | solution.py:41
  143.4 17.0 %copy-start.6 = (bf16[1,8,16,8,2,64]{5,4,3,2,1,0:T(2,128)(2,1)S(1)}, bf16[1,8,16,8,2,64]{5,4,3,2,1,0:T(2,128)(2,1)}, u32[]{:S(2)}) copy-start(bf16[1,8,16,8,2,64]{5,4,3,2,1,0:T(2,128)(2,1)} %stack.50) | copy-start | bytes 786436
  143.4 17.0 %copy-start.7 = (bf16[1,8,16,8,2,64]{5,4,3,2,1,0:T(2,128)(2,1)S(1)}, bf16[1,8,16,8,2,64]{5,4,3,2,1,0:T(2,128)(2,1)}, u32[]{:S(2)}) copy-start(bf16[1,8,16,8,2,64]{5,4,3,2,1,0:T(2,128)(2,1)} %stack.51) | copy-start | bytes 786436
  143.4 19.0 %copy-start.3 = (bf16[256,1024]{1,0:T(8,128)(2,1)}, bf16[256,1024]{1,0:T(8,128)(2,1)S(1)}, u32[]{:S(2)}) copy-start(bf16[256,1024]{1,0:T(8,128)(2,1)S(1)} %collective-permute-done.8.refs_2_) | copy-start | bytes 1572868
  144.1 20.9 %collective-permute-start.10 = (bf16[128,1024]{1,0:T(8,128)(2,1)}, bf16[128,1024]{1,0:T(8,128)(2,1)S(1)}, u32[]{:S(2)}, u32[]{:S(2)}) collective-permute-start(bf16[128,1024]{1,0:T(8,128)(2,1)} %slice.161), channel_id=1, source_target_pairs={{8,0},{12,4},{16,8},{20,12},{24,16},{28,20},{0,24},{4,28},{9,1},{1... | collective-permute-start | bytes 786440 | tf_op jit(solution)/shard_map/ppermute | solution.py:56
  148.7 13.7 %copy-start.4 = (bf16[256,1024]{1,0:T(8,128)(2,1)}, bf16[256,1024]{1,0:T(8,128)(2,1)S(1)}, u32[]{:S(2)}) copy-start(bf16[256,1024]{1,0:T(8,128)(2,1)S(1)} %collective-permute-done.7.refs_1_) | copy-start | bytes 1572868
  149.5 15.5 %collective-permute-start.9 = (bf16[128,1024]{1,0:T(8,128)(2,1)}, bf16[128,1024]{1,0:T(8,128)(2,1)}, u32[]{:S(2)}, u32[]{:S(2)}) collective-permute-start(bf16[128,1024]{1,0:T(8,128)(2,1)} %slice.160), channel_id=1, source_target_pairs={{0,8},{4,12},{8,16},{12,20},{16,24},{20,28},{24,0},{28,4},{1,9},{5... | collective-permute-start | bytes 786440 | tf_op jit(solution)/shard_map/ppermute | solution.py:55
  151.5 10.9 %copy-start.5 = (bf16[256,1024]{1,0:T(8,128)(2,1)}, bf16[256,1024]{1,0:T(8,128)(2,1)S(1)}, u32[]{:S(2)}) copy-start(bf16[256,1024]{1,0:T(8,128)(2,1)S(1)} %collective-permute-done.15.refs_7_) | copy-start | bytes 1572868
  152.3 12.8 %collective-permute-start.17 = (bf16[128,1024]{1,0:T(8,128)(2,1)}, bf16[128,1024]{1,0:T(8,128)(2,1)}, u32[]{:S(2)}, u32[]{:S(2)}) collective-permute-start(bf16[128,1024]{1,0:T(8,128)(2,1)} %slice.164), channel_id=1, source_target_pairs={{1,0},{2,1},{3,2},{0,3},{5,4},{6,5},{7,6},{4,7},{9,8},{10,9},{11,1... | collective-permute-start | bytes 786440 | tf_op jit(solution)/shard_map/ppermute | solution.py:56
  158.5 9.0 %collective-permute-start.16 = (bf16[128,1024]{1,0:T(8,128)(2,1)}, bf16[128,1024]{1,0:T(8,128)(2,1)}, u32[]{:S(2)}, u32[]{:S(2)}) collective-permute-start(bf16[128,1024]{1,0:T(8,128)(2,1)} %slice.163), channel_id=1, source_target_pairs={{0,1},{1,2},{2,3},{3,0},{4,5},{5,6},{6,7},{7,4},{8,9},{9,10},{10,1... | collective-permute-start | bytes 786440 | tf_op jit(solution)/shard_map/ppermute | solution.py:55
  175.1 6.6 %collective-permute-start.19 = (bf16[200,1024]{1,0:T(8,128)(2,1)}, bf16[200,1024]{1,0:T(8,128)(2,1)S(1)}, u32[]{:S(2)}, u32[]{:S(2)}) collective-permute-start(bf16[200,1024]{1,0:T(8,128)(2,1)} %first.1.refs_14_), channel_id=1, source_target_pairs={{0,32},{32,0},{64,96},{96,64},{128,160},{160,128},{192,224},{224,1... | collective-permute-start | bytes 1228808 | tf_op jit(solution)/shard_map/ppermute | solution.py:169
  (5 other events, 12.0 us)

commit v2 on v0

v2 whole, which is shorter than its diff:
```python
import jax
import jax.numpy as jnp
from jax import lax
from jax.experimental import pallas as pl
from jax.experimental.pallas import tpu as pltpu
from jax.sharding import PartitionSpec as P

STEP = 0.04
BF = jnp.bfloat16
F32 = jnp.float32
VM = pltpu.VMEM
OFFS = (0, -1, 1, 2)
ALL = ("quad", "gy", "gx")


def device(quad, gy, gx):
    return (quad * 8 + gy) * 4 + gx


def plane_shift(phase, step):
    pairs = []
    for quad in range(16):
        for gy in range(8):
            for gx in range(4):
                if (quad + phase) % 2 == 0:
                    to = device(quad, gy, (gx + step) % 4)
                else:
                    to = device(quad, (gy + 2 * step) % 8, gx)
                pairs.append((device(quad, gy, gx), to))
    return pairs


def shape(dims, kind):
    return jax.ShapeDtypeStruct(dims, kind)


def halves(low, high):
    lane = lax.broadcasted_iota(jnp.int32, low.shape, 1)
    return jnp.where(lane < 64, low, high)


def swapped(x):
    return pltpu.roll(x, 64, 1)


def channels_kernel(modes_ref, logs_ref, chan_ref, last_ref, lead_ref, scr_ref, log_ref):
    scr_ref[...] = modes_ref[...].astype(F32)
    log_ref[...] = logs_ref[...]
    zeros = jnp.zeros((48, 128), F32)
    for y in range(8):
        block = scr_ref[pl.ds(y, 64, stride=8), :]
        logs = log_ref[pl.ds(y, 8, stride=8), :]
        high = logs.astype(BF).astype(F32)
        turned = jnp.concatenate([block, high, logs - high, zeros], axis=0).T
        chan_ref[y] = turned
        last_ref[y * 8 : y * 8 + 8] = turned[120:128].astype(BF)
        lead_ref[y * 8 : y * 8 + 8] = turned[0:8].astype(BF)


def pack_rows(ext_ref, r, out_ref, scr_ref):
    scr_ref[...] = jnp.zeros_like(scr_ref)
    scr_ref[0:132, :] = halves(ext_ref[r, 0:132, :], swapped(ext_ref[r + 1, 0:132, :]))
    lane = lax.broadcasted_iota(jnp.int32, (33, 128), 1)
    logs = jnp.zeros((33, 128), F32)
    for g in range(4):
        for k in range(2):
            at = g * 32 + k * 16
            piece = pltpu.roll(ext_ref[r + k, g * 33 : (g + 1) * 33, :], (at - 64) % 128, 1)
            logs = jnp.where((lane >= at) & (lane < at + 16), piece, logs)
    scr_ref[136:169, :] = logs
    out_ref[...] = scr_ref[...].astype(BF)


def edges_kernel(chan_ref, left_ref, right_ref, ext_ref, low_ref, top_ref, scr_ref):
    left, right = left_ref[...].astype(F32), right_ref[...].astype(F32)
    for y in range(8):
        ext_ref[y, 0:2, :] = left[y * 8 + 6 : y * 8 + 8]
        ext_ref[y, 2:130, :] = chan_ref[y]
        ext_ref[y, 130:132, :] = right[y * 8 : y * 8 + 2]
    pack_rows(ext_ref, 6, low_ref, scr_ref)
    pack_rows(ext_ref, 0, top_ref, scr_ref)


def unpack_rows(got_ref, r, full_ref):
    got = got_ref[...].astype(F32)
    modes, logs = got[0:132], got[136:169]
    lane = lax.broadcasted_iota(jnp.int32, (33, 128), 1)
    for k in range(2):
        full_ref[r + k, 0:132, :] = modes if k == 0 else swapped(modes)
        for g in range(4):
            piece = pltpu.roll(logs, (64 - g * 32 - k * 16) % 128, 1)
            old = full_ref[r + k, g * 33 : (g + 1) * 33, :]
            full_ref[r + k, g * 33 : (g + 1) * 33, :] = jnp.where(lane < 64, old, piece)


def patches_kernel(at_ref, ext_ref, above_ref, below_ref, pars_ref, send_ref, logp_ref, full_ref, joint_ref, scr_ref):
    full_ref[2:10, 0:132, :] = ext_ref[:, 0:132, :]
    unpack_rows(above_ref, 0, full_ref)
    unpack_rows(below_ref, 10, full_ref)
    for r in range(6):
        joint_ref[r, 0:132, :] = halves(full_ref[r, 0:132, :], swapped(full_ref[r + 6, 0:132, :]))
    pars = pars_ref[...]
    high = pars.astype(BF).astype(F32)
    for d in range(8):
        for r in range(6):
            scr_ref[r * 20 : r * 20 + 20, :] = joint_ref[r, 16 * d : 16 * d + 20, :]
        scr_ref[120:140, :] = high
        scr_ref[140:160, :] = pars - high
        send_ref[d] = scr_ref[...].astype(BF)
    start = pl.multiple_of(at_ref[0] * 16, 16)
    for r in range(12):
        got = full_ref[r, pl.ds(start, 24), :]
        logp_ref[r * 20 : r * 20 + 20, :] = (got + pltpu.roll(got, 120, 1))[0:20]


def prepare_kernel(at_ref, mine_ref, theirs_ref, logp_ref, state_ref, coef_ref, wr_ref, scr_ref, par_ref):
    core = at_ref[1]
    full = jnp.zeros((8, 128), jnp.int32) + core
    for z in range(8):
        mine, theirs = mine_ref[z].astype(F32), theirs_ref[z].astype(F32)
        scr_ref[z * 160 : (z + 1) * 160, :] = mine
        flag = full[0:1, :] == 0
        zero = jnp.where(flag, mine[0:120], theirs[0:120])
        one = jnp.where(flag, theirs[0:120], mine[0:120])
        both = jnp.concatenate([halves(zero, swapped(one)), halves(swapped(zero), one)], axis=0)
        state_ref[:, z * 128 : (z + 1) * 128] = both.astype(BF)
    sub = lax.broadcasted_iota(jnp.int32, (8, 128), 0)
    grp = lax.broadcasted_iota(jnp.int32, (8, 128), 1) // 16
    for v in range(10):
        for h in range(2):
            at = 120 + v * 2 + h
            got = scr_ref[pl.ds(at, 8, stride=160), :] + scr_ref[pl.ds(at + 20, 8, stride=160), :]
            for s in (1, 2, 4):
                up = pltpu.roll(pltpu.roll(got, 8 - s, 0), 16 * s, 1)
                down = pltpu.roll(pltpu.roll(got, s, 0), 128 - 16 * s, 1)
                mine, bit = (sub & s) > 0, (grp & s) > 0
                got = jnp.where(mine == bit, got, jnp.where(mine, down, up))
            par_ref[v, h * 8 : h * 8 + 8, :] = got
    cols = [logp_ref[:, 64 + j : 65 + j] for j in range(8)]
    for n in range(16):
        p = at_ref[2 + n]
        for v in range(2):
            wr_ref[v, n : n + 1, :] = par_ref[v, pl.ds(p, 1), :]
        acc = cols[0] * par_ref[2, pl.ds(p, 1), :]
        for j in range(1, 8):
            acc = acc + cols[j] * par_ref[2 + j, pl.ds(p, 1), :]
        coef_ref[n] = jnp.exp(acc)


def drive(f_ref, h, coef_ref, c, rows, skip, rate, weight):
    def f(d):
        return f_ref[h, 20 + d : 20 + d + rows, :]

    def k(d):
        return coef_ref[c, skip + 20 + d : skip + 20 + d + rows, :]

    mid, kmid = f(0), k(0)
    total = (kmid + k(-20)) * (f(-20) - mid)
    for d in (20, -1, 1):
        total = total + (kmid + k(d)) * (f(d) - mid)
    total = total + rate * (mid - mid * mid * mid)
    return (weight * total).astype(BF)


def sweep(state, basis_refs, coef_ref, wr_ref, f_ref, acc_ref, rows, skip):
    acc_ref[...] = jnp.zeros_like(acc_ref)
    c = 0
    for ref in basis_refs:
        for s in range(0, ref.shape[0], 256):
            block = ref[s : s + 256, :]
            field = lax.dot_general(state, block, (((1,), (1,)), ((), ())), preferred_element_type=F32)
            parts = []
            for h in range(2):
                f_ref[h, : field.shape[0], :] = field[:, h * 128 : (h + 1) * 128]
                weight, rate = wr_ref[0, c : c + 1, :], wr_ref[1, c : c + 1, :]
                parts.append(drive(f_ref, h, coef_ref, c, rows, skip, rate, weight))
                c += 1
            acc_ref[...] += jnp.dot(jnp.concatenate(parts, axis=1), block, preferred_element_type=F32)


def first_kernel(b0, b1, b2, b3, b4, state_ref, coef_ref, wr_ref, out_ref, f_ref, acc_ref):
    sweep(state_ref[...], (b0, b1, b2, b3, b4), coef_ref, wr_ref, f_ref, acc_ref, 200, 0)
    out_ref[...] = acc_ref[...].astype(BF)


def second_kernel(
    edge_ref, b0, b1, b2, b3, b4, state_ref, coef_ref, wr_ref, own_ref, other_ref, out_ref, f_ref, acc_ref
):
    total = own_ref[...].astype(F32) + other_ref[...].astype(F32)
    now = state_ref[...].astype(F32)[20:220]
    cell = lax.broadcasted_iota(jnp.int32, (200, 128), 0).astype(F32)
    row = jnp.floor((cell + 0.5) * 0.05)
    col = cell - 20.0 * row
    low = jnp.where(edge_ref[0] == 1, 1.0, 0.0)
    high = jnp.where(edge_ref[1] == 1, 8.0, 9.0)
    left = jnp.where(edge_ref[2] == 1, 2.0, 0.0)
    right = jnp.where(edge_ref[3] == 1, 17.0, 19.0)
    inside = (row >= low) & (row <= high) & (col >= left) & (col <= right)
    keep = jnp.where(inside, 1.0, 0.0)[:, 0:1]
    state = ((now + STEP * total) * keep).astype(BF)
    sweep(state, (b0, b1, b2, b3, b4), coef_ref, wr_ref, f_ref, acc_ref, 160, 20)
    for z in range(8):
        for y in range(4):
            low = acc_ref[y * 20 + 2 : y * 20 + 18, z * 128 : (z + 1) * 128]
            high = acc_ref[y * 20 + 82 : y * 20 + 98, z * 128 : (z + 1) * 128]
            out_ref[2 * z, y * 16 : y * 16 + 16, :] = halves(low, swapped(high)).astype(BF)
            out_ref[2 * z + 1, y * 16 : y * 16 + 16, :] = halves(swapped(low), high).astype(BF)


def finish_kernel(back_ref, modes_ref, out_ref, scr_ref):
    for y in range(4):
        parts = [
            back_ref[2 * z, y * 16 : y * 16 + 16, :].astype(F32) + back_ref[2 * z + 1, y * 16 : y * 16 + 16, :].astype(F32)
            for z in range(8)
        ]
        turned = jnp.concatenate(parts, axis=0).T
        scr_ref[pl.ds(y, 64, stride=8), :] = turned[0:64]
        scr_ref[pl.ds(y + 4, 64, stride=8), :] = turned[64:128]
    out_ref[...] = modes_ref[...].astype(F32) + STEP * scr_ref[...]


SMEM = pl.BlockSpec(memory_space=pltpu.SMEM)
WHOLE = pl.BlockSpec(memory_space=pltpu.VMEM)


def call(kernel, outs, scratch, scalars, *args):
    specs = [SMEM] * scalars + [WHOLE] * (len(args) - scalars)
    single = not isinstance(outs, (list, tuple))
    return pl.pallas_call(
        kernel,
        out_shape=outs,
        in_specs=specs,
        out_specs=WHOLE if single else [WHOLE] * len(outs),
        scratch_shapes=scratch,
        name=kernel.__name__,
    )(*args)


def body(modes_now, basis_rows, quad_weights, germ_nodes, log_fields, reaction_rates):
    quad, gy, gx = lax.axis_index("quad"), lax.axis_index("gy"), lax.axis_index("gx")
    zl, core, y, x = quad // 2, quad % 2, gy // 2, gx
    columns = [list(range(0, 16, 2)), list(range(1, 16, 2))]
    swap = [(i, i ^ 1) for i in range(16)]

    part = lax.dynamic_slice_in_dim(basis_rows, (y * 4 + x) * 16, 16, axis=0)
    send = jnp.broadcast_to(part[None], (8, 16, 1024))
    shard = lax.all_to_all(send, "quad", 0, 0, axis_index_groups=columns, tiled=True).reshape(128, 1024)

    modes = modes_now.reshape(512, 128)
    chan, last, lead = call(
        channels_kernel,
        [shape((8, 128, 128), F32), shape((64, 128), BF), shape((64, 128), BF)],
        [VM((512, 128), F32), VM((64, 128), F32)],
        0,
        modes,
        log_fields.reshape(64, 128),
    )
    right = [(i, i + 1) for i in range(3)]
    from_left = lax.ppermute(last, "gx", right)
    from_right = lax.ppermute(lead, "gx", [(j, i) for i, j in right])
    ext, low, top = call(
        edges_kernel,
        [shape((8, 136, 128), F32), shape((176, 128), BF), shape((176, 128), BF)],
        [VM((176, 128), F32)],
        0,
        chan,
        from_left,
        from_right,
    )
    down = [(i, i + 1) for i in range(7)]
    above = lax.ppermute(low, "gy", down)
    below = lax.ppermute(top, "gy", [(j, i) for i, j in down])
    pars = jnp.concatenate([quad_weights[None], reaction_rates[None], germ_nodes.T], axis=0).reshape(20, 128)
    offs = jnp.asarray(OFFS, jnp.int32)
    outer, inner = offs[:, None], offs[None, :]
    dy, dx = jnp.where(core == 0, outer, inner), jnp.where(core == 0, inner, outer)
    order = (((y + dy) % 4) * 4 + (x + dx) % 4).reshape(16)
    at = jnp.concatenate([jnp.stack([zl, core]), order]).astype(jnp.int32)
    patch, logp = call(
        patches_kernel,
        [shape((8, 160, 128), BF), shape((240, 128), F32)],
        [VM((12, 152, 128), F32), VM((6, 136, 128), F32), VM((160, 128), F32)],
        1,
        at,
        ext,
        above,
        below,
        pars,
    )
    mine = lax.all_to_all(patch, "quad", 0, 0, axis_index_groups=columns, tiled=True)
    theirs = lax.ppermute(mine, "quad", swap)

    fwd, bwd = plane_shift(0, 1), plane_shift(0, -1)
    less = lax.ppermute(shard, ALL, fwd)
    more = lax.ppermute(shard, ALL, bwd)
    far = lax.ppermute(less, ALL, fwd)
    line = jnp.concatenate([shard, less, more, far], axis=0)
    fwd, bwd = plane_shift(1, 1), plane_shift(1, -1)
    less = lax.ppermute(line, ALL, fwd)
    more = lax.ppermute(line, ALL, bwd)
    far0 = lax.ppermute(less[:256], ALL, fwd)
    far1 = lax.ppermute(more[256:], ALL, bwd)
    blocks = (line, less, more, far0, far1)

    state, coef, wr = call(
        prepare_kernel,
        [shape((240, 1024), BF), shape((16, 240, 128), F32), shape((2, 16, 128), F32)],
        [VM((1280, 128), F32), VM((10, 16, 128), F32)],
        1,
        at,
        mine,
        theirs,
        logp,
    )
    own = call(
        first_kernel,
        shape((200, 1024), BF),
        [VM((2, 240, 128), F32), VM((200, 1024), F32)],
        0,
        *blocks,
        state,
        coef,
        wr,
    )
    other = lax.ppermute(own, "quad", swap)
    edge = jnp.stack([gy == 0, gy == 7, (gx == 0) & (zl == 0), (gx == 3) & (zl == 7)]).astype(jnp.int32)
    out = call(
        second_kernel,
        shape((16, 64, 128), BF),
        [VM((2, 200, 128), F32), VM((160, 1024), F32)],
        1,
        edge,
        *blocks,
        state,
        coef,
        wr,
        own,
        other,
    )
    back = lax.all_to_all(out, "quad", 0, 0, tiled=True)
    result = call(finish_kernel, shape((512, 128), F32), [VM((512, 128), F32)], 0, back, modes)
    return result.reshape(64, 8, 128)


def solution(mesh):
    in_specs = (
        P("quad", "gy", "gx"),
        P("quad", None),
        P("quad"),
        P("quad", None),
        P(None, "gy", "gx"),
        P("quad"),
    )
    out_specs = P("quad", "gy", "gx")
    return jax.shard_map(body, mesh=mesh, in_specs=in_specs, out_specs=out_specs, check_vma=False)
```

time: 530 us -> 156 us (0.29); the launches traced: 522 us -> 154 us
  waiting for transfers between devices: 438 us -> 9.12 us
  blocking collectives: 0 us -> 46.6 us
  Pallas kernels: 0 us -> 28.6 us
  starting transfers between devices: 44.4 us -> 58.5 us
  between operations: 13.4 us -> 0.28 us
  matrix products: 9.14 us -> 0 us
    unnamed x6 -> x0, waiting for transfers between devices: 221 us -> none
    all_gather x2 -> x0, waiting for transfers between devices: 179 us -> none  [realize(): lax.all_gather(block_flat, 'quad', axis=0, tiled=True)]
    all_to_all x0 -> x2, blocking collectives: none -> 46.6 us  [the longest x1 25.1 us: body(): lax.all_to_all(send, 'quad', 0, 0, axis_index_groups=columns, tiled=True)]
    ppermute x12 -> x13, waiting for transfers between devices: 38.3 us -> 6.25 us  [the longest x1 4.07 us: body(): below = lax.ppermute(top, 'gy', [(j, i) for i, j in down])]
    pallas_call x0 -> x7, Pallas kernels: none -> 28.6 us  [call(): pl.pallas_call(kernel, out_shape=outs, in_specs=specs, out_specs=WHOLE if...]
    dot_general x5 -> x0, matrix products: 9.14 us -> none  [the longest x2 4.87 us: realize(): jnp.dot(basis_rows, lax.all_gather(block_flat, 'quad', axis=0, tiled=True...]
    all_to_all x0 -> x1, starting transfers between devices: none -> 9.02 us  [body(): lax.all_to_all(patch, 'quad', 0, 0, axis_index_groups=columns, tiled=True)]
    unnamed x20 -> x22, local copies, waits for them, and re-layouts: 11.8 us -> 4.54 us
  transfers between devices with their start and end apart: 16 -> 14, of which waited for: 10 -> 4; matrix products, arithmetic and copies ran while one was open for 1% -> 4% of each run, Pallas kernels for 0% -> 8%
where the time goes in v2:
time: 156 us; the launch traced here: 154 us
  starting transfers between devices  58.5 us (38%)
  blocking collectives  46.6 us (30%)
  Pallas kernels  28.6 us (18%)
  waiting for transfers between devices  9.12 us (6%)
  local copies, waits for them, and re-layouts  8.11 us (5%)
  other arithmetic  2.88 us (2%)
    pallas_call x7, Pallas kernels, call(): pl.pallas_call(kernel, out_shape=outs, in_specs=specs, out_specs=WHOLE if...  28.6 us
    all_to_all x1, blocking collectives, body(): lax.all_to_all(send, 'quad', 0, 0, axis_index_groups=columns, tiled=True)  25.1 us
    all_to_all x1, blocking collectives, body(): back = lax.all_to_all(out, 'quad', 0, 0, tiled=True)  21.5 us
    ppermute x1, starting transfers between devices, body(): theirs = lax.ppermute(mine, 'quad', swap)  10.9 us
    all_to_all x1, starting transfers between devices, body(): lax.all_to_all(patch, 'quad', 0, 0, axis_index_groups=columns, tiled=True)  9.02 us
    ppermute x1, starting transfers between devices, body(): above = lax.ppermute(low, 'gy', down)  7.93 us
    ppermute x1, starting transfers between devices, body(): more = lax.ppermute(line, ALL, bwd)  5.26 us
    ppermute x1, starting transfers between devices, body(): far1 = lax.ppermute(more[256:], ALL, bwd)  5.2 us
  transfers between devices with their start and end apart: 14, of which 4 were waited for; matrix products, arithmetic and copies ran while one was open for 4% of the time, Pallas kernels for 8%

profile of v2, /device:TPU:1, one launch (start us, length us, event | category | flops | bytes accessed | tf_op | source)
XLA Modules:
  0.0 154.0 jit_solution(15638822113936331128)
XLA Ops:
  0.0 1.0 copy-done
  1.1 25.1 %all_to_all.15 = bf16[8,16,1024]{2,1,0:T(8,128)(2,1)S(1)} all-to-all(bf16[8,16,1024]{2,1,0:T(8,128)(2,1)S(1)} %broadcast_in_dim.42), channel_id=1, replica_groups={{0,64,128,192,256,320,384,448},{32,96,160,224,288,352,416,480},{1,65,12..., dimensions={0} | all-to-all | bytes 524288 | tf_op jit(solution)/shard_map/all_to_all | solution.py:247
  26.2 3.2 %collective-permute-start = (bf16[128,1024]{1,0:T(8,128)(2,1)S(1)}, bf16[128,1024]{1,0:T(8,128)(2,1)S(1)}, u32[]{:S(2)}, u32[]{:S(2)}) collective-permute-start(bf16[128,1024]{1,0:T(8,128)(2,1)S(1)} %bitcast.13), channel_id=1, source_target_pairs={{0,1},{1,2},{2,3},{3,0},{4,5},{5,6},{6,7},{7,4},{8,9},{9,10},{10,1... | collective-permute-start | bytes 786440 | tf_op jit(solution)/shard_map/ppermute | solution.py:294
  29.4 1.9 %channels_kernel.1 = (f32[8,128,128]{2,1,0:T(8,128)}, bf16[64,128]{1,0:T(8,128)(2,1)}, bf16[64,128]{1,0:T(8,128)(2,1)}) custom-call(bf16[512,128]{1,0:T(8,128)(2,1)} %bitcast.16, f32[64,128]{1,0:T(8,128)} %bitcast.18), custom_call_target="tpu_custom_call" | custom-call | tf_op jit(solution)/shard_map/channels_kernel/pallas_call | solution.py:229
  31.3 3.1 %collective-permute-start.7 = (bf16[64,128]{1,0:T(8,128)(2,1)}, bf16[64,128]{1,0:T(8,128)(2,1)S(1)}, u32[]{:S(2)}, u32[]{:S(2)}) collective-permute-start(bf16[64,128]{1,0:T(8,128)(2,1)} %get-tuple-element.17), channel_id=1, source_target_pairs={{0,1},{1,2},{2,3},{4,5},{5,6},{6,7},{8,9},{9,10},{10,11},{12,13},{... | collective-permute-start | bytes 49160 | tf_op jit(solution)/shard_map/ppermute | solution.py:259
  34.4 1.3 collective-permute-start.8
  35.8 0.8 select_add_fusion
  36.7 3.3 %collective-permute-start.1 = (bf16[128,1024]{1,0:T(8,128)(2,1)S(1)}, bf16[128,1024]{1,0:T(8,128)(2,1)S(1)}, u32[]{:S(2)}, u32[]{:S(2)}) collective-permute-start(bf16[128,1024]{1,0:T(8,128)(2,1)S(1)} %bitcast.14), channel_id=1, source_target_pairs={{0,3},{1,0},{2,1},{3,2},{4,7},{5,4},{6,5},{7,6},{8,11},{9,8},{10,9... | collective-permute-start | bytes 786440 | tf_op jit(solution)/shard_map/ppermute | solution.py:295
  40.1 1.9 %collective-permute-start.2 = (bf16[128,1024]{1,0:T(8,128)(2,1)S(1)}, bf16[128,1024]{1,0:T(8,128)(2,1)S(1)}, u32[]{:S(2)}, u32[]{:S(2)}) collective-permute-start(bf16[128,1024]{1,0:T(8,128)(2,1)S(1)} %collective-permute-done), channel_id=1, source_target_pairs={{0,1},{1,2},{2,3},{3,0},{4,5},{5,6},{6,7},{7,4},{8,9},{9,10},{10,1... | collective-permute-start | bytes 786440 | tf_op jit(solution)/shard_map/ppermute | solution.py:296
  43.4 2.0 %edges_kernel.1 = (f32[8,136,128]{2,1,0:T(8,128)}, bf16[176,128]{1,0:T(8,128)(2,1)}, bf16[176,128]{1,0:T(8,128)(2,1)}) custom-call(f32[8,128,128]{2,1,0:T(8,128)} %get-tuple-element.16.chan_ref, bf16[64,128]{1,0:T(8,128)(2,1)} %copy-done.9, bf16[64,128]{1,0:T(8,128)(2,1)} %copy-done.10), custom_call_target="tpu_custom_call" | custom-call | tf_op jit(solution)/shard_map/edges_kernel/pallas_call | solution.py:229
  45.4 7.9 %collective-permute-start.9 = (bf16[176,128]{1,0:T(8,128)(2,1)}, bf16[176,128]{1,0:T(8,128)(2,1)S(1)}, u32[]{:S(2)}, u32[]{:S(2)}) collective-permute-start(bf16[176,128]{1,0:T(8,128)(2,1)} %get-tuple-element.20), channel_id=1, source_target_pairs={{0,4},{4,8},{8,12},{12,16},{16,20},{20,24},{24,28},{1,5},{5,9},{9,... | collective-permute-start | bytes 135176 | tf_op jit(solution)/shard_map/ppermute | solution.py:271
  53.4 1.3 collective-permute-start.10
  54.8 5.3 %collective-permute-start.4 = (bf16[512,1024]{1,0:T(8,128)(2,1)S(1)}, bf16[512,1024]{1,0:T(8,128)(2,1)S(1)}, u32[]{:S(2)}, u32[]{:S(2)}) collective-permute-start(bf16[512,1024]{1,0:T(8,128)(2,1)S(1)} %pad_maximum_fusion.b0), channel_id=1, source_target_pairs={{0,24},{1,25},{2,26},{3,27},{4,28},{5,29},{6,30},{7,31},{8,0},{9,1... | collective-permute-start | bytes 3145736 | tf_op jit(solution)/shard_map/ppermute | solution.py:300
  60.0 1.9 %collective-permute-start.3 = (bf16[512,1024]{1,0:T(8,128)(2,1)S(1)}, bf16[512,1024]{1,0:T(8,128)(2,1)}, u32[]{:S(2)}, u32[]{:S(2)}) collective-permute-start(bf16[512,1024]{1,0:T(8,128)(2,1)S(1)} %pad_maximum_fusion.b0), channel_id=1, source_target_pairs={{0,8},{1,9},{2,10},{3,11},{4,12},{5,13},{6,14},{7,15},{8,16},{9,17... | collective-permute-start | bytes 3145736 | tf_op jit(solution)/shard_map/ppermute | solution.py:299
  63.2 4.1 %collective-permute-done.10.below_ref = bf16[176,128]{1,0:T(8,128)(2,1)S(1)} collective-permute-done((bf16[176,128]{1,0:T(8,128)(2,1)}, bf16[176,128]{1,0:T(8,128)(2,1)S(1)}, u32[]{:S(2)}, u32[]{:S(2)}) %collective-permute-start.10) | collective-permute-done | bytes 45088 | tf_op jit(solution)/shard_map/ppermute | solution.py:272
  67.9 2.1 %patches_kernel.1 = (bf16[8,160,128]{2,1,0:T(8,128)(2,1)}, f32[240,128]{1,0:T(8,128)}) custom-call(s32[18]{0:T(128)} %pad_add_fusion.at_ref, f32[8,136,128]{2,1,0:T(8,128)} %get-tuple-element.19.ext_ref, bf16[176,128]{1,0:T(8,128)(2,1)} %copy-done.7, bf16[176,128]{1,0:T(8,128)(2,1)} %copy-done.8, f32[20,128]{1,0:T(8,128)} %reshape.34.pars_ref), custom_call_target="tpu_custom_call" | custom-call | tf_op jit(solution)/shard_map/patches_kernel/pallas_call | solution.py:229
  70.0 9.0 %all-to-all-start.1 = ((bf16[8,160,128]{2,1,0:T(8,128)(2,1)}), bf16[8,160,128]{2,1,0:T(8,128)(2,1)S(1)}, u32[]{:S(2)}, u32[]{:S(2)}) async-start(bf16[8,160,128]{2,1,0:T(8,128)(2,1)} %get-tuple-element.22), calls=%async_computation.1 | async-start | bytes 655360 | tf_op jit(solution)/shard_map/all_to_all | solution.py:290
  79.1 0.9 slice.9
  80.0 5.2 %collective-permute-start.6 = (bf16[256,1024]{1,0:T(8,128)(2,1)}, bf16[256,1024]{1,0:T(8,128)(2,1)S(1)}, u32[]{:S(2)}, u32[]{:S(2)}) collective-permute-start(bf16[256,1024]{1,0:T(8,128)(2,1)} %slice.9), channel_id=1, source_target_pairs={{0,24},{1,25},{2,26},{3,27},{4,28},{5,29},{6,30},{7,31},{8,0},{9,1... | collective-permute-start | bytes 1572872 | tf_op jit(solution)/shard_map/ppermute | solution.py:302
  85.2 1.9 %slice.8 = bf16[256,1024]{1,0:T(8,128)(2,1)} slice(bf16[512,1024]{1,0:T(8,128)(2,1)} %collective-permute-done.3.b1), slice={[0:256], [0:1024]} | slice | bytes 1048576 | tf_op jit(solution)/shard_map/slice | solution.py:301
  87.1 1.9 %collective-permute-start.5 = (bf16[256,1024]{1,0:T(8,128)(2,1)}, bf16[256,1024]{1,0:T(8,128)(2,1)}, u32[]{:S(2)}, u32[]{:S(2)}) collective-permute-start(bf16[256,1024]{1,0:T(8,128)(2,1)} %slice.8), channel_id=1, source_target_pairs={{0,8},{1,9},{2,10},{3,11},{4,12},{5,13},{6,14},{7,15},{8,16},{9,17... | collective-permute-start | bytes 1572872 | tf_op jit(solution)/shard_map/ppermute | solution.py:301
  89.0 2.9 %all-to-all-done.1.mine_ref = bf16[8,160,128]{2,1,0:T(8,128)(2,1)S(1)} async-done(((bf16[8,160,128]{2,1,0:T(8,128)(2,1)}), bf16[8,160,128]{2,1,0:T(8,128)(2,1)S(1)}, u32[]{:S(2)}, u32[]{:S(2)}) %all-to-all-start.1) | async-done | bytes 327712 | tf_op jit(solution)/shard_map/all_to_all | solution.py:290
  91.9 10.9 %collective-permute-start.11 = (bf16[8,160,128]{2,1,0:T(8,128)(2,1)S(1)}, bf16[8,160,128]{2,1,0:T(8,128)(2,1)S(1)}, u32[]{:S(2)}, u32[]{:S(2)}) collective-permute-start(bf16[8,160,128]{2,1,0:T(8,128)(2,1)S(1)} %all-to-all-done.1.mine_ref), channel_id=1, source_target_pairs={{0,32},{32,0},{64,96},{96,64},{128,160},{160,128},{192,224},{224,1... | collective-permute-start | bytes 983048 | tf_op jit(solution)/shard_map/ppermute | solution.py:291
  102.7 1.2 collective-permute-done.11.theirs_ref
  104.7 6.6 %prepare_kernel.1 = (bf16[240,1024]{1,0:T(8,128)(2,1)}, f32[16,240,128]{2,1,0:T(8,128)}, f32[2,16,128]{2,1,0:T(8,128)}) custom-call(s32[18]{0:T(128)} %pad_add_fusion.at_ref, bf16[8,160,128]{2,1,0:T(8,128)(2,1)} %copy-done.4, bf16[8,160,128]{2,1,0:T(8,128)(2,1)} %copy-done.6, f32[240,128]{1,0:T(8,128)} %get-tuple-element.23.logp_ref), custom_call_target="tpu_custom_call" | custom-call | tf_op jit(solution)/shard_map/prepare_kernel/pallas_call | solution.py:229
  111.3 0.8 copy-done.3
  112.1 6.9 %first_kernel.1.own_ref = bf16[200,1024]{1,0:T(8,128)(2,1)} custom-call(bf16[512,1024]{1,0:T(8,128)(2,1)} %copy-done.1, bf16[512,1024]{1,0:T(8,128)(2,1)} %collective-permute-done.3.b1, bf16[512,1024]{1,0:T(8,128)(2,1)} %copy-done.2, bf16[256,1024]{1,0:T(8,128)(2,1)} %collective-permute-done.5.b3, bf16[256,1024]{1,0:T(8,128)(2,1)} %copy-done.3, ...), custom_call_target="tpu_custom_call" | custom-call | tf_op jit(solution)/shard_map/first_kernel/pallas_call | solution.py:229
  119.0 2.3 %collective-permute-start.12 = (bf16[200,1024]{1,0:T(8,128)(2,1)}, bf16[200,1024]{1,0:T(8,128)(2,1)S(1)}, u32[]{:S(2)}, u32[]{:S(2)}) collective-permute-start(bf16[200,1024]{1,0:T(8,128)(2,1)} %first_kernel.1.own_ref), channel_id=1, source_target_pairs={{0,32},{32,0},{64,96},{96,64},{128,160},{160,128},{192,224},{224,1... | collective-permute-start | bytes 1228808 | tf_op jit(solution)/shard_map/ppermute | solution.py:325
  122.0 0.9 collective-permute-done.12.other_ref
  123.7 7.1 %second_kernel.1 = bf16[16,64,128]{2,1,0:T(8,128)(2,1)} custom-call(s32[4]{0:T(128)} %add_convert_fusion.edge_ref, bf16[512,1024]{1,0:T(8,128)(2,1)} %copy-done.1, bf16[512,1024]{1,0:T(8,128)(2,1)} %collective-permute-done.3.b1, bf16[512,1024]{1,0:T(8,128)(2,1)} %copy-done.2, bf16[256,1024]{1,0:T(8,128)(2,1)} %collective-permute-done.5.b3, ...), custom_call_target="tpu_custom_call" | custom-call | tf_op jit(solution)/shard_map/second_kernel/pallas_call | solution.py:229
  130.7 21.5 %all_to_all.16.back_ref = bf16[16,64,128]{2,1,0:T(8,128)(2,1)} all-to-all(bf16[16,64,128]{2,1,0:T(8,128)(2,1)} %second_kernel.1), channel_id=1, replica_groups=mesh['quad'=16,'gy'=8,'gx'=4] {'quad'}, dimensions={0} | all-to-all | bytes 524288 | tf_op jit(solution)/shard_map/all_to_all | solution.py:340
  152.2 1.8 %finish_kernel.1 = f32[512,128]{1,0:T(8,128)} custom-call(bf16[16,64,128]{2,1,0:T(8,128)(2,1)} %all_to_all.16.back_ref, bf16[512,128]{1,0:T(8,128)(2,1)} %bitcast.17), custom_call_target="tpu_custom_call" | custom-call | tf_op jit(solution)/shard_map/finish_kernel/pallas_call | solution.py:229
  (40 shorter events, 5.6 us)
Async XLA Ops:
  0.0 1.0 copy-start
  26.2 13.9 %collective-permute-start = (bf16[128,1024]{1,0:T(8,128)(2,1)S(1)}, bf16[128,1024]{1,0:T(8,128)(2,1)S(1)}, u32[]{:S(2)}, u32[]{:S(2)}) collective-permute-start(bf16[128,1024]{1,0:T(8,128)(2,1)S(1)} %bitcast.13), channel_id=1, source_target_pairs={{0,1},{1,2},{2,3},{3,0},{4,5},{5,6},{6,7},{7,4},{8,9},{9,10},{10,1... | collective-permute-start | bytes 786440 | tf_op jit(solution)/shard_map/ppermute | solution.py:294
  31.3 11.5 %collective-permute-start.7 = (bf16[64,128]{1,0:T(8,128)(2,1)}, bf16[64,128]{1,0:T(8,128)(2,1)S(1)}, u32[]{:S(2)}, u32[]{:S(2)}) collective-permute-start(bf16[64,128]{1,0:T(8,128)(2,1)} %get-tuple-element.17), channel_id=1, source_target_pairs={{0,1},{1,2},{2,3},{4,5},{5,6},{6,7},{8,9},{9,10},{10,11},{12,13},{... | collective-permute-start | bytes 49160 | tf_op jit(solution)/shard_map/ppermute | solution.py:259
  34.4 8.4 %collective-permute-start.8 = (bf16[64,128]{1,0:T(8,128)(2,1)}, bf16[64,128]{1,0:T(8,128)(2,1)S(1)}, u32[]{:S(2)}, u32[]{:S(2)}) collective-permute-start(bf16[64,128]{1,0:T(8,128)(2,1)} %get-tuple-element.18), channel_id=1, source_target_pairs={{1,0},{2,1},{3,2},{5,4},{6,5},{7,6},{9,8},{10,9},{11,10},{13,12},{... | collective-permute-start | bytes 49160 | tf_op jit(solution)/shard_map/ppermute | solution.py:260
  36.7 17.9 %collective-permute-start.1 = (bf16[128,1024]{1,0:T(8,128)(2,1)S(1)}, bf16[128,1024]{1,0:T(8,128)(2,1)S(1)}, u32[]{:S(2)}, u32[]{:S(2)}) collective-permute-start(bf16[128,1024]{1,0:T(8,128)(2,1)S(1)} %bitcast.14), channel_id=1, source_target_pairs={{0,3},{1,0},{2,1},{3,2},{4,7},{5,4},{6,5},{7,6},{8,11},{9,8},{10,9... | collective-permute-start | bytes 786440 | tf_op jit(solution)/shard_map/ppermute | solution.py:295
  40.1 14.6 %collective-permute-start.2 = (bf16[128,1024]{1,0:T(8,128)(2,1)S(1)}, bf16[128,1024]{1,0:T(8,128)(2,1)S(1)}, u32[]{:S(2)}, u32[]{:S(2)}) collective-permute-start(bf16[128,1024]{1,0:T(8,128)(2,1)S(1)} %collective-permute-done), channel_id=1, source_target_pairs={{0,1},{1,2},{2,3},{3,0},{4,5},{5,6},{6,7},{7,4},{8,9},{9,10},{10,1... | collective-permute-start | bytes 786440 | tf_op jit(solution)/shard_map/ppermute | solution.py:296
  42.8 0.6 copy-start.9
  42.8 0.6 copy-start.10
  45.4 17.8 %collective-permute-start.9 = (bf16[176,128]{1,0:T(8,128)(2,1)}, bf16[176,128]{1,0:T(8,128)(2,1)S(1)}, u32[]{:S(2)}, u32[]{:S(2)}) collective-permute-start(bf16[176,128]{1,0:T(8,128)(2,1)} %get-tuple-element.20), channel_id=1, source_target_pairs={{0,4},{4,8},{8,12},{12,16},{16,20},{20,24},{24,28},{1,5},{5,9},{9,... | collective-permute-start | bytes 135176 | tf_op jit(solution)/shard_map/ppermute | solution.py:271
  53.4 13.9 %collective-permute-start.10 = (bf16[176,128]{1,0:T(8,128)(2,1)}, bf16[176,128]{1,0:T(8,128)(2,1)S(1)}, u32[]{:S(2)}, u32[]{:S(2)}) collective-permute-start(bf16[176,128]{1,0:T(8,128)(2,1)} %get-tuple-element.21), channel_id=1, source_target_pairs={{4,0},{8,4},{12,8},{16,12},{20,16},{24,20},{28,24},{5,1},{9,5},{13... | collective-permute-start | bytes 135176 | tf_op jit(solution)/shard_map/ppermute | solution.py:272
  54.8 56.6 %copy-start.1 = (bf16[512,1024]{1,0:T(8,128)(2,1)}, bf16[512,1024]{1,0:T(8,128)(2,1)S(1)}, u32[]{:S(2)}) copy-start(bf16[512,1024]{1,0:T(8,128)(2,1)S(1)} %pad_maximum_fusion.b0) | copy-start | bytes 3145732
  54.8 24.3 %collective-permute-start.4 = (bf16[512,1024]{1,0:T(8,128)(2,1)S(1)}, bf16[512,1024]{1,0:T(8,128)(2,1)S(1)}, u32[]{:S(2)}, u32[]{:S(2)}) collective-permute-start(bf16[512,1024]{1,0:T(8,128)(2,1)S(1)} %pad_maximum_fusion.b0), channel_id=1, source_target_pairs={{0,24},{1,25},{2,26},{3,27},{4,28},{5,29},{6,30},{7,31},{8,0},{9,1... | collective-permute-start | bytes 3145736 | tf_op jit(solution)/shard_map/ppermute | solution.py:300
  60.0 25.2 %collective-permute-start.3 = (bf16[512,1024]{1,0:T(8,128)(2,1)S(1)}, bf16[512,1024]{1,0:T(8,128)(2,1)}, u32[]{:S(2)}, u32[]{:S(2)}) collective-permute-start(bf16[512,1024]{1,0:T(8,128)(2,1)S(1)} %pad_maximum_fusion.b0), channel_id=1, source_target_pairs={{0,8},{1,9},{2,10},{3,11},{4,12},{5,13},{6,14},{7,15},{8,16},{9,17... | collective-permute-start | bytes 3145736 | tf_op jit(solution)/shard_map/ppermute | solution.py:299
  63.2 4.1 %copy-start.7 = (bf16[176,128]{1,0:T(8,128)(2,1)}, bf16[176,128]{1,0:T(8,128)(2,1)S(1)}, u32[]{:S(2)}) copy-start(bf16[176,128]{1,0:T(8,128)(2,1)S(1)} %collective-permute-done.9.above_ref) | copy-start | bytes 135172
  67.3 0.6 copy-start.8
  70.0 21.8 %all-to-all-start.1 = ((bf16[8,160,128]{2,1,0:T(8,128)(2,1)}), bf16[8,160,128]{2,1,0:T(8,128)(2,1)S(1)}, u32[]{:S(2)}, u32[]{:S(2)}) async-start(bf16[8,160,128]{2,1,0:T(8,128)(2,1)} %get-tuple-element.22), calls=%async_computation.1 | async-start | bytes 655360 | tf_op jit(solution)/shard_map/all_to_all | solution.py:290
  79.1 32.3 %copy-start.2 = (bf16[512,1024]{1,0:T(8,128)(2,1)}, bf16[512,1024]{1,0:T(8,128)(2,1)S(1)}, u32[]{:S(2)}) copy-start(bf16[512,1024]{1,0:T(8,128)(2,1)S(1)} %collective-permute-done.4.b2) | copy-start | bytes 3145732
  80.0 31.3 %collective-permute-start.6 = (bf16[256,1024]{1,0:T(8,128)(2,1)}, bf16[256,1024]{1,0:T(8,128)(2,1)S(1)}, u32[]{:S(2)}, u32[]{:S(2)}) collective-permute-start(bf16[256,1024]{1,0:T(8,128)(2,1)} %slice.9), channel_id=1, source_target_pairs={{0,24},{1,25},{2,26},{3,27},{4,28},{5,29},{6,30},{7,31},{8,0},{9,1... | collective-permute-start | bytes 1572872 | tf_op jit(solution)/shard_map/ppermute | solution.py:302
  87.1 24.2 %collective-permute-start.5 = (bf16[256,1024]{1,0:T(8,128)(2,1)}, bf16[256,1024]{1,0:T(8,128)(2,1)}, u32[]{:S(2)}, u32[]{:S(2)}) collective-permute-start(bf16[256,1024]{1,0:T(8,128)(2,1)} %slice.8), channel_id=1, source_target_pairs={{0,8},{1,9},{2,10},{3,11},{4,12},{5,13},{6,14},{7,15},{8,16},{9,17... | collective-permute-start | bytes 1572872 | tf_op jit(solution)/shard_map/ppermute | solution.py:301
  91.9 12.8 %copy-start.4 = (bf16[8,160,128]{2,1,0:T(8,128)(2,1)}, bf16[8,160,128]{2,1,0:T(8,128)(2,1)S(1)}, u32[]{:S(2)}) copy-start(bf16[8,160,128]{2,1,0:T(8,128)(2,1)S(1)} %all-to-all-done.1.mine_ref) | copy-start | bytes 983044
  91.9 12.1 %collective-permute-start.11 = (bf16[8,160,128]{2,1,0:T(8,128)(2,1)S(1)}, bf16[8,160,128]{2,1,0:T(8,128)(2,1)S(1)}, u32[]{:S(2)}, u32[]{:S(2)}) collective-permute-start(bf16[8,160,128]{2,1,0:T(8,128)(2,1)S(1)} %all-to-all-done.1.mine_ref), channel_id=1, source_target_pairs={{0,32},{32,0},{64,96},{96,64},{128,160},{160,128},{192,224},{224,1... | collective-permute-start | bytes 983048 | tf_op jit(solution)/shard_map/ppermute | solution.py:291
  104.0 0.7 copy-start.6
  111.3 0.8 copy-start.3
  119.0 3.8 %collective-permute-start.12 = (bf16[200,1024]{1,0:T(8,128)(2,1)}, bf16[200,1024]{1,0:T(8,128)(2,1)S(1)}, u32[]{:S(2)}, u32[]{:S(2)}) collective-permute-start(bf16[200,1024]{1,0:T(8,128)(2,1)} %first_kernel.1.own_ref), channel_id=1, source_target_pairs={{0,32},{32,0},{64,96},{96,64},{128,160},{160,128},{192,224},{224,1... | collective-permute-start | bytes 1228808 | tf_op jit(solution)/shard_map/ppermute | solution.py:325
  122.9 0.8 copy-start.5

commit v3 on v2

v3 whole, which is shorter than its diff:
```python
import jax
import jax.numpy as jnp
from jax import lax
from jax.experimental import pallas as pl
from jax.experimental.pallas import tpu as pltpu
from jax.sharding import PartitionSpec as P


STEP = 0.04
BF = jnp.bfloat16
F32 = jnp.float32
VM = pltpu.VMEM
OFFS = (0, -1, 1, 2)
ARRIVAL = tuple((o, i) for o, half in ((0, 0), (0, 2), (1, 0), (2, 0), (1, 2), (2, 2), (3, 0), (3, 2)) for i in (half, half + 1))
ALL = ("quad", "gy", "gx")


def device(quad, gy, gx):
    return (quad * 8 + gy) * 4 + gx


def plane_shift(phase, step):
    pairs = []
    for quad in range(16):
        for gy in range(8):
            for gx in range(4):
                if (quad + phase) % 2 == 0:
                    to = device(quad, gy, (gx + step) % 4)
                else:
                    to = device(quad, (gy + 2 * step) % 8, gx)
                pairs.append((device(quad, gy, gx), to))
    return pairs


def shape(dims, kind):
    return jax.ShapeDtypeStruct(dims, kind)


def halves(low, high):
    lane = lax.broadcasted_iota(jnp.int32, low.shape, 1)
    return jnp.where(lane < 64, low, high)


def swapped(x):
    return pltpu.roll(x, 64, 1)


def rows_kernel(modes_ref, logs_ref, low_ref, top_ref, scr_ref, log_ref):
    scr_ref[...] = modes_ref[...].astype(F32)
    log_ref[...] = logs_ref[...]
    for out_ref, first in ((low_ref, 6), (top_ref, 0)):
        for k in range(2):
            logs = log_ref[pl.ds(first + k, 8, stride=8), :]
            high = logs.astype(BF).astype(F32)
            block = scr_ref[pl.ds(first + k, 64, stride=8), :]
            out_ref[k * 80 : k * 80 + 80, :] = jnp.concatenate([block, high, logs - high], axis=0).astype(BF)


def channels_kernel(modes_ref, logs_ref, chan_ref, scr_ref, log_ref):
    scr_ref[...] = modes_ref[...].astype(F32)
    log_ref[...] = logs_ref[...]
    zeros = jnp.zeros((48, 128), F32)
    for y in range(8):
        block = scr_ref[pl.ds(y, 64, stride=8), :]
        logs = log_ref[pl.ds(y, 8, stride=8), :]
        high = logs.astype(BF).astype(F32)
        chan_ref[y] = jnp.concatenate([block, high, logs - high, zeros], axis=0).T


def edges_kernel(chan_ref, above_ref, below_ref, full_ref, last_ref, lead_ref):
    zeros = jnp.zeros((48, 128), F32)
    for got_ref, first in ((above_ref, 0), (below_ref, 10)):
        got = got_ref[...].astype(F32)
        for k in range(2):
            full_ref[first + k, 8:136, :] = jnp.concatenate([got[k * 80 : k * 80 + 80], zeros], axis=0).T
    full_ref[2:10, 8:136, :] = chan_ref[...]
    for r in range(12):
        last_ref[r * 8 : r * 8 + 8] = full_ref[r, 128:136, :].astype(BF)
        lead_ref[r * 8 : r * 8 + 8] = full_ref[r, 8:16, :].astype(BF)


def patches_kernel(at_ref, full_ref, left_ref, right_ref, pars_ref, send_ref, logp_ref, wide_ref, joint_ref, scr_ref):
    left, right = left_ref[...].astype(F32), right_ref[...].astype(F32)
    for r in range(12):
        wide_ref[r, 0:8, :] = left[r * 8 : r * 8 + 8]
        wide_ref[r, 8:136, :] = full_ref[r, 8:136, :]
        wide_ref[r, 136:144, :] = right[r * 8 : r * 8 + 8]
    for r in range(6):
        joint_ref[r] = halves(wide_ref[r, 6:138, :], swapped(wide_ref[r + 6, 6:138, :]))
    pars = pars_ref[...]
    high = pars.astype(BF).astype(F32)
    for d in range(8):
        for r in range(6):
            scr_ref[r * 20 : r * 20 + 20, :] = joint_ref[r, 16 * d : 16 * d + 20, :]
        scr_ref[120:140, :] = high
        scr_ref[140:160, :] = pars - high
        send_ref[d] = scr_ref[...].astype(BF)
    start = pl.multiple_of(at_ref[0] * 16, 16)
    for r in range(12):
        got = wide_ref[r, pl.ds(start, 32), :]
        logp_ref[r * 20 : r * 20 + 20, :] = (got + pltpu.roll(got, 120, 1))[6:26]


def coef_kernel(at_ref, mine_ref, logp_ref, coef_ref, wr_ref, scr_ref, par_ref):
    for z in range(8):
        scr_ref[z * 40 : (z + 1) * 40, :] = mine_ref[z].astype(F32)[120:160]
    sub = lax.broadcasted_iota(jnp.int32, (8, 128), 0)
    grp = lax.broadcasted_iota(jnp.int32, (8, 128), 1) // 16
    for v in range(10):
        for h in range(2):
            at = v * 2 + h
            got = scr_ref[pl.ds(at, 8, stride=40), :] + scr_ref[pl.ds(at + 20, 8, stride=40), :]
            for s in (1, 2, 4):
                up = pltpu.roll(pltpu.roll(got, 8 - s, 0), 16 * s, 1)
                down = pltpu.roll(pltpu.roll(got, s, 0), 128 - 16 * s, 1)
                mine, bit = (sub & s) > 0, (grp & s) > 0
                got = jnp.where(mine == bit, got, jnp.where(mine, down, up))
            par_ref[v, h * 8 : h * 8 + 8, :] = got
    cols = [logp_ref[:, 64 + j : 65 + j] for j in range(8)]
    for n in range(16):
        p = at_ref[2 + n]
        for v in range(2):
            wr_ref[v, n : n + 1, :] = par_ref[v, pl.ds(p, 1), :]
        acc = cols[0] * par_ref[2, pl.ds(p, 1), :]
        for j in range(1, 8):
            acc = acc + cols[j] * par_ref[2 + j, pl.ds(p, 1), :]
        coef_ref[n] = jnp.exp(acc)


def state_kernel(at_ref, mine_ref, theirs_ref, state_ref):
    first = jnp.zeros((1, 128), jnp.int32) + at_ref[1] == 0
    for z in range(8):
        mine, theirs = mine_ref[z].astype(F32)[0:120], theirs_ref[z].astype(F32)[0:120]
        zero, one = jnp.where(first, mine, theirs), jnp.where(first, theirs, mine)
        both = jnp.concatenate([halves(zero, swapped(one)), halves(swapped(zero), one)], axis=0)
        state_ref[:, z * 128 : (z + 1) * 128] = both.astype(BF)


def drive(f_ref, h, coef_ref, c, rows, skip, rate, weight):
    def f(d):
        return f_ref[h, 20 + d : 20 + d + rows, :]

    def k(d):
        return coef_ref[c, skip + 20 + d : skip + 20 + d + rows, :]

    mid, kmid = f(0), k(0)
    total = (kmid + k(-20)) * (f(-20) - mid)
    for d in (20, -1, 1):
        total = total + (kmid + k(d)) * (f(d) - mid)
    total = total + rate * (mid - mid * mid * mid)
    return (weight * total).astype(BF)


def sweep(state, basis_refs, coef_ref, wr_ref, f_ref, acc_ref, rows, skip, c=0):
    for ref in basis_refs:
        block = ref[...]
        field = lax.dot_general(state, block, (((1,), (1,)), ((), ())), preferred_element_type=F32)
        parts = []
        for h in range(2):
            f_ref[h, : field.shape[0], :] = field[:, h * 128 : (h + 1) * 128]
            weight, rate = wr_ref[0, c : c + 1, :], wr_ref[1, c : c + 1, :]
            parts.append(drive(f_ref, h, coef_ref, c, rows, skip, rate, weight))
            c += 1
        acc_ref[...] += jnp.dot(jnp.concatenate(parts, axis=1), block, preferred_element_type=F32)


def early_kernel(b0, b1, b2, b3, state_ref, coef_ref, wr_ref, acc_ref, f_ref):
    acc_ref[...] = jnp.zeros_like(acc_ref)
    sweep(state_ref[...], (b0, b1, b2, b3), coef_ref, wr_ref, f_ref, acc_ref, 200, 0)


def late_kernel(b4, b5, b6, b7, state_ref, coef_ref, wr_ref, sum_ref, out_ref, f_ref, acc_ref):
    acc_ref[...] = sum_ref[...]
    sweep(state_ref[...], (b4, b5, b6, b7), coef_ref, wr_ref, f_ref, acc_ref, 200, 0, 8)
    out_ref[...] = acc_ref[...].astype(BF)


def second_kernel(
    edge_ref, b0, b1, b2, b3, b4, b5, b6, b7, state_ref, coef_ref, wr_ref, own_ref, other_ref, out_ref, f_ref, acc_ref
):
    total = own_ref[...].astype(F32) + other_ref[...].astype(F32)
    now = state_ref[...].astype(F32)[20:220]
    cell = lax.broadcasted_iota(jnp.int32, (200, 128), 0).astype(F32)
    row = jnp.floor((cell + 0.5) * 0.05)
    col = cell - 20.0 * row
    low = jnp.where(edge_ref[0] == 1, 1.0, 0.0)
    high = jnp.where(edge_ref[1] == 1, 8.0, 9.0)
    left = jnp.where(edge_ref[2] == 1, 2.0, 0.0)
    right = jnp.where(edge_ref[3] == 1, 17.0, 19.0)
    inside = (row >= low) & (row <= high) & (col >= left) & (col <= right)
    keep = jnp.where(inside, 1.0, 0.0)[:, 0:1]
    state = ((now + STEP * total) * keep).astype(BF)
    acc_ref[...] = jnp.zeros_like(acc_ref)
    sweep(state, (b0, b1, b2, b3, b4, b5, b6, b7), coef_ref, wr_ref, f_ref, acc_ref, 160, 20)
    for z in range(8):
        for y in range(4):
            low = acc_ref[y * 20 + 2 : y * 20 + 18, z * 128 : (z + 1) * 128]
            high = acc_ref[y * 20 + 82 : y * 20 + 98, z * 128 : (z + 1) * 128]
            out_ref[2 * z, y * 16 : y * 16 + 16, :] = halves(low, swapped(high)).astype(BF)
            out_ref[2 * z + 1, y * 16 : y * 16 + 16, :] = halves(swapped(low), high).astype(BF)


def finish_kernel(back_ref, modes_ref, out_ref, scr_ref):
    for y in range(4):
        parts = [
            back_ref[2 * z, y * 16 : y * 16 + 16, :].astype(F32) + back_ref[2 * z + 1, y * 16 : y * 16 + 16, :].astype(F32)
            for z in range(8)
        ]
        turned = jnp.concatenate(parts, axis=0).T
        scr_ref[pl.ds(y, 64, stride=8), :] = turned[0:64]
        scr_ref[pl.ds(y + 4, 64, stride=8), :] = turned[64:128]
    out_ref[...] = modes_ref[...].astype(F32) + STEP * scr_ref[...]


SMEM = pl.BlockSpec(memory_space=pltpu.SMEM)
WHOLE = pl.BlockSpec(memory_space=pltpu.VMEM)


def call(kernel, outs, scratch, scalars, *args):
    specs = [SMEM] * scalars + [WHOLE] * (len(args) - scalars)
    single = not isinstance(outs, (list, tuple))
    return pl.pallas_call(
        kernel,
        out_shape=outs,
        in_specs=specs,
        out_specs=WHOLE if single else [WHOLE] * len(outs),
        scratch_shapes=scratch,
    )(*args)


def update(modes_now, basis_rows, quad_weights, germ_nodes, log_fields, reaction_rates):
    quad, gy, gx = lax.axis_index("quad"), lax.axis_index("gy"), lax.axis_index("gx")
    zl, core, y, x = quad // 2, quad % 2, gy // 2, gx
    columns = [list(range(0, 16, 2)), list(range(1, 16, 2))]
    swap = [(i, i ^ 1) for i in range(16)]

    part = lax.dynamic_slice_in_dim(basis_rows, (y * 4 + x) * 16, 16, axis=0)
    send = jnp.broadcast_to(part[None], (8, 16, 1024))
    shard = lax.all_to_all(send, "quad", 0, 0, axis_index_groups=columns, tiled=True).reshape(128, 1024)

    modes, logs = modes_now.reshape(512, 128), log_fields.reshape(64, 128)
    scratch = [VM((512, 128), F32), VM((64, 128), F32)]
    low, top = call(rows_kernel, [shape((160, 128), BF)] * 2, scratch, 0, modes, logs)
    down, right = [(i, i + 1) for i in range(7)], [(i, i + 1) for i in range(3)]
    above = lax.ppermute(low, "gy", down)
    below = lax.ppermute(top, "gy", [(j, i) for i, j in down])
    chan = call(channels_kernel, shape((8, 128, 128), F32), scratch, 0, modes, logs)
    full, last, lead = call(
        edges_kernel,
        [shape((12, 144, 128), F32), shape((96, 128), BF), shape((96, 128), BF)],
        [],
        0,
        chan,
        above,
        below,
    )
    from_left = lax.ppermute(last, "gx", right)
    from_right = lax.ppermute(lead, "gx", [(j, i) for i, j in right])
    pars = jnp.concatenate([quad_weights[None], reaction_rates[None], germ_nodes.T], axis=0).reshape(20, 128)
    outer = jnp.asarray([OFFS[o] for o, _ in ARRIVAL], jnp.int32)
    inner = jnp.asarray([OFFS[i] for _, i in ARRIVAL], jnp.int32)
    dy, dx = jnp.where(core == 0, outer, inner), jnp.where(core == 0, inner, outer)
    order = ((y + dy) % 4) * 4 + (x + dx) % 4
    at = jnp.concatenate([jnp.stack([zl, core]), order]).astype(jnp.int32)
    patch, logp = call(
        patches_kernel,
        [shape((8, 160, 128), BF), shape((240, 128), F32)],
        [VM((12, 176, 128), F32), VM((6, 132, 128), F32), VM((160, 128), F32)],
        1,
        at,
        full,
        from_left,
        from_right,
        pars,
    )
    mine = lax.all_to_all(patch, "quad", 0, 0, axis_index_groups=columns, tiled=True)
    theirs = lax.ppermute(mine, "quad", swap)

    fwd, bwd = plane_shift(0, 1), plane_shift(0, -1)
    less = lax.ppermute(shard, ALL, fwd)
    more = lax.ppermute(shard, ALL, bwd)
    near = jnp.concatenate([shard, less], axis=0)
    far = lax.ppermute(less, ALL, fwd)
    fwd, bwd = plane_shift(1, 1), plane_shift(1, -1)
    near_less = lax.ppermute(near, ALL, fwd)
    near_more = lax.ppermute(near, ALL, bwd)
    away = jnp.concatenate([more, far], axis=0)
    away_less = lax.ppermute(away, ALL, fwd)
    away_more = lax.ppermute(away, ALL, bwd)
    near_far = lax.ppermute(near_less, ALL, fwd)
    away_far = lax.ppermute(away_more, ALL, bwd)
    blocks = (near, away, near_less, near_more, away_less, away_more, near_far, away_far)

    coef, wr = call(
        coef_kernel,
        [shape((16, 240, 128), F32), shape((2, 16, 128), F32)],
        [VM((320, 128), F32), VM((10, 16, 128), F32)],
        1,
        at,
        mine,
        logp,
    )
    state = call(state_kernel, shape((240, 1024), BF), [], 1, at, mine, theirs)
    part = call(
        early_kernel, shape((200, 1024), F32), [VM((2, 240, 128), F32)], 0, *blocks[:4], state, coef, wr
    )
    own = call(
        late_kernel,
        shape((200, 1024), BF),
        [VM((2, 240, 128), F32), VM((200, 1024), F32)],
        0,
        *blocks[4:],
        state,
        coef,
        wr,
        part,
    )
    other = lax.ppermute(own, "quad", swap)
    edge = jnp.stack([gy == 0, gy == 7, (gx == 0) & (zl == 0), (gx == 3) & (zl == 7)]).astype(jnp.int32)
    out = call(
        second_kernel,
        shape((16, 64, 128), BF),
        [VM((2, 200, 128), F32), VM((160, 1024), F32)],
        1,
        edge,
        *blocks,
        state,
        coef,
        wr,
        own,
        other,
    )
    back = lax.all_to_all(out, "quad", 0, 0, tiled=True)
    result = call(finish_kernel, shape((512, 128), F32), [VM((512, 128), F32)], 0, back, modes)
    return result.reshape(64, 8, 128)


def solution(mesh):
    in_specs = (
        P("quad", "gy", "gx"),
        P("quad", None),
        P("quad"),
        P("quad", None),
        P(None, "gy", "gx"),
        P("quad"),
    )
    out_specs = P("quad", "gy", "gx")
    return jax.shard_map(update, mesh=mesh, in_specs=in_specs, out_specs=out_specs, check_vma=False)
```

time: 156 us -> 159 us (1.019)
  starting transfers between devices: 58.5 us -> 84.1 us
  blocking collectives: 46.6 us -> 27.1 us
  Pallas kernels: 28.6 us -> 33.2 us
  waiting for transfers between devices: 9.12 us -> 5.5 us
  local copies, waits for them, and re-layouts: 8.11 us -> 5.17 us
    all_to_all x2 -> x1, blocking collectives: 46.6 us -> 27.1 us  [update(): back = lax.all_to_all(out, 'quad', 0, 0, tiled=True)]
    all_to_all x1 -> x2, starting transfers between devices: 9.02 us -> 22.4 us  [the longest x1 13.1 us: update(): lax.all_to_all(send, 'quad', 0, 0, axis_index_groups=columns, tiled=True)]
    ppermute x13 -> x15, starting transfers between devices: 49.5 us -> 61.8 us  [the longest x1 10.2 us: update(): theirs = lax.ppermute(mine, 'quad', swap)]
    pallas_call x7 -> x10, Pallas kernels: 28.6 us -> 33.2 us  [call(): pl.pallas_call(kernel, out_shape=outs, in_specs=specs, out_specs=WHOLE if...]
    slice x2 -> x0, local copies, waits for them, and re-layouts: 2.78 us -> none  [the longest x1 1.87 us: body(): far0 = lax.ppermute(less[:256], ALL, fwd)]
    all_to_all x1 -> x2, waiting for transfers between devices: 2.87 us -> 0.75 us  [the longest x1 0.75 us: update(): lax.all_to_all(send, 'quad', 0, 0, axis_index_groups=columns, tiled=True)]
    ppermute x13 -> x15, waiting for transfers between devices: 6.25 us -> 4.75 us  [the longest x1 2.31 us: update(): far = lax.ppermute(less, ALL, fwd)]
    unnamed x22 -> x25, local copies, waits for them, and re-layouts: 4.54 us -> 3.82 us
  transfers between devices with their start and end apart: 14 -> 17, of which waited for: 4 -> 4; matrix products, arithmetic and copies ran while one was open for 4% -> 2% of each run, Pallas kernels for 8% -> 12%
where the time goes in v3:
time: 159 us; the launch traced here: 158 us
  starting transfers between devices  84.1 us (53%)
  Pallas kernels  33.2 us (21%)
  blocking collectives  27.1 us (17%)
  waiting for transfers between devices  5.5 us (3%)
  local copies, waits for them, and re-layouts  5.17 us (3%)
  other arithmetic  2.63 us (2%)
    pallas_call x10, Pallas kernels, call(): pl.pallas_call(kernel, out_shape=outs, in_specs=specs, out_specs=WHOLE if...  33.2 us
    all_to_all x1, blocking collectives, update(): back = lax.all_to_all(out, 'quad', 0, 0, tiled=True)  27.1 us
    all_to_all x1, starting transfers between devices, update(): lax.all_to_all(send, 'quad', 0, 0, axis_index_groups=columns, tiled=True)  13.1 us
    ppermute x1, starting transfers between devices, update(): theirs = lax.ppermute(mine, 'quad', swap)  10.2 us
    all_to_all x1, starting transfers between devices, update(): lax.all_to_all(patch, 'quad', 0, 0, axis_index_groups=columns, tiled=True)  9.31 us
    ppermute x1, starting transfers between devices, update(): less = lax.ppermute(shard, ALL, fwd)  8.13 us
    ppermute x1, starting transfers between devices, update(): above = lax.ppermute(low, 'gy', down)  7.92 us
    ppermute x1, starting transfers between devices, update(): away_more = lax.ppermute(away, ALL, bwd)  5.55 us
  transfers between devices with their start and end apart: 17, of which 4 were waited for; matrix products, arithmetic and copies ran while one was open for 2% of the time, Pallas kernels for 12%

profile of v3, /device:TPU:1, one launch (start us, length us, event | category | flops | bytes accessed | tf_op | source)
XLA Modules:
  0.0 158.1 jit_solution(15313535411198252934)
XLA Ops:
  0.0 1.0 copy-done
  1.8 13.1 %all-to-all-start = ((bf16[8,16,1024]{2,1,0:T(8,128)(2,1)}), bf16[8,16,1024]{2,1,0:T(8,128)(2,1)S(1)}, u32[]{:S(2)}, u32[]{:S(2)}) async-start(bf16[8,16,1024]{2,1,0:T(8,128)(2,1)} %broadcast_in_dim.12), calls=%async_computation | async-start | bytes 524288 | tf_op jit(solution)/shard_map/all_to_all | solution.py:239
  14.8 1.6 shard_map.83
  16.4 7.9 %collective-permute-start.9 = (bf16[160,128]{1,0:T(8,128)(2,1)}, bf16[160,128]{1,0:T(8,128)(2,1)S(1)}, u32[]{:S(2)}, u32[]{:S(2)}) collective-permute-start(bf16[160,128]{1,0:T(8,128)(2,1)} %get-tuple-element.14), channel_id=1, source_target_pairs={{0,4},{4,8},{8,12},{12,16},{16,20},{20,24},{24,28},{1,5},{5,9},{9,... | collective-permute-start | bytes 122888 | tf_op jit(solution)/shard_map/ppermute | solution.py:245
  24.3 1.3 collective-permute-start.10
  27.1 8.1 %collective-permute-start = (bf16[128,1024]{1,0:T(8,128)(2,1)S(1)}, bf16[128,1024]{1,0:T(8,128)(2,1)S(1)}, u32[]{:S(2)}, u32[]{:S(2)}) collective-permute-start(bf16[128,1024]{1,0:T(8,128)(2,1)S(1)} %bitcast.16), channel_id=1, source_target_pairs={{0,1},{1,2},{2,3},{3,0},{4,5},{5,6},{6,7},{7,4},{8,9},{9,10},{10,1... | collective-permute-start | bytes 786440 | tf_op jit(solution)/shard_map/ppermute | solution.py:280
  36.0 1.9 %shard_map.82.chan_ref = f32[8,128,128]{2,1,0:T(8,128)} custom-call(bf16[512,128]{1,0:T(8,128)(2,1)} %bitcast.14, f32[64,128]{1,0:T(8,128)} %bitcast.20), custom_call_target="tpu_custom_call" | custom-call | tf_op jit(solution)/shard_map/pallas_call | solution.py:222
  37.9 1.1 collective-permute-done.10.below_ref
  39.6 2.1 %shard_map.84 = (f32[12,144,128]{2,1,0:T(8,128)}, bf16[96,128]{1,0:T(8,128)(2,1)}, bf16[96,128]{1,0:T(8,128)(2,1)}) custom-call(f32[8,128,128]{2,1,0:T(8,128)} %shard_map.82.chan_ref, bf16[160,128]{1,0:T(8,128)(2,1)} %copy-done.8, bf16[160,128]{1,0:T(8,128)(2,1)} %copy-done.9), custom_call_target="tpu_custom_call" | custom-call | tf_op jit(solution)/shard_map/pallas_call | solution.py:222
  41.7 3.1 %collective-permute-start.11 = (bf16[96,128]{1,0:T(8,128)(2,1)}, bf16[96,128]{1,0:T(8,128)(2,1)S(1)}, u32[]{:S(2)}, u32[]{:S(2)}) collective-permute-start(bf16[96,128]{1,0:T(8,128)(2,1)} %get-tuple-element.17), channel_id=1, source_target_pairs={{0,1},{1,2},{2,3},{4,5},{5,6},{6,7},{8,9},{9,10},{10,11},{12,13},{... | collective-permute-start | bytes 73736 | tf_op jit(solution)/shard_map/ppermute | solution.py:257
  44.8 1.3 collective-permute-start.12
  46.1 4.6 %collective-permute-start.1 = (bf16[128,1024]{1,0:T(8,128)(2,1)S(1)}, bf16[128,1024]{1,0:T(8,128)(2,1)S(1)}, u32[]{:S(2)}, u32[]{:S(2)}) collective-permute-start(bf16[128,1024]{1,0:T(8,128)(2,1)S(1)} %bitcast.17), channel_id=1, source_target_pairs={{0,3},{1,0},{2,1},{3,2},{4,7},{5,4},{6,5},{7,6},{8,11},{9,8},{10,9... | collective-permute-start | bytes 786440 | tf_op jit(solution)/shard_map/ppermute | solution.py:281
  52.6 2.2 %shard_map.85 = (bf16[8,160,128]{2,1,0:T(8,128)(2,1)}, f32[240,128]{1,0:T(8,128)}) custom-call(s32[18]{0:T(128)} %pad_add_fusion.at_ref, f32[12,144,128]{2,1,0:T(8,128)} %get-tuple-element.16.full_ref, bf16[96,128]{1,0:T(8,128)(2,1)} %copy-done.10, bf16[96,128]{1,0:T(8,128)(2,1)} %copy-done.11, f32[20,128]{1,0:T(8,128)} %reshape.19.pars_ref), custom_call_target="tpu_custom_call" | custom-call | tf_op jit(solution)/shard_map/pallas_call | solution.py:222
  54.8 9.3 %all-to-all-start.1 = ((bf16[8,160,128]{2,1,0:T(8,128)(2,1)}), bf16[8,160,128]{2,1,0:T(8,128)(2,1)S(1)}, u32[]{:S(2)}, u32[]{:S(2)}) async-start(bf16[8,160,128]{2,1,0:T(8,128)(2,1)} %get-tuple-element.19), calls=%async_computation.1 | async-start | bytes 655360 | tf_op jit(solution)/shard_map/all_to_all | solution.py:276
  64.1 1.9 %collective-permute-start.2 = (bf16[128,1024]{1,0:T(8,128)(2,1)S(1)}, bf16[128,1024]{1,0:T(8,128)(2,1)S(1)}, u32[]{:S(2)}, u32[]{:S(2)}) collective-permute-start(bf16[128,1024]{1,0:T(8,128)(2,1)S(1)} %collective-permute-done), channel_id=1, source_target_pairs={{0,1},{1,2},{2,3},{3,0},{4,5},{5,6},{6,7},{7,4},{8,9},{9,10},{10,1... | collective-permute-start | bytes 786440 | tf_op jit(solution)/shard_map/ppermute | solution.py:283
  66.1 4.0 %collective-permute-start.3 = (bf16[256,1024]{1,0:T(8,128)(2,1)S(1)}, bf16[256,1024]{1,0:T(8,128)(2,1)S(1)}, u32[]{:S(2)}, u32[]{:S(2)}) collective-permute-start(bf16[256,1024]{1,0:T(8,128)(2,1)S(1)} %pad_maximum_fusion.b0), channel_id=1, source_target_pairs={{0,8},{1,9},{2,10},{3,11},{4,12},{5,13},{6,14},{7,15},{8,16},{9,17... | collective-permute-start | bytes 1572872 | tf_op jit(solution)/shard_map/ppermute | solution.py:285
  70.1 2.3 %collective-permute-done.2 = bf16[128,1024]{1,0:T(8,128)(2,1)S(1)} collective-permute-done((bf16[128,1024]{1,0:T(8,128)(2,1)S(1)}, bf16[128,1024]{1,0:T(8,128)(2,1)S(1)}, u32[]{:S(2)}, u32[]{:S(2)}) %collective-permute-start.2) | collective-permute-done | bytes 262176 | tf_op jit(solution)/shard_map/ppermute | solution.py:283
  72.5 5.6 %collective-permute-start.6 = (bf16[256,1024]{1,0:T(8,128)(2,1)S(1)}, bf16[256,1024]{1,0:T(8,128)(2,1)S(1)}, u32[]{:S(2)}, u32[]{:S(2)}) collective-permute-start(bf16[256,1024]{1,0:T(8,128)(2,1)S(1)} %constant_dynamic-update-slice_fusion.b1), channel_id=1, source_target_pairs={{0,24},{1,25},{2,26},{3,27},{4,28},{5,29},{6,30},{7,31},{8,0},{9,1... | collective-permute-start | bytes 1572872 | tf_op jit(solution)/shard_map/ppermute | solution.py:289
  78.0 2.2 %collective-permute-start.4 = (bf16[256,1024]{1,0:T(8,128)(2,1)S(1)}, bf16[256,1024]{1,0:T(8,128)(2,1)S(1)}, u32[]{:S(2)}, u32[]{:S(2)}) collective-permute-start(bf16[256,1024]{1,0:T(8,128)(2,1)S(1)} %pad_maximum_fusion.b0), channel_id=1, source_target_pairs={{0,24},{1,25},{2,26},{3,27},{4,28},{5,29},{6,30},{7,31},{8,0},{9,1... | collective-permute-start | bytes 1572872 | tf_op jit(solution)/shard_map/ppermute | solution.py:286
  80.2 3.1 %collective-permute-start.5 = (bf16[256,1024]{1,0:T(8,128)(2,1)S(1)}, bf16[256,1024]{1,0:T(8,128)(2,1)}, u32[]{:S(2)}, u32[]{:S(2)}) collective-permute-start(bf16[256,1024]{1,0:T(8,128)(2,1)S(1)} %constant_dynamic-update-slice_fusion.b1), channel_id=1, source_target_pairs={{0,8},{1,9},{2,10},{3,11},{4,12},{5,13},{6,14},{7,15},{8,16},{9,17... | collective-permute-start | bytes 1572872 | tf_op jit(solution)/shard_map/ppermute | solution.py:288
  83.4 1.9 %collective-permute-start.7 = (bf16[256,1024]{1,0:T(8,128)(2,1)S(1)}, bf16[256,1024]{1,0:T(8,128)(2,1)}, u32[]{:S(2)}, u32[]{:S(2)}) collective-permute-start(bf16[256,1024]{1,0:T(8,128)(2,1)S(1)} %collective-permute-done.3.b2), channel_id=1, source_target_pairs={{0,8},{1,9},{2,10},{3,11},{4,12},{5,13},{6,14},{7,15},{8,16},{9,17... | collective-permute-start | bytes 1572872 | tf_op jit(solution)/shard_map/ppermute | solution.py:290
  85.3 4.6 %collective-permute-start.8 = (bf16[256,1024]{1,0:T(8,128)(2,1)S(1)}, bf16[256,1024]{1,0:T(8,128)(2,1)}, u32[]{:S(2)}, u32[]{:S(2)}) collective-permute-start(bf16[256,1024]{1,0:T(8,128)(2,1)S(1)} %collective-permute-done.6.b5), channel_id=1, source_target_pairs={{0,24},{1,25},{2,26},{3,27},{4,28},{5,29},{6,30},{7,31},{8,0},{9,1... | collective-permute-start | bytes 1572872 | tf_op jit(solution)/shard_map/ppermute | solution.py:291
  89.9 10.2 %collective-permute-start.13 = (bf16[8,160,128]{2,1,0:T(8,128)(2,1)S(1)}, bf16[8,160,128]{2,1,0:T(8,128)(2,1)}, u32[]{:S(2)}, u32[]{:S(2)}) collective-permute-start(bf16[8,160,128]{2,1,0:T(8,128)(2,1)S(1)} %all-to-all-done.1.mine_ref), channel_id=1, source_target_pairs={{0,32},{32,0},{64,96},{96,64},{128,160},{160,128},{192,224},{224,1... | collective-permute-start | bytes 983048 | tf_op jit(solution)/shard_map/ppermute | solution.py:277
  100.2 4.0 %shard_map.87 = (f32[16,240,128]{2,1,0:T(8,128)}, f32[2,16,128]{2,1,0:T(8,128)}) custom-call(s32[18]{0:T(128)} %pad_add_fusion.at_ref, bf16[8,160,128]{2,1,0:T(8,128)(2,1)} %copy-done.3, f32[240,128]{1,0:T(8,128)} %get-tuple-element.20.logp_ref), custom_call_target="tpu_custom_call" | custom-call | tf_op jit(solution)/shard_map/pallas_call | solution.py:222
  104.2 2.1 %shard_map.86.state_ref = bf16[240,1024]{1,0:T(8,128)(2,1)} custom-call(s32[18]{0:T(128)} %pad_add_fusion.at_ref, bf16[8,160,128]{2,1,0:T(8,128)(2,1)} %copy-done.3, bf16[8,160,128]{2,1,0:T(8,128)(2,1)} %collective-permute-done.13.theirs_ref), custom_call_target="tpu_custom_call" | custom-call | tf_op jit(solution)/shard_map/pallas_call | solution.py:222
  107.1 5.1 %shard_map.88.sum_ref = f32[200,1024]{1,0:T(8,128)} custom-call(bf16[256,1024]{1,0:T(8,128)(2,1)} %copy-done.1, bf16[256,1024]{1,0:T(8,128)(2,1)} %copy-done.2, bf16[256,1024]{1,0:T(8,128)(2,1)} %copy-done.4, bf16[256,1024]{1,0:T(8,128)(2,1)} %copy-done.6, bf16[240,1024]{1,0:T(8,128)(2,1)} %shard_map.86.state_ref, ...), custom_call_target="tpu_custom_call" | custom-call | tf_op jit(solution)/shard_map/pallas_call | solution.py:222
  112.2 5.2 %shard_map.89.own_ref = bf16[200,1024]{1,0:T(8,128)(2,1)} custom-call(bf16[256,1024]{1,0:T(8,128)(2,1)} %collective-permute-done.5.b4, bf16[256,1024]{1,0:T(8,128)(2,1)} %copy-done.5, bf16[256,1024]{1,0:T(8,128)(2,1)} %collective-permute-done.7.b6, bf16[256,1024]{1,0:T(8,128)(2,1)} %collective-permute-done.8.b7, bf16[240,1024]{1,0:T(8,128)(2,1)} %shard_map.86.state_ref, ...), custom_call_target="tpu_custom_call" | custom-call | tf_op jit(solution)/shard_map/pallas_call | solution.py:222
  117.4 1.9 %collective-permute-start.14 = (bf16[200,1024]{1,0:T(8,128)(2,1)}, bf16[200,1024]{1,0:T(8,128)(2,1)S(1)}, u32[]{:S(2)}, u32[]{:S(2)}) collective-permute-start(bf16[200,1024]{1,0:T(8,128)(2,1)} %shard_map.89.own_ref), channel_id=1, source_target_pairs={{0,32},{32,0},{64,96},{96,64},{128,160},{160,128},{192,224},{224,1... | collective-permute-start | bytes 1228808 | tf_op jit(solution)/shard_map/ppermute | solution.py:318
  119.9 1.3 collective-permute-done.14.other_ref
  122.0 7.1 %shard_map.90 = bf16[16,64,128]{2,1,0:T(8,128)(2,1)} custom-call(s32[4]{0:T(128)} %add_convert_fusion.edge_ref, bf16[256,1024]{1,0:T(8,128)(2,1)} %copy-done.1, bf16[256,1024]{1,0:T(8,128)(2,1)} %copy-done.2, bf16[256,1024]{1,0:T(8,128)(2,1)} %copy-done.4, bf16[256,1024]{1,0:T(8,128)(2,1)} %copy-done.6, bf16[256,1024]{1,0:T(8,128)(2,1)} %collective-permute-done.5.b4, ...), custom_call_target="tpu_custom_call" | custom-call | tf_op jit(solution)/shard_map/pallas_call | solution.py:222
  129.1 27.1 %all_to_all.15.back_ref = bf16[16,64,128]{2,1,0:T(8,128)(2,1)} all-to-all(bf16[16,64,128]{2,1,0:T(8,128)(2,1)} %shard_map.90), channel_id=1, replica_groups=mesh['quad'=16,'gy'=8,'gx'=4] {'quad'}, dimensions={0} | all-to-all | bytes 524288 | tf_op jit(solution)/shard_map/all_to_all | solution.py:333
  156.3 1.8 %shard_map.91 = f32[512,128]{1,0:T(8,128)} custom-call(bf16[16,64,128]{2,1,0:T(8,128)(2,1)} %all_to_all.15.back_ref, bf16[512,128]{1,0:T(8,128)(2,1)} %bitcast.15), custom_call_target="tpu_custom_call" | custom-call | tf_op jit(solution)/shard_map/pallas_call | solution.py:222
  (47 shorter events, 7.5 us)
Async XLA Ops:
  0.0 1.0 copy-start
  1.8 25.3 %all-to-all-start = ((bf16[8,16,1024]{2,1,0:T(8,128)(2,1)}), bf16[8,16,1024]{2,1,0:T(8,128)(2,1)S(1)}, u32[]{:S(2)}, u32[]{:S(2)}) async-start(bf16[8,16,1024]{2,1,0:T(8,128)(2,1)} %broadcast_in_dim.12), calls=%async_computation | async-start | bytes 524288 | tf_op jit(solution)/shard_map/all_to_all | solution.py:239
  16.4 21.5 %collective-permute-start.9 = (bf16[160,128]{1,0:T(8,128)(2,1)}, bf16[160,128]{1,0:T(8,128)(2,1)S(1)}, u32[]{:S(2)}, u32[]{:S(2)}) collective-permute-start(bf16[160,128]{1,0:T(8,128)(2,1)} %get-tuple-element.14), channel_id=1, source_target_pairs={{0,4},{4,8},{8,12},{12,16},{16,20},{20,24},{24,28},{1,5},{5,9},{9,... | collective-permute-start | bytes 122888 | tf_op jit(solution)/shard_map/ppermute | solution.py:245
  24.3 14.6 %collective-permute-start.10 = (bf16[160,128]{1,0:T(8,128)(2,1)}, bf16[160,128]{1,0:T(8,128)(2,1)S(1)}, u32[]{:S(2)}, u32[]{:S(2)}) collective-permute-start(bf16[160,128]{1,0:T(8,128)(2,1)} %get-tuple-element.15), channel_id=1, source_target_pairs={{4,0},{8,4},{12,8},{16,12},{20,16},{24,20},{28,24},{5,1},{9,5},{13... | collective-permute-start | bytes 122888 | tf_op jit(solution)/shard_map/ppermute | solution.py:246
  27.1 37.0 %collective-permute-start = (bf16[128,1024]{1,0:T(8,128)(2,1)S(1)}, bf16[128,1024]{1,0:T(8,128)(2,1)S(1)}, u32[]{:S(2)}, u32[]{:S(2)}) collective-permute-start(bf16[128,1024]{1,0:T(8,128)(2,1)S(1)} %bitcast.16), channel_id=1, source_target_pairs={{0,1},{1,2},{2,3},{3,0},{4,5},{5,6},{6,7},{7,4},{8,9},{9,10},{10,1... | collective-permute-start | bytes 786440 | tf_op jit(solution)/shard_map/ppermute | solution.py:280
  37.9 1.1 copy-start.8
  39.0 0.6 copy-start.9
  41.7 10.3 %collective-permute-start.11 = (bf16[96,128]{1,0:T(8,128)(2,1)}, bf16[96,128]{1,0:T(8,128)(2,1)S(1)}, u32[]{:S(2)}, u32[]{:S(2)}) collective-permute-start(bf16[96,128]{1,0:T(8,128)(2,1)} %get-tuple-element.17), channel_id=1, source_target_pairs={{0,1},{1,2},{2,3},{4,5},{5,6},{6,7},{8,9},{9,10},{10,11},{12,13},{... | collective-permute-start | bytes 73736 | tf_op jit(solution)/shard_map/ppermute | solution.py:257
  44.8 7.2 %collective-permute-start.12 = (bf16[96,128]{1,0:T(8,128)(2,1)}, bf16[96,128]{1,0:T(8,128)(2,1)S(1)}, u32[]{:S(2)}, u32[]{:S(2)}) collective-permute-start(bf16[96,128]{1,0:T(8,128)(2,1)} %get-tuple-element.18), channel_id=1, source_target_pairs={{1,0},{2,1},{3,2},{5,4},{6,5},{7,6},{9,8},{10,9},{11,10},{13,12},{... | collective-permute-start | bytes 73736 | tf_op jit(solution)/shard_map/ppermute | solution.py:258
  46.1 24.0 %collective-permute-start.1 = (bf16[128,1024]{1,0:T(8,128)(2,1)S(1)}, bf16[128,1024]{1,0:T(8,128)(2,1)S(1)}, u32[]{:S(2)}, u32[]{:S(2)}) collective-permute-start(bf16[128,1024]{1,0:T(8,128)(2,1)S(1)} %bitcast.17), channel_id=1, source_target_pairs={{0,3},{1,0},{2,1},{3,2},{4,7},{5,4},{6,5},{7,6},{8,11},{9,8},{10,9... | collective-permute-start | bytes 786440 | tf_op jit(solution)/shard_map/ppermute | solution.py:281
  52.0 0.6 copy-start.10
  52.0 0.6 copy-start.11
  54.8 35.1 %all-to-all-start.1 = ((bf16[8,160,128]{2,1,0:T(8,128)(2,1)}), bf16[8,160,128]{2,1,0:T(8,128)(2,1)S(1)}, u32[]{:S(2)}, u32[]{:S(2)}) async-start(bf16[8,160,128]{2,1,0:T(8,128)(2,1)} %get-tuple-element.19), calls=%async_computation.1 | async-start | bytes 655360 | tf_op jit(solution)/shard_map/all_to_all | solution.py:276
  64.1 8.3 %collective-permute-start.2 = (bf16[128,1024]{1,0:T(8,128)(2,1)S(1)}, bf16[128,1024]{1,0:T(8,128)(2,1)S(1)}, u32[]{:S(2)}, u32[]{:S(2)}) collective-permute-start(bf16[128,1024]{1,0:T(8,128)(2,1)S(1)} %collective-permute-done), channel_id=1, source_target_pairs={{0,1},{1,2},{2,3},{3,0},{4,5},{5,6},{6,7},{7,4},{8,9},{9,10},{10,1... | collective-permute-start | bytes 786440 | tf_op jit(solution)/shard_map/ppermute | solution.py:283
  66.1 40.2 %copy-start.1 = (bf16[256,1024]{1,0:T(8,128)(2,1)}, bf16[256,1024]{1,0:T(8,128)(2,1)S(1)}, u32[]{:S(2)}) copy-start(bf16[256,1024]{1,0:T(8,128)(2,1)S(1)} %pad_maximum_fusion.b0) | copy-start | bytes 1572868
  66.1 17.2 %collective-permute-start.3 = (bf16[256,1024]{1,0:T(8,128)(2,1)S(1)}, bf16[256,1024]{1,0:T(8,128)(2,1)S(1)}, u32[]{:S(2)}, u32[]{:S(2)}) collective-permute-start(bf16[256,1024]{1,0:T(8,128)(2,1)S(1)} %pad_maximum_fusion.b0), channel_id=1, source_target_pairs={{0,8},{1,9},{2,10},{3,11},{4,12},{5,13},{6,14},{7,15},{8,16},{9,17... | collective-permute-start | bytes 1572872 | tf_op jit(solution)/shard_map/ppermute | solution.py:285
  72.5 33.8 %copy-start.2 = (bf16[256,1024]{1,0:T(8,128)(2,1)}, bf16[256,1024]{1,0:T(8,128)(2,1)S(1)}, u32[]{:S(2)}) copy-start(bf16[256,1024]{1,0:T(8,128)(2,1)S(1)} %constant_dynamic-update-slice_fusion.b1) | copy-start | bytes 1572868
  72.5 12.8 %collective-permute-start.6 = (bf16[256,1024]{1,0:T(8,128)(2,1)S(1)}, bf16[256,1024]{1,0:T(8,128)(2,1)S(1)}, u32[]{:S(2)}, u32[]{:S(2)}) collective-permute-start(bf16[256,1024]{1,0:T(8,128)(2,1)S(1)} %constant_dynamic-update-slice_fusion.b1), channel_id=1, source_target_pairs={{0,24},{1,25},{2,26},{3,27},{4,28},{5,29},{6,30},{7,31},{8,0},{9,1... | collective-permute-start | bytes 1572872 | tf_op jit(solution)/shard_map/ppermute | solution.py:289
  78.0 28.3 %collective-permute-start.4 = (bf16[256,1024]{1,0:T(8,128)(2,1)S(1)}, bf16[256,1024]{1,0:T(8,128)(2,1)S(1)}, u32[]{:S(2)}, u32[]{:S(2)}) collective-permute-start(bf16[256,1024]{1,0:T(8,128)(2,1)S(1)} %pad_maximum_fusion.b0), channel_id=1, source_target_pairs={{0,24},{1,25},{2,26},{3,27},{4,28},{5,29},{6,30},{7,31},{8,0},{9,1... | collective-permute-start | bytes 1572872 | tf_op jit(solution)/shard_map/ppermute | solution.py:286
  80.2 31.9 %collective-permute-start.5 = (bf16[256,1024]{1,0:T(8,128)(2,1)S(1)}, bf16[256,1024]{1,0:T(8,128)(2,1)}, u32[]{:S(2)}, u32[]{:S(2)}) collective-permute-start(bf16[256,1024]{1,0:T(8,128)(2,1)S(1)} %constant_dynamic-update-slice_fusion.b1), channel_id=1, source_target_pairs={{0,8},{1,9},{2,10},{3,11},{4,12},{5,13},{6,14},{7,15},{8,16},{9,17... | collective-permute-start | bytes 1572872 | tf_op jit(solution)/shard_map/ppermute | solution.py:288
  83.4 23.0 %copy-start.4 = (bf16[256,1024]{1,0:T(8,128)(2,1)}, bf16[256,1024]{1,0:T(8,128)(2,1)S(1)}, u32[]{:S(2)}) copy-start(bf16[256,1024]{1,0:T(8,128)(2,1)S(1)} %collective-permute-done.3.b2) | copy-start | bytes 1572868
  83.4 28.8 %collective-permute-start.7 = (bf16[256,1024]{1,0:T(8,128)(2,1)S(1)}, bf16[256,1024]{1,0:T(8,128)(2,1)}, u32[]{:S(2)}, u32[]{:S(2)}) collective-permute-start(bf16[256,1024]{1,0:T(8,128)(2,1)S(1)} %collective-permute-done.3.b2), channel_id=1, source_target_pairs={{0,8},{1,9},{2,10},{3,11},{4,12},{5,13},{6,14},{7,15},{8,16},{9,17... | collective-permute-start | bytes 1572872 | tf_op jit(solution)/shard_map/ppermute | solution.py:290
  85.3 26.9 %copy-start.5 = (bf16[256,1024]{1,0:T(8,128)(2,1)}, bf16[256,1024]{1,0:T(8,128)(2,1)S(1)}, u32[]{:S(2)}) copy-start(bf16[256,1024]{1,0:T(8,128)(2,1)S(1)} %collective-permute-done.6.b5) | copy-start | bytes 1572868
  85.3 26.8 %collective-permute-start.8 = (bf16[256,1024]{1,0:T(8,128)(2,1)S(1)}, bf16[256,1024]{1,0:T(8,128)(2,1)}, u32[]{:S(2)}, u32[]{:S(2)}) collective-permute-start(bf16[256,1024]{1,0:T(8,128)(2,1)S(1)} %collective-permute-done.6.b5), channel_id=1, source_target_pairs={{0,24},{1,25},{2,26},{3,27},{4,28},{5,29},{6,30},{7,31},{8,0},{9,1... | collective-permute-start | bytes 1572872 | tf_op jit(solution)/shard_map/ppermute | solution.py:291
  89.9 10.2 %copy-start.3 = (bf16[8,160,128]{2,1,0:T(8,128)(2,1)}, bf16[8,160,128]{2,1,0:T(8,128)(2,1)S(1)}, u32[]{:S(2)}) copy-start(bf16[8,160,128]{2,1,0:T(8,128)(2,1)S(1)} %all-to-all-done.1.mine_ref) | copy-start | bytes 983044
  89.9 14.3 %collective-permute-start.13 = (bf16[8,160,128]{2,1,0:T(8,128)(2,1)S(1)}, bf16[8,160,128]{2,1,0:T(8,128)(2,1)}, u32[]{:S(2)}, u32[]{:S(2)}) collective-permute-start(bf16[8,160,128]{2,1,0:T(8,128)(2,1)S(1)} %all-to-all-done.1.mine_ref), channel_id=1, source_target_pairs={{0,32},{32,0},{64,96},{96,64},{128,160},{160,128},{192,224},{224,1... | collective-permute-start | bytes 983048 | tf_op jit(solution)/shard_map/ppermute | solution.py:277
  106.3 0.8 copy-start.6
  117.4 3.8 %collective-permute-start.14 = (bf16[200,1024]{1,0:T(8,128)(2,1)}, bf16[200,1024]{1,0:T(8,128)(2,1)S(1)}, u32[]{:S(2)}, u32[]{:S(2)}) collective-permute-start(bf16[200,1024]{1,0:T(8,128)(2,1)} %shard_map.89.own_ref), channel_id=1, source_target_pairs={{0,32},{32,0},{64,96},{96,64},{128,160},{160,128},{192,224},{224,1... | collective-permute-start | bytes 1228808 | tf_op jit(solution)/shard_map/ppermute | solution.py:318
  121.3 0.7 copy-start.7

commit v4 on v3

v4 whole, which is shorter than its diff:
```python
import itertools

import jax
import jax.numpy as jnp
from jax import lax
from jax.experimental import pallas as pl
from jax.experimental.pallas import tpu as pltpu
from jax.sharding import Mesh
from jax.sharding import PartitionSpec as P


STEP = 0.04
BF = jnp.bfloat16
F32 = jnp.float32
VM = pltpu.VMEM
OFFS = (0, -1, 1, 2)
ARRIVAL = tuple((o, i) for o, half in ((0, 0), (0, 2), (1, 0), (2, 0), (1, 2), (2, 2), (3, 0), (3, 2)) for i in (half, half + 1))
ALL = ("zl", "core", "y", "zh", "x")
SPLIT = (8, 2, 4, 2, 4)


def shift(moves):
    every = list(itertools.product(*map(range, SPLIT)))
    number = {at: i for i, at in enumerate(every)}
    pairs = ((number[at], number.get(moves(*at))) for at in every)
    return [(i, j) for i, j in pairs if j is not None]


def plane_shift(phase, step):
    def moves(zl, core, y, zh, x):
        if (core + phase) % 2 == 0:
            return zl, core, y, zh, (x + step) % 4
        return zl, core, (y + step) % 4, zh, x

    return shift(moves)


def shape(dims, kind):
    return jax.ShapeDtypeStruct(dims, kind)


def halves(low, high):
    lane = lax.broadcasted_iota(jnp.int32, low.shape, 1)
    return jnp.where(lane < 64, low, high)


def swapped(x):
    return pltpu.roll(x, 64, 1)


def rows_kernel(at_ref, modes_ref, logs_ref, out_ref, scr_ref, log_ref):
    scr_ref[...] = modes_ref[...].astype(F32)
    log_ref[...] = logs_ref[...]
    upper = jnp.zeros((1, 128), jnp.int32) + at_ref[0] == 0
    for k in range(2):
        logs = jnp.where(upper, log_ref[pl.ds(k, 8, stride=8), :], log_ref[pl.ds(6 + k, 8, stride=8), :])
        high = logs.astype(BF).astype(F32)
        block = jnp.where(upper, scr_ref[pl.ds(k, 64, stride=8), :], scr_ref[pl.ds(6 + k, 64, stride=8), :])
        out_ref[k * 80 : k * 80 + 80, :] = jnp.concatenate([block, high, logs - high], axis=0).astype(BF)


def channels_kernel(modes_ref, logs_ref, chan_ref, scr_ref, log_ref):
    scr_ref[...] = modes_ref[...].astype(F32)
    log_ref[...] = logs_ref[...]
    zeros = jnp.zeros((48, 128), F32)
    for y in range(8):
        block = scr_ref[pl.ds(y, 64, stride=8), :]
        logs = log_ref[pl.ds(y, 8, stride=8), :]
        high = logs.astype(BF).astype(F32)
        chan_ref[y] = jnp.concatenate([block, high, logs - high, zeros], axis=0).T


def edges_kernel(at_ref, chan_ref, got_ref, full_ref, last_ref, lead_ref):
    lower = at_ref[0]
    zeros = jnp.zeros((48, 128), F32)
    got = got_ref[...].astype(F32)
    for k in range(2):
        full_ref[8 - 8 * lower + k, 8:136, :] = jnp.concatenate([got[k * 80 : k * 80 + 80], zeros], axis=0).T
    for r in range(8):
        full_ref[2 * lower + r, 8:136, :] = chan_ref[r]
    for r in range(10):
        last_ref[r * 8 : r * 8 + 8] = full_ref[r, 128:136, :].astype(BF)
        lead_ref[r * 8 : r * 8 + 8] = full_ref[r, 8:16, :].astype(BF)


def patches_kernel(at_ref, full_ref, left_ref, right_ref, pars_ref, send_ref, wide_ref, cell_ref, scr_ref):
    left, right = left_ref[...].astype(F32), right_ref[...].astype(F32)
    for r in range(10):
        wide_ref[r, 0:8, :] = left[r * 8 : r * 8 + 8]
        wide_ref[r, 8:136, :] = full_ref[r, 8:136, :]
        wide_ref[r, 136:144, :] = right[r * 8 : r * 8 + 8]
    lower = jnp.zeros((1, 128), jnp.int32) + at_ref[0] == 1
    pars = pars_ref[...]
    high = pars.astype(BF).astype(F32)
    scr_ref[60:80, :] = jnp.where(lower, pars - high, high)
    scr_ref[88:96, :] = jnp.zeros((8, 128), F32)
    lane = lax.broadcasted_iota(jnp.int32, (15, 128), 1)
    for d in range(16):
        for r in range(10):
            cell_ref[r * 12 : r * 12 + 12, :] = wide_ref[r, 8 * d + 6 : 8 * d + 18, :]
        scr_ref[0:60, :] = halves(cell_ref[0:60, :], swapped(cell_ref[60:120, :]))
        logs = jnp.zeros((15, 128), F32)
        for g in range(8):
            piece = pltpu.roll(cell_ref[g * 15 : g * 15 + 15, :], (g * 16 - 64) % 128, 1)
            logs = jnp.where((lane >= g * 16) & (lane < g * 16 + 16), piece, logs)
        scr_ref[80:95, :] = logs
        send_ref[d] = scr_ref[...].astype(BF)


PLACES = (((0, 5, 2), (5, 8, 7), (8, 10, 18)), ((0, 2, 0), (2, 5, 10), (5, 10, 13)))


def coef_kernel(at_ref, mine_ref, coef_ref, wr_ref, scr_ref, par_ref, cell_ref, log_ref):
    for z in range(16):
        scr_ref[z * 20 : (z + 1) * 20, :] = mine_ref[z].astype(F32)[60:80]
    sub = lax.broadcasted_iota(jnp.int32, (8, 128), 0)
    grp = lax.broadcasted_iota(jnp.int32, (8, 128), 1) // 16
    for v in range(10):
        for h in range(2):
            at = v * 2 + h
            got = scr_ref[pl.ds(at, 8, stride=20), :] + scr_ref[pl.ds(at + 160, 8, stride=20), :]
            for s in (1, 2, 4):
                up = pltpu.roll(pltpu.roll(got, 8 - s, 0), 16 * s, 1)
                down = pltpu.roll(pltpu.roll(got, s, 0), 128 - 16 * s, 1)
                mine, bit = (sub & s) > 0, (grp & s) > 0
                got = jnp.where(mine == bit, got, jnp.where(mine, down, up))
            par_ref[v, h * 8 : h * 8 + 8, :] = got
    for zh in range(2):
        logs = mine_ref[zh * 8].astype(F32)[80:96]
        logs = logs + pltpu.roll(logs, 120, 1)
        for g in range(8):
            cell_ref[g * 15 : g * 15 + 15, :] = pltpu.roll(logs, (128 - g * 16) % 128, 1)[0:15]
        for first, last, row in PLACES[zh]:
            log_ref[row * 12 : (row + last - first) * 12, :] = cell_ref[first * 12 : last * 12, :]
    cols = [log_ref[:, j : j + 1] for j in range(8)]
    for n in range(16):
        p = at_ref[2 + n]
        for v in range(2):
            wr_ref[v, n : n + 1, :] = par_ref[v, pl.ds(p, 1), :]
        acc = cols[0] * par_ref[2, pl.ds(p, 1), :]
        for j in range(1, 8):
            acc = acc + cols[j] * par_ref[2 + j, pl.ds(p, 1), :]
        coef_ref[n] = jnp.exp(acc)


def state_kernel(at_ref, mine_ref, theirs_ref, state_ref, scr_ref):
    first = jnp.zeros((1, 128), jnp.int32) + at_ref[1] == 0
    for z in range(8):
        for zh in range(2):
            mine, theirs = mine_ref[zh * 8 + z].astype(F32)[0:60], theirs_ref[zh * 8 + z].astype(F32)[0:60]
            zero, one = jnp.where(first, mine, theirs), jnp.where(first, theirs, mine)
            both = (halves(zero, swapped(one)), halves(swapped(zero), one))
            for lo, hi, row in PLACES[zh]:
                piece = both[lo // 5][(lo % 5) * 12 : (lo % 5 + hi - lo) * 12]
                scr_ref[row * 12 : (row + hi - lo) * 12, :] = piece
        state_ref[:, z * 128 : (z + 1) * 128] = scr_ref[...].astype(BF)


def drive(f_ref, h, coef_ref, c, rows, skip, rate, weight):
    def f(d):
        return f_ref[h, 12 + d : 12 + d + rows, :]

    def k(d):
        return coef_ref[c, skip + 12 + d : skip + 12 + d + rows, :]

    mid, kmid = f(0), k(0)
    total = (kmid + k(-12)) * (f(-12) - mid)
    for d in (12, -1, 1):
        total = total + (kmid + k(d)) * (f(d) - mid)
    total = total + rate * (mid - mid * mid * mid)
    return (weight * total).astype(BF)


def sweep(state, basis_refs, coef_ref, wr_ref, f_ref, acc_ref, rows, skip, c=0):
    for ref in basis_refs:
        block = ref[...]
        field = lax.dot_general(state, block, (((1,), (1,)), ((), ())), preferred_element_type=F32)
        parts = []
        for h in range(2):
            f_ref[h, : field.shape[0], :] = field[:, h * 128 : (h + 1) * 128]
            weight, rate = wr_ref[0, c : c + 1, :], wr_ref[1, c : c + 1, :]
            parts.append(drive(f_ref, h, coef_ref, c, rows, skip, rate, weight))
            c += 1
        acc_ref[...] += jnp.dot(jnp.concatenate(parts, axis=1), block, preferred_element_type=F32)


def first_kernel(*refs):
    blocks, (state_ref, coef_ref, wr_ref, out_ref, f_ref, acc_ref) = refs[:8], refs[8:]
    acc_ref[...] = jnp.zeros_like(acc_ref)
    sweep(state_ref[...], blocks, coef_ref, wr_ref, f_ref, acc_ref, 216, 0)
    out_ref[...] = acc_ref[...].astype(BF)


def second_kernel(edge_ref, *refs):
    blocks, (state_ref, coef_ref, wr_ref, own_ref, other_ref, out_ref, f_ref, acc_ref) = refs[:8], refs[8:]
    total = own_ref[...].astype(F32) + other_ref[...].astype(F32)
    now = state_ref[...].astype(F32)[12:228]
    cell = lax.broadcasted_iota(jnp.int32, (216, 128), 0).astype(F32)
    row = jnp.floor((cell + 0.5) * (1.0 / 12.0))
    col = cell - 12.0 * row
    low = jnp.where(edge_ref[0] == 1, 1.0, 0.0)
    high = jnp.where(edge_ref[1] == 1, 16.0, 17.0)
    left = jnp.where(edge_ref[2] == 1, 2.0, 0.0)
    right = jnp.where(edge_ref[3] == 1, 9.0, 11.0)
    inside = (row >= low) & (row <= high) & (col >= left) & (col <= right)
    keep = jnp.where(inside, 1.0, 0.0)[:, 0:1]
    state = ((now + STEP * total) * keep).astype(BF)
    acc_ref[...] = jnp.zeros_like(acc_ref)
    sweep(state, blocks, coef_ref, wr_ref, f_ref, acc_ref, 192, 12)
    for zh in range(2):
        for z in range(8):
            to = (zh * 8 + z) * 2
            for y in range(4):
                at = (zh * 8 + y) * 12 + 2
                low = acc_ref[at : at + 8, z * 128 : (z + 1) * 128]
                high = acc_ref[at + 48 : at + 56, z * 128 : (z + 1) * 128]
                out_ref[to, y * 8 : y * 8 + 8, :] = halves(low, swapped(high)).astype(BF)
                out_ref[to + 1, y * 8 : y * 8 + 8, :] = halves(swapped(low), high).astype(BF)


def finish_kernel(back_ref, modes_ref, out_ref, scr_ref):
    for y in range(4):
        parts = [
            back_ref[2 * d, y * 8 : y * 8 + 8, :].astype(F32) + back_ref[2 * d + 1, y * 8 : y * 8 + 8, :].astype(F32)
            for d in range(16)
        ]
        turned = jnp.concatenate(parts, axis=0).T
        scr_ref[pl.ds(y, 64, stride=8), :] = turned[0:64]
        scr_ref[pl.ds(y + 4, 64, stride=8), :] = turned[64:128]
    out_ref[...] = modes_ref[...].astype(F32) + STEP * scr_ref[...]


SMEM = pl.BlockSpec(memory_space=pltpu.SMEM)
WHOLE = pl.BlockSpec(memory_space=pltpu.VMEM)


def call(kernel, outs, scratch, scalars, *args):
    specs = [SMEM] * scalars + [WHOLE] * (len(args) - scalars)
    single = not isinstance(outs, (list, tuple))
    return pl.pallas_call(
        kernel,
        out_shape=outs,
        in_specs=specs,
        out_specs=WHOLE if single else [WHOLE] * len(outs),
        scratch_shapes=scratch,
    )(*args)


def update(modes_now, basis_rows, quad_weights, germ_nodes, log_fields, reaction_rates):
    zl, core, y, zh, x = (lax.axis_index(axis) for axis in ALL)
    outer = jnp.asarray([OFFS[o] for o, _ in ARRIVAL], jnp.int32)
    inner = jnp.asarray([OFFS[i] for _, i in ARRIVAL], jnp.int32)
    dy, dx = jnp.where(core == 0, outer, inner), jnp.where(core == 0, inner, outer)
    order = ((y + dy) % 4) * 4 + (x + dx) % 4
    at = jnp.concatenate([jnp.stack([zh, core]), order]).astype(jnp.int32)

    part = lax.dynamic_slice_in_dim(basis_rows, (y * 4 + x) * 16, 16, axis=0)
    send = jnp.broadcast_to(part[None], (8, 16, 1024))
    shard = lax.all_to_all(send, "zl", 0, 0, tiled=True).reshape(128, 1024)

    modes, logs = modes_now.reshape(512, 128), log_fields.reshape(64, 128)
    scratch = [VM((512, 128), F32), VM((64, 128), F32)]
    rows = call(rows_kernel, shape((160, 128), BF), scratch, 1, at, modes, logs)

    def toward(zl, core, y, zh, x):
        return zl, core, y + 2 * zh - 1, zh, x

    got = lax.ppermute(rows, ALL, shift(toward))
    chan = call(channels_kernel, shape((8, 128, 128), F32), scratch, 0, modes, logs)
    full, last, lead = call(
        edges_kernel,
        [shape((10, 144, 128), F32), shape((80, 128), BF), shape((80, 128), BF)],
        [],
        1,
        at,
        chan,
        got,
    )
    right = [(i, i + 1) for i in range(3)]
    from_left = lax.ppermute(last, "x", right)
    from_right = lax.ppermute(lead, "x", [(j, i) for i, j in right])
    pars = jnp.concatenate([quad_weights[None], reaction_rates[None], germ_nodes.T], axis=0).reshape(20, 128)
    patch = call(
        patches_kernel,
        shape((16, 96, 128), BF),
        [VM((10, 144, 128), F32), VM((120, 128), F32), VM((96, 128), F32)],
        1,
        at,
        full,
        from_left,
        from_right,
        pars,
    )
    mine = lax.all_to_all(patch, ("zh", "zl"), 0, 0, tiled=True)
    theirs = lax.ppermute(mine, "core", [(0, 1), (1, 0)])

    fwd, bwd = plane_shift(0, 1), plane_shift(0, -1)
    less = lax.ppermute(shard, ALL, fwd)
    more = lax.ppermute(shard, ALL, bwd)
    near = jnp.concatenate([shard, less], axis=0)
    far = lax.ppermute(less, ALL, fwd)
    fwd, bwd = plane_shift(1, 1), plane_shift(1, -1)
    near_less = lax.ppermute(near, ALL, fwd)
    near_more = lax.ppermute(near, ALL, bwd)
    away = jnp.concatenate([more, far], axis=0)
    away_less = lax.ppermute(away, ALL, fwd)
    away_more = lax.ppermute(away, ALL, bwd)
    near_far = lax.ppermute(near_less, ALL, fwd)
    away_far = lax.ppermute(away_more, ALL, bwd)
    blocks = (near, away, near_less, near_more, away_less, away_more, near_far, away_far)

    coef, wr = call(
        coef_kernel,
        [shape((16, 240, 128), F32), shape((2, 16, 128), F32)],
        [VM((320, 128), F32), VM((10, 16, 128), F32), VM((120, 128), F32), VM((240, 128), F32)],
        1,
        at,
        mine,
    )
    state = call(state_kernel, shape((240, 1024), BF), [VM((240, 128), F32)], 1, at, mine, theirs)
    own = call(
        first_kernel,
        shape((216, 1024), BF),
        [VM((2, 240, 128), F32), VM((216, 1024), F32)],
        0,
        *blocks,
        state,
        coef,
        wr,
    )
    other = lax.ppermute(own, "core", [(0, 1), (1, 0)])
    strip = zh * 8 + zl
    edge = jnp.stack([y == 0, y == 3, (x == 0) & (strip == 0), (x == 3) & (strip == 15)]).astype(jnp.int32)
    out = call(
        second_kernel,
        shape((32, 32, 128), BF),
        [VM((2, 216, 128), F32), VM((192, 1024), F32)],
        1,
        edge,
        *blocks,
        state,
        coef,
        wr,
        own,
        other,
    )
    back = lax.all_to_all(out, ("zh", "zl", "core"), 0, 0, tiled=True)
    result = call(finish_kernel, shape((512, 128), F32), [VM((512, 128), F32)], 0, back, modes)
    return result.reshape(64, 8, 128)


def solution(mesh):
    fine = Mesh(mesh.devices.reshape(SPLIT), ALL)
    quad = ("zl", "core")
    in_specs = (P(quad, ("y", "zh"), "x"), P(quad, None), P(quad), P(quad, None), P(None, ("y", "zh"), "x"), P(quad))
    out_specs = P(quad, ("y", "zh"), "x")
    return jax.shard_map(update, mesh=fine, in_specs=in_specs, out_specs=out_specs, check_vma=False)
```

time: 159 us -> 153 us (0.962)
  starting transfers between devices: 84.1 us -> 68.9 us
  blocking collectives: 27.1 us -> 34.6 us
  waiting for transfers between devices: 5.5 us -> 11 us
  Pallas kernels: 33.2 us -> 30.2 us
    all_to_all x1, blocking collectives: 27.1 us -> 34.6 us  [update(): back = lax.all_to_all(out, ('zh', 'zl', 'core'), 0, 0, tiled=True)]
    ppermute x6 -> x5, starting transfers between devices: 25.7 us -> 19.5 us  [the longest x1 11.9 us: update(): theirs = lax.ppermute(mine, 'core', [(0, 1), (1, 0)])]
    ppermute x1, starting transfers between devices: 8.13 us -> 3.2 us  [update(): less = lax.ppermute(shard, ALL, fwd)]
    ppermute x6 -> x5, waiting for transfers between devices: 2.42 us -> 5.8 us  [the longest x1 2.78 us: update(): from_right = lax.ppermute(lead, 'x', [(j, i) for i, j in right])]
    pallas_call x10 -> x9, Pallas kernels: 33.2 us -> 30.2 us  [call(): pl.pallas_call(kernel, out_shape=outs, in_specs=specs, out_specs=WHOLE if...]
    ppermute x1, starting transfers between devices: 5.55 us -> 2.92 us  [update(): away_more = lax.ppermute(away, ALL, bwd)]
    ppermute x1, waiting for transfers between devices: 0.01 us -> 1.82 us  [update(): less = lax.ppermute(shard, ALL, fwd)]
    ppermute x1, starting transfers between devices: 2.17 us -> 3.93 us  [update(): near_more = lax.ppermute(near, ALL, bwd)]
  transfers between devices with their start and end apart: 17 -> 16, of which waited for: 4 -> 5; matrix products, arithmetic and copies ran while one was open for 2% -> 2% of each run, Pallas kernels for 12% -> 10%
where the time goes in v4:
time: 153 us; the launch traced here: 152 us
  starting transfers between devices  68.9 us (45%)
  blocking collectives  34.6 us (23%)
  Pallas kernels  30.2 us (20%)
  waiting for transfers between devices  11 us (7%)
  local copies, waits for them, and re-layouts  5.15 us (3%)
  other arithmetic  2 us (1%)
    all_to_all x1, blocking collectives, update(): back = lax.all_to_all(out, ('zh', 'zl', 'core'), 0, 0, tiled=True)  34.6 us
    pallas_call x9, Pallas kernels, call(): pl.pallas_call(kernel, out_shape=outs, in_specs=specs, out_specs=WHOLE if...  30.2 us
    all_to_all x1, starting transfers between devices, update(): shard = lax.all_to_all(send, 'zl', 0, 0, tiled=True).reshape(128, 1024)  13.1 us
    ppermute x1, starting transfers between devices, update(): theirs = lax.ppermute(mine, 'core', [(0, 1), (1, 0)])  11.9 us
    all_to_all x1, starting transfers between devices, update(): mine = lax.all_to_all(patch, ('zh', 'zl'), 0, 0, tiled=True)  9.45 us
    ppermute x1, starting transfers between devices, update(): away_far = lax.ppermute(away_more, ALL, bwd)  4.57 us
    ppermute x1, starting transfers between devices, update(): near_more = lax.ppermute(near, ALL, bwd)  3.93 us
    unnamed x29, local copies, waits for them, and re-layouts  3.8 us
  transfers between devices with their start and end apart: 16, of which 5 were waited for; matrix products, arithmetic and copies ran while one was open for 2% of the time, Pallas kernels for 10%

profile of v4, /device:TPU:1, one launch (start us, length us, event | category | flops | bytes accessed | tf_op | source)
XLA Modules:
  0.0 152.2 jit_solution(3967930625224930719)
XLA Ops:
  0.0 1.0 copy-done
  1.8 13.1 %all-to-all-start = ((bf16[8,16,1024]{2,1,0:T(8,128)(2,1)}), bf16[8,16,1024]{2,1,0:T(8,128)(2,1)S(1)}, u32[]{:S(2)}, u32[]{:S(2)}) async-start(bf16[8,16,1024]{2,1,0:T(8,128)(2,1)} %broadcast_in_dim.12), calls=%async_computation | async-start | bytes 524288 | tf_op jit(solution)/shard_map/all_to_all | solution.py:259
  16.2 1.6 %shard_map.83 = bf16[160,128]{1,0:T(8,128)(2,1)} custom-call(s32[18]{0:T(128)} %pad_add_fusion.at_ref, bf16[512,128]{1,0:T(8,128)(2,1)} %bitcast.13, f32[64,128]{1,0:T(8,128)} %bitcast.19), custom_call_target="tpu_custom_call" | custom-call | tf_op jit(solution)/shard_map/pallas_call | solution.py:240
  17.8 1.3 collective-permute-start.9
  19.0 2.0 %shard_map.82.chan_ref = f32[8,128,128]{2,1,0:T(8,128)} custom-call(bf16[512,128]{1,0:T(8,128)(2,1)} %bitcast.14, f32[64,128]{1,0:T(8,128)} %bitcast.20), custom_call_target="tpu_custom_call" | custom-call | tf_op jit(solution)/shard_map/pallas_call | solution.py:240
  21.0 1.7 %collective-permute-done.9.got_ref = bf16[160,128]{1,0:T(8,128)(2,1)S(1)} collective-permute-done((bf16[160,128]{1,0:T(8,128)(2,1)}, bf16[160,128]{1,0:T(8,128)(2,1)S(1)}, u32[]{:S(2)}, u32[]{:S(2)}) %collective-permute-start.9) | collective-permute-done | bytes 40992 | tf_op jit(solution)/shard_map/ppermute | solution.py:268
  23.3 2.1 %shard_map.84 = (f32[10,144,128]{2,1,0:T(8,128)}, bf16[80,128]{1,0:T(8,128)(2,1)}, bf16[80,128]{1,0:T(8,128)(2,1)}) custom-call(s32[18]{0:T(128)} %pad_add_fusion.at_ref, f32[8,128,128]{2,1,0:T(8,128)} %shard_map.82.chan_ref, bf16[160,128]{1,0:T(8,128)(2,1)} %copy-done.8), custom_call_target="tpu_custom_call" | custom-call | tf_op jit(solution)/shard_map/pallas_call | solution.py:240
  25.4 3.1 %collective-permute-start.10 = (bf16[80,128]{1,0:T(8,128)(2,1)}, bf16[80,128]{1,0:T(8,128)(2,1)S(1)}, u32[]{:S(2)}, u32[]{:S(2)}) collective-permute-start(bf16[80,128]{1,0:T(8,128)(2,1)} %get-tuple-element.11), channel_id=1, source_target_pairs={{0,1},{1,2},{2,3},{4,5},{5,6},{6,7},{8,9},{9,10},{10,11},{12,13},{... | collective-permute-start | bytes 61448 | tf_op jit(solution)/shard_map/ppermute | solution.py:280
  28.6 1.3 collective-permute-start.11
  30.5 2.8 %collective-permute-done.11.right_ref = bf16[80,128]{1,0:T(8,128)(2,1)S(1)} collective-permute-done((bf16[80,128]{1,0:T(8,128)(2,1)}, bf16[80,128]{1,0:T(8,128)(2,1)S(1)}, u32[]{:S(2)}, u32[]{:S(2)}) %collective-permute-start.11) | collective-permute-done | bytes 20512 | tf_op jit(solution)/shard_map/ppermute | solution.py:281
  33.9 2.5 %shard_map.85 = bf16[16,96,128]{2,1,0:T(8,128)(2,1)} custom-call(s32[18]{0:T(128)} %pad_add_fusion.at_ref, f32[10,144,128]{2,1,0:T(8,128)} %get-tuple-element.10.full_ref, bf16[80,128]{1,0:T(8,128)(2,1)} %copy-done.9, bf16[80,128]{1,0:T(8,128)(2,1)} %copy-done.10, f32[20,128]{1,0:T(8,128)} %reshape.19.pars_ref), custom_call_target="tpu_custom_call" | custom-call | tf_op jit(solution)/shard_map/pallas_call | solution.py:240
  36.4 9.4 %all-to-all-start.1 = ((bf16[16,96,128]{2,1,0:T(8,128)(2,1)}), bf16[16,96,128]{2,1,0:T(8,128)(2,1)S(1)}, u32[]{:S(2)}, u32[]{:S(2)}) async-start(bf16[16,96,128]{2,1,0:T(8,128)(2,1)} %shard_map.85), calls=%async_computation.1 | async-start | bytes 786432 | tf_op jit(solution)/shard_map/all_to_all | solution.py:294
  45.9 3.2 %collective-permute-start = (bf16[128,1024]{1,0:T(8,128)(2,1)S(1)}, bf16[128,1024]{1,0:T(8,128)(2,1)S(1)}, u32[]{:S(2)}, u32[]{:S(2)}) collective-permute-start(bf16[128,1024]{1,0:T(8,128)(2,1)S(1)} %bitcast.16), channel_id=1, source_target_pairs={{0,1},{1,2},{2,3},{3,0},{4,5},{5,6},{6,7},{7,4},{8,9},{9,10},{10,1... | collective-permute-start | bytes 786440 | tf_op jit(solution)/shard_map/ppermute | solution.py:298
  49.1 3.3 %collective-permute-start.1 = (bf16[128,1024]{1,0:T(8,128)(2,1)S(1)}, bf16[128,1024]{1,0:T(8,128)(2,1)S(1)}, u32[]{:S(2)}, u32[]{:S(2)}) collective-permute-start(bf16[128,1024]{1,0:T(8,128)(2,1)S(1)} %bitcast.17), channel_id=1, source_target_pairs={{0,3},{1,0},{2,1},{3,2},{4,7},{5,4},{6,5},{7,6},{8,11},{9,8},{10,9... | collective-permute-start | bytes 786440 | tf_op jit(solution)/shard_map/ppermute | solution.py:299
  52.4 1.8 %collective-permute-done = bf16[128,1024]{1,0:T(8,128)(2,1)S(1)} collective-permute-done((bf16[128,1024]{1,0:T(8,128)(2,1)S(1)}, bf16[128,1024]{1,0:T(8,128)(2,1)S(1)}, u32[]{:S(2)}, u32[]{:S(2)}) %collective-permute-start) | collective-permute-done | bytes 262176 | tf_op jit(solution)/shard_map/ppermute | solution.py:298
  54.2 2.0 %collective-permute-start.2 = (bf16[128,1024]{1,0:T(8,128)(2,1)S(1)}, bf16[128,1024]{1,0:T(8,128)(2,1)S(1)}, u32[]{:S(2)}, u32[]{:S(2)}) collective-permute-start(bf16[128,1024]{1,0:T(8,128)(2,1)S(1)} %collective-permute-done), channel_id=1, source_target_pairs={{0,1},{1,2},{2,3},{3,0},{4,5},{5,6},{6,7},{7,4},{8,9},{9,10},{10,1... | collective-permute-start | bytes 786440 | tf_op jit(solution)/shard_map/ppermute | solution.py:301
  56.2 3.1 %collective-permute-start.3 = (bf16[256,1024]{1,0:T(8,128)(2,1)S(1)}, bf16[256,1024]{1,0:T(8,128)(2,1)S(1)}, u32[]{:S(2)}, u32[]{:S(2)}) collective-permute-start(bf16[256,1024]{1,0:T(8,128)(2,1)S(1)} %pad_maximum_fusion.refs_0_), channel_id=1, source_target_pairs={{0,8},{1,9},{2,10},{3,11},{4,12},{5,13},{6,14},{7,15},{8,16},{9,17... | collective-permute-start | bytes 1572872 | tf_op jit(solution)/shard_map/ppermute | solution.py:303
  59.4 3.4 %collective-permute-done.2 = bf16[128,1024]{1,0:T(8,128)(2,1)S(1)} collective-permute-done((bf16[128,1024]{1,0:T(8,128)(2,1)S(1)}, bf16[128,1024]{1,0:T(8,128)(2,1)S(1)}, u32[]{:S(2)}, u32[]{:S(2)}) %collective-permute-start.2) | collective-permute-done | bytes 262176 | tf_op jit(solution)/shard_map/ppermute | solution.py:301
  62.8 2.9 %collective-permute-start.6 = (bf16[256,1024]{1,0:T(8,128)(2,1)S(1)}, bf16[256,1024]{1,0:T(8,128)(2,1)S(1)}, u32[]{:S(2)}, u32[]{:S(2)}) collective-permute-start(bf16[256,1024]{1,0:T(8,128)(2,1)S(1)} %constant_dynamic-update-slice_fusion.refs_1_), channel_id=1, source_target_pairs={{0,24},{1,25},{2,26},{3,27},{4,28},{5,29},{6,30},{7,31},{8,0},{9,1... | collective-permute-start | bytes 1572872 | tf_op jit(solution)/shard_map/ppermute | solution.py:307
  65.8 3.9 %collective-permute-start.4 = (bf16[256,1024]{1,0:T(8,128)(2,1)S(1)}, bf16[256,1024]{1,0:T(8,128)(2,1)S(1)}, u32[]{:S(2)}, u32[]{:S(2)}) collective-permute-start(bf16[256,1024]{1,0:T(8,128)(2,1)S(1)} %pad_maximum_fusion.refs_0_), channel_id=1, source_target_pairs={{0,24},{1,25},{2,26},{3,27},{4,28},{5,29},{6,30},{7,31},{8,0},{9,1... | collective-permute-start | bytes 1572872 | tf_op jit(solution)/shard_map/ppermute | solution.py:304
  69.7 1.9 %collective-permute-start.5 = (bf16[256,1024]{1,0:T(8,128)(2,1)S(1)}, bf16[256,1024]{1,0:T(8,128)(2,1)}, u32[]{:S(2)}, u32[]{:S(2)}) collective-permute-start(bf16[256,1024]{1,0:T(8,128)(2,1)S(1)} %constant_dynamic-update-slice_fusion.refs_1_), channel_id=1, source_target_pairs={{0,8},{1,9},{2,10},{3,11},{4,12},{5,13},{6,14},{7,15},{8,16},{9,17... | collective-permute-start | bytes 1572872 | tf_op jit(solution)/shard_map/ppermute | solution.py:306
  71.6 1.9 %collective-permute-start.7 = (bf16[256,1024]{1,0:T(8,128)(2,1)S(1)}, bf16[256,1024]{1,0:T(8,128)(2,1)}, u32[]{:S(2)}, u32[]{:S(2)}) collective-permute-start(bf16[256,1024]{1,0:T(8,128)(2,1)S(1)} %collective-permute-done.3.refs_2_), channel_id=1, source_target_pairs={{0,8},{1,9},{2,10},{3,11},{4,12},{5,13},{6,14},{7,15},{8,16},{9,17... | collective-permute-start | bytes 1572872 | tf_op jit(solution)/shard_map/ppermute | solution.py:308
  73.6 4.6 %collective-permute-start.8 = (bf16[256,1024]{1,0:T(8,128)(2,1)S(1)}, bf16[256,1024]{1,0:T(8,128)(2,1)}, u32[]{:S(2)}, u32[]{:S(2)}) collective-permute-start(bf16[256,1024]{1,0:T(8,128)(2,1)S(1)} %collective-permute-done.6.refs_5_), channel_id=1, source_target_pairs={{0,24},{1,25},{2,26},{3,27},{4,28},{5,29},{6,30},{7,31},{8,0},{9,1... | collective-permute-start | bytes 1572872 | tf_op jit(solution)/shard_map/ppermute | solution.py:309
  78.2 11.9 %collective-permute-start.12 = (bf16[16,96,128]{2,1,0:T(8,128)(2,1)S(1)}, bf16[16,96,128]{2,1,0:T(8,128)(2,1)}, u32[]{:S(2)}, u32[]{:S(2)}) collective-permute-start(bf16[16,96,128]{2,1,0:T(8,128)(2,1)S(1)} %all-to-all-done.1.mine_ref), channel_id=1, source_target_pairs={{0,32},{32,0},{1,33},{33,1},{2,34},{34,2},{3,35},{35,3},{4,36},{36... | collective-permute-start | bytes 1179656 | tf_op jit(solution)/shard_map/ppermute | solution.py:295
  90.1 4.2 %shard_map.87 = (f32[16,240,128]{2,1,0:T(8,128)}, f32[2,16,128]{2,1,0:T(8,128)}) custom-call(s32[18]{0:T(128)} %pad_add_fusion.at_ref, bf16[16,96,128]{2,1,0:T(8,128)(2,1)} %copy-done.2), custom_call_target="tpu_custom_call" | custom-call | tf_op jit(solution)/shard_map/pallas_call | solution.py:240
  94.3 2.2 %shard_map.86.refs_8_ = bf16[240,1024]{1,0:T(8,128)(2,1)} custom-call(s32[18]{0:T(128)} %pad_add_fusion.at_ref, bf16[16,96,128]{2,1,0:T(8,128)(2,1)} %copy-done.2, bf16[16,96,128]{2,1,0:T(8,128)(2,1)} %collective-permute-done.12.theirs_ref), custom_call_target="tpu_custom_call" | custom-call | tf_op jit(solution)/shard_map/pallas_call | solution.py:240
  97.3 6.8 %shard_map.88.refs_11_ = bf16[216,1024]{1,0:T(8,128)(2,1)} custom-call(bf16[256,1024]{1,0:T(8,128)(2,1)} %copy-done.1, bf16[256,1024]{1,0:T(8,128)(2,1)} %copy-done.3, bf16[256,1024]{1,0:T(8,128)(2,1)} %copy-done.4, bf16[256,1024]{1,0:T(8,128)(2,1)} %copy-done.6, bf16[256,1024]{1,0:T(8,128)(2,1)} %collective-permute-done.5.refs_4_, ...), custom_call_target="tpu_custom_call" | custom-call | tf_op jit(solution)/shard_map/pallas_call | solution.py:240
  104.1 1.9 %collective-permute-start.13 = (bf16[216,1024]{1,0:T(8,128)(2,1)}, bf16[216,1024]{1,0:T(8,128)(2,1)S(1)}, u32[]{:S(2)}, u32[]{:S(2)}) collective-permute-start(bf16[216,1024]{1,0:T(8,128)(2,1)} %shard_map.88.refs_11_), channel_id=1, source_target_pairs={{0,32},{32,0},{1,33},{33,1},{2,34},{34,2},{3,35},{35,3},{4,36},{36... | collective-permute-start | bytes 1327112 | tf_op jit(solution)/shard_map/ppermute | solution.py:331
  106.7 1.3 collective-permute-done.13.refs_12_
  108.8 7.0 %shard_map.89 = bf16[32,32,128]{2,1,0:T(8,128)(2,1)} custom-call(s32[4]{0:T(128)} %add_convert_fusion.edge_ref, bf16[256,1024]{1,0:T(8,128)(2,1)} %copy-done.1, bf16[256,1024]{1,0:T(8,128)(2,1)} %copy-done.3, bf16[256,1024]{1,0:T(8,128)(2,1)} %copy-done.4, bf16[256,1024]{1,0:T(8,128)(2,1)} %copy-done.6, bf16[256,1024]{1,0:T(8,128)(2,1)} %collective-permute-done.5.refs_4_, ...), custom_call_target="tpu_custom_call" | custom-call | tf_op jit(solution)/shard_map/pallas_call | solution.py:240
  115.8 34.6 %all_to_all.15.back_ref = bf16[32,32,128]{2,1,0:T(8,128)(2,1)} all-to-all(bf16[32,32,128]{2,1,0:T(8,128)(2,1)} %shard_map.89), channel_id=1, replica_groups=mesh['zl'=8,'core'=2,'y'=4,'zh'=2,'x'=4] {'zh','zl','core'}, dimensions={0} | all-to-all | bytes 524288 | tf_op jit(solution)/shard_map/all_to_all | solution.py:347
  150.4 1.8 %shard_map.90 = f32[512,128]{1,0:T(8,128)} custom-call(bf16[32,32,128]{2,1,0:T(8,128)(2,1)} %all_to_all.15.back_ref, bf16[512,128]{1,0:T(8,128)(2,1)} %bitcast.15), custom_call_target="tpu_custom_call" | custom-call | tf_op jit(solution)/shard_map/pallas_call | solution.py:240
  (48 shorter events, 6.2 us)
Async XLA Ops:
  0.0 1.0 copy-start
  0.0 29.8 %copy-start.12 = (f32[256]{0:T(256)S(1)}, f32[256]{0:T(256)}, u32[]{:S(2)}) copy-start(f32[256]{0:T(256)} %param.13) | copy-start | bytes 3076
  0.0 29.9 %copy-start.11 = (f32[256,8]{0,1:T(8,128)S(1)}, f32[256,8]{0,1:T(8,128)}, u32[]{:S(2)}) copy-start(f32[256,8]{0,1:T(8,128)} %param.11) | copy-start | bytes 24580
  0.0 29.9 %copy-start.13 = (f32[256]{0:T(256)S(1)}, f32[256]{0:T(256)}, u32[]{:S(2)}) copy-start(f32[256]{0:T(256)} %param.10) | copy-start | bytes 3076
  1.8 34.6 %all-to-all-start = ((bf16[8,16,1024]{2,1,0:T(8,128)(2,1)}), bf16[8,16,1024]{2,1,0:T(8,128)(2,1)S(1)}, u32[]{:S(2)}, u32[]{:S(2)}) async-start(bf16[8,16,1024]{2,1,0:T(8,128)(2,1)} %broadcast_in_dim.12), calls=%async_computation | async-start | bytes 524288 | tf_op jit(solution)/shard_map/all_to_all | solution.py:259
  17.8 4.9 %collective-permute-start.9 = (bf16[160,128]{1,0:T(8,128)(2,1)}, bf16[160,128]{1,0:T(8,128)(2,1)S(1)}, u32[]{:S(2)}, u32[]{:S(2)}) collective-permute-start(bf16[160,128]{1,0:T(8,128)(2,1)} %shard_map.83), channel_id=1, source_target_pairs={{4,12},{5,13},{6,14},{7,15},{8,0},{9,1},{10,2},{11,3},{12,20},{13,... | collective-permute-start | bytes 122888 | tf_op jit(solution)/shard_map/ppermute | solution.py:268
  22.7 0.6 copy-start.8
  25.4 5.1 %collective-permute-start.10 = (bf16[80,128]{1,0:T(8,128)(2,1)}, bf16[80,128]{1,0:T(8,128)(2,1)S(1)}, u32[]{:S(2)}, u32[]{:S(2)}) collective-permute-start(bf16[80,128]{1,0:T(8,128)(2,1)} %get-tuple-element.11), channel_id=1, source_target_pairs={{0,1},{1,2},{2,3},{4,5},{5,6},{6,7},{8,9},{9,10},{10,11},{12,13},{... | collective-permute-start | bytes 61448 | tf_op jit(solution)/shard_map/ppermute | solution.py:280
  28.6 4.7 %collective-permute-start.11 = (bf16[80,128]{1,0:T(8,128)(2,1)}, bf16[80,128]{1,0:T(8,128)(2,1)S(1)}, u32[]{:S(2)}, u32[]{:S(2)}) collective-permute-start(bf16[80,128]{1,0:T(8,128)(2,1)} %get-tuple-element.12), channel_id=1, source_target_pairs={{1,0},{2,1},{3,2},{5,4},{6,5},{7,6},{9,8},{10,9},{11,10},{13,12},{... | collective-permute-start | bytes 61448 | tf_op jit(solution)/shard_map/ppermute | solution.py:281
  30.5 2.8 %copy-start.9 = (bf16[80,128]{1,0:T(8,128)(2,1)}, bf16[80,128]{1,0:T(8,128)(2,1)S(1)}, u32[]{:S(2)}) copy-start(bf16[80,128]{1,0:T(8,128)(2,1)S(1)} %collective-permute-done.10.left_ref) | copy-start | bytes 61444
  33.3 0.6 copy-start.10
  36.4 41.8 %all-to-all-start.1 = ((bf16[16,96,128]{2,1,0:T(8,128)(2,1)}), bf16[16,96,128]{2,1,0:T(8,128)(2,1)S(1)}, u32[]{:S(2)}, u32[]{:S(2)}) async-start(bf16[16,96,128]{2,1,0:T(8,128)(2,1)} %shard_map.85), calls=%async_computation.1 | async-start | bytes 786432 | tf_op jit(solution)/shard_map/all_to_all | solution.py:294
  45.9 8.3 %collective-permute-start = (bf16[128,1024]{1,0:T(8,128)(2,1)S(1)}, bf16[128,1024]{1,0:T(8,128)(2,1)S(1)}, u32[]{:S(2)}, u32[]{:S(2)}) collective-permute-start(bf16[128,1024]{1,0:T(8,128)(2,1)S(1)} %bitcast.16), channel_id=1, source_target_pairs={{0,1},{1,2},{2,3},{3,0},{4,5},{5,6},{6,7},{7,4},{8,9},{9,10},{10,1... | collective-permute-start | bytes 786440 | tf_op jit(solution)/shard_map/ppermute | solution.py:298
  49.1 10.3 %collective-permute-start.1 = (bf16[128,1024]{1,0:T(8,128)(2,1)S(1)}, bf16[128,1024]{1,0:T(8,128)(2,1)S(1)}, u32[]{:S(2)}, u32[]{:S(2)}) collective-permute-start(bf16[128,1024]{1,0:T(8,128)(2,1)S(1)} %bitcast.17), channel_id=1, source_target_pairs={{0,3},{1,0},{2,1},{3,2},{4,7},{5,4},{6,5},{7,6},{8,11},{9,8},{10,9... | collective-permute-start | bytes 786440 | tf_op jit(solution)/shard_map/ppermute | solution.py:299
  54.2 8.6 %collective-permute-start.2 = (bf16[128,1024]{1,0:T(8,128)(2,1)S(1)}, bf16[128,1024]{1,0:T(8,128)(2,1)S(1)}, u32[]{:S(2)}, u32[]{:S(2)}) collective-permute-start(bf16[128,1024]{1,0:T(8,128)(2,1)S(1)} %collective-permute-done), channel_id=1, source_target_pairs={{0,1},{1,2},{2,3},{3,0},{4,5},{5,6},{6,7},{7,4},{8,9},{9,10},{10,1... | collective-permute-start | bytes 786440 | tf_op jit(solution)/shard_map/ppermute | solution.py:301
  56.2 40.3 %copy-start.1 = (bf16[256,1024]{1,0:T(8,128)(2,1)}, bf16[256,1024]{1,0:T(8,128)(2,1)S(1)}, u32[]{:S(2)}) copy-start(bf16[256,1024]{1,0:T(8,128)(2,1)S(1)} %pad_maximum_fusion.refs_0_) | copy-start | bytes 1572868
  56.2 15.4 %collective-permute-start.3 = (bf16[256,1024]{1,0:T(8,128)(2,1)S(1)}, bf16[256,1024]{1,0:T(8,128)(2,1)S(1)}, u32[]{:S(2)}, u32[]{:S(2)}) collective-permute-start(bf16[256,1024]{1,0:T(8,128)(2,1)S(1)} %pad_maximum_fusion.refs_0_), channel_id=1, source_target_pairs={{0,8},{1,9},{2,10},{3,11},{4,12},{5,13},{6,14},{7,15},{8,16},{9,17... | collective-permute-start | bytes 1572872 | tf_op jit(solution)/shard_map/ppermute | solution.py:303
  62.8 33.7 %copy-start.3 = (bf16[256,1024]{1,0:T(8,128)(2,1)}, bf16[256,1024]{1,0:T(8,128)(2,1)S(1)}, u32[]{:S(2)}) copy-start(bf16[256,1024]{1,0:T(8,128)(2,1)S(1)} %constant_dynamic-update-slice_fusion.refs_1_) | copy-start | bytes 1572868
  62.8 10.7 %collective-permute-start.6 = (bf16[256,1024]{1,0:T(8,128)(2,1)S(1)}, bf16[256,1024]{1,0:T(8,128)(2,1)S(1)}, u32[]{:S(2)}, u32[]{:S(2)}) collective-permute-start(bf16[256,1024]{1,0:T(8,128)(2,1)S(1)} %constant_dynamic-update-slice_fusion.refs_1_), channel_id=1, source_target_pairs={{0,24},{1,25},{2,26},{3,27},{4,28},{5,29},{6,30},{7,31},{8,0},{9,1... | collective-permute-start | bytes 1572872 | tf_op jit(solution)/shard_map/ppermute | solution.py:307
  65.8 30.7 %collective-permute-start.4 = (bf16[256,1024]{1,0:T(8,128)(2,1)S(1)}, bf16[256,1024]{1,0:T(8,128)(2,1)S(1)}, u32[]{:S(2)}, u32[]{:S(2)}) collective-permute-start(bf16[256,1024]{1,0:T(8,128)(2,1)S(1)} %pad_maximum_fusion.refs_0_), channel_id=1, source_target_pairs={{0,24},{1,25},{2,26},{3,27},{4,28},{5,29},{6,30},{7,31},{8,0},{9,1... | collective-permute-start | bytes 1572872 | tf_op jit(solution)/shard_map/ppermute | solution.py:304
  69.7 26.8 %collective-permute-start.5 = (bf16[256,1024]{1,0:T(8,128)(2,1)S(1)}, bf16[256,1024]{1,0:T(8,128)(2,1)}, u32[]{:S(2)}, u32[]{:S(2)}) collective-permute-start(bf16[256,1024]{1,0:T(8,128)(2,1)S(1)} %constant_dynamic-update-slice_fusion.refs_1_), channel_id=1, source_target_pairs={{0,8},{1,9},{2,10},{3,11},{4,12},{5,13},{6,14},{7,15},{8,16},{9,17... | collective-permute-start | bytes 1572872 | tf_op jit(solution)/shard_map/ppermute | solution.py:306
  71.6 24.9 %copy-start.4 = (bf16[256,1024]{1,0:T(8,128)(2,1)}, bf16[256,1024]{1,0:T(8,128)(2,1)S(1)}, u32[]{:S(2)}) copy-start(bf16[256,1024]{1,0:T(8,128)(2,1)S(1)} %collective-permute-done.3.refs_2_) | copy-start | bytes 1572868
  71.6 24.8 %collective-permute-start.7 = (bf16[256,1024]{1,0:T(8,128)(2,1)S(1)}, bf16[256,1024]{1,0:T(8,128)(2,1)}, u32[]{:S(2)}, u32[]{:S(2)}) collective-permute-start(bf16[256,1024]{1,0:T(8,128)(2,1)S(1)} %collective-permute-done.3.refs_2_), channel_id=1, source_target_pairs={{0,8},{1,9},{2,10},{3,11},{4,12},{5,13},{6,14},{7,15},{8,16},{9,17... | collective-permute-start | bytes 1572872 | tf_op jit(solution)/shard_map/ppermute | solution.py:308
  73.6 23.0 %copy-start.5 = (bf16[256,1024]{1,0:T(8,128)(2,1)}, bf16[256,1024]{1,0:T(8,128)(2,1)S(1)}, u32[]{:S(2)}) copy-start(bf16[256,1024]{1,0:T(8,128)(2,1)S(1)} %collective-permute-done.6.refs_5_) | copy-start | bytes 1572868
  73.6 22.9 %collective-permute-start.8 = (bf16[256,1024]{1,0:T(8,128)(2,1)S(1)}, bf16[256,1024]{1,0:T(8,128)(2,1)}, u32[]{:S(2)}, u32[]{:S(2)}) collective-permute-start(bf16[256,1024]{1,0:T(8,128)(2,1)S(1)} %collective-permute-done.6.refs_5_), channel_id=1, source_target_pairs={{0,24},{1,25},{2,26},{3,27},{4,28},{5,29},{6,30},{7,31},{8,0},{9,1... | collective-permute-start | bytes 1572872 | tf_op jit(solution)/shard_map/ppermute | solution.py:309
  78.2 11.9 %copy-start.2 = (bf16[16,96,128]{2,1,0:T(8,128)(2,1)}, bf16[16,96,128]{2,1,0:T(8,128)(2,1)S(1)}, u32[]{:S(2)}) copy-start(bf16[16,96,128]{2,1,0:T(8,128)(2,1)S(1)} %all-to-all-done.1.mine_ref) | copy-start | bytes 1179652
  78.2 16.1 %collective-permute-start.12 = (bf16[16,96,128]{2,1,0:T(8,128)(2,1)S(1)}, bf16[16,96,128]{2,1,0:T(8,128)(2,1)}, u32[]{:S(2)}, u32[]{:S(2)}) collective-permute-start(bf16[16,96,128]{2,1,0:T(8,128)(2,1)S(1)} %all-to-all-done.1.mine_ref), channel_id=1, source_target_pairs={{0,32},{32,0},{1,33},{33,1},{2,34},{34,2},{3,35},{35,3},{4,36},{36... | collective-permute-start | bytes 1179656 | tf_op jit(solution)/shard_map/ppermute | solution.py:295
  96.5 0.8 copy-start.6
  104.1 3.9 %collective-permute-start.13 = (bf16[216,1024]{1,0:T(8,128)(2,1)}, bf16[216,1024]{1,0:T(8,128)(2,1)S(1)}, u32[]{:S(2)}, u32[]{:S(2)}) collective-permute-start(bf16[216,1024]{1,0:T(8,128)(2,1)} %shard_map.88.refs_11_), channel_id=1, source_target_pairs={{0,32},{32,0},{1,33},{33,1},{2,34},{34,2},{3,35},{35,3},{4,36},{36... | collective-permute-start | bytes 1327112 | tf_op jit(solution)/shard_map/ppermute | solution.py:331
  108.0 0.8 copy-start.7
